TPU v7x, 32 devices: a whole 2x2x4 slice. The times are simulated.
32 devices in a mesh: dp: 8 (over z, y), fsdp: 4 (over x, core).
Axes of the slice: x: 2, y: 2, z: 4, core: 2. Of those that a mesh axis runs over, the one named last changes fastest.
Arguments:
- adapter_token_input: bfloat16 [512, 32, 4096], P('dp', None, 'fsdp'), may hold values from -6 to 6
- output_gradient_rows: bfloat16 [512, 32, 2048], P('dp', None, 'fsdp'), may hold values from -6 to 6
- adapter_down_weight: bfloat16 [64, 4096], P(None, 'fsdp'), may hold values from -0.09375 to 0.09375
- real_token_count: int32 [512], P('dp'), may hold values from 1 to 32, 10240 in all
- projection: bfloat16 [131072, 4096], P('fsdp', 'dp'), may hold values from -0.015625 to 0.015625
- targets: bfloat16 [256, 4096], P(None, 'dp'), may hold values from -6 to 6
Outputs:
- scores: float32 [512, 256], P('fsdp', 'dp')
Inputs may be any that keep to these rules, and one draw needn't show every extreme that they name: real_token_count[e] counts the real positions of example e, from position 0; the counts sum to 10240 and the largest equals 32.
All inputs are finite; a program needn't handle non-finite values. No bound on the sum of `real_token_count` on one device may be relied on, other than what follows from the above.
Results may differ from a plain program's by a relative error of at most 0.0042.
Values may be sent and summed in bfloat16 or wider, within the bound.
No kernel may reach another device: no remote copies, remote signals or barrier semaphores. Data moves between devices by JAX's collectives and lax.ppermute only.
A program may use at most 192 MiB of HBM per device.

v0:
```python
import jax
import jax.numpy as jnp
from jax import lax
from jax.sharding import PartitionSpec as P

K = 4096


def example_grads(grad_rows, acts_rows):
    formed = jnp.einsum("elo,elr->eor", grad_rows, acts_rows, preferred_element_type=jnp.float32)
    return formed.astype(jnp.bfloat16).reshape(grad_rows.shape[0], -1)


def per_device(
    adapter_token_input,
    output_gradient_rows,
    adapter_down_weight,
    real_token_count,
    projection,
    targets,
):
    pool_dev, seq_len, width_dev = adapter_token_input.shape
    adapter_rank = adapter_down_weight.shape[0]
    partial_rank = jnp.dot(
        adapter_token_input.reshape(pool_dev * seq_len, width_dev),
        adapter_down_weight.T,
        preferred_element_type=jnp.float32,
    )
    summed = lax.psum(partial_rank, "fsdp")
    positions = lax.broadcasted_iota(jnp.int32, (pool_dev, seq_len), 1)
    keep = (positions < real_token_count[:, None]).astype(jnp.float32)
    rank_acts = (summed.reshape(pool_dev, seq_len, adapter_rank) * keep[:, :, None]).astype(
        jnp.bfloat16
    )
    local_grads = example_grads(output_gradient_rows, rank_acts)
    features = jnp.dot(
        lax.all_gather(local_grads, "dp", axis=0, tiled=True),
        projection,
        preferred_element_type=jnp.float32,
    )
    pooled = lax.psum_scatter(features, "fsdp", scatter_dimension=0, tiled=True)
    target_f = targets.astype(jnp.float32)
    pool_sq = jnp.sum(pooled * pooled, axis=1)
    target_sq = jnp.sum(target_f * target_f, axis=1)
    feature_count = jnp.float32(K)
    pool_tot, target_tot = lax.psum((pool_sq, target_sq), "dp")
    pool_unit = pooled / jnp.sqrt(pool_tot + 1e-06)[:, None]
    target_unit = target_f / jnp.sqrt(target_tot + 1e-06)[:, None]
    partial_cos = jnp.dot(
        pool_unit,
        target_unit.T,
        precision=lax.Precision.HIGHEST,
        preferred_element_type=jnp.float32,
    )
    cosines = lax.psum_scatter(partial_cos, "dp", scatter_dimension=1, tiled=True)
    return cosines * jnp.sqrt(feature_count)


def solution(mesh):
    return jax.shard_map(
        per_device,
        mesh=mesh,
        in_specs=(
            P("dp", None, "fsdp"),
            P("dp", None, "fsdp"),
            P(None, "fsdp"),
            P("dp"),
            P("fsdp", "dp"),
            P(None, "dp"),
        ),
        out_specs=P("fsdp", "dp"),
        check_vma=False,
    )
```

profile of v0, /device:TPU:0, one launch (start us, length us, event | category | flops | bytes accessed | tf_op | source)
XLA Modules:
  0.0 856.9 jit_solution(353426869703234761)
XLA Ops:
  6.5 0.0 copy-start
  6.5 0.0 all-reduce.3.cloned.1.call-start
  6.5 0.0 copy-start.3
  6.5 4.6 fusion.7
  11.2 0.0 all-reduce.3.cloned.1.call-update
  11.2 0.0 all-gather.2.cloned.1.call-start
  11.2 0.0 copy-done.3
  11.3 0.1 fusion.6
  11.3 38.8 %all-reduce.3.cloned.1.call-done = f32[64,32,64]{2,1,0:T(8,128)} async-done(((f32[64,32,64]{2,1,0:T(8,128)}), f32[64,32,64]{2,1,0:T(8,128)}) %all-reduce.3.cloned.1.call-update) | async-done | bytes 524304 | tf_op jit(solution)/shard_map/psum | solution.py:29
  50.2 0.0 copy-done
  50.2 6.0 convert_bitcast_fusion
  56.1 8.4 copy.9
  64.5 10.6 %reshape.33 = bf16[64,32768]{1,0:T(8,128)(2,1)} reshape(bf16[64,512,64]{2,1,0:T(8,128)(2,1)} %copy.9) | data formatting | bytes 8388608 | tf_op jit(solution)/shard_map/reshape | solution.py:11
  75.1 0.0 all-gather.2.cloned.1.call-update
  75.2 0.0 copy-start.2
  75.2 0.0 reduce-scatter.3.cloned.1.call-start
  75.2 638.2 %all-gather.2.cloned.1.call-done = bf16[512,32768]{1,0:T(8,128)(2,1)} async-done(((bf16[64,32768]{1,0:T(8,128)(2,1)}), bf16[512,32768]{1,0:T(8,128)(2,1)}) %all-gather.2.cloned.1.call-update) | async-done | bytes 33554448 | tf_op jit(solution)/shard_map/all_gather | solution.py:37
  713.4 0.0 copy-start.1
  713.4 27.8 %fusion.8 = f32[512,512]{1,0:T(8,128)} fusion(bf16[512,32768]{1,0:T(8,128)(2,1)} %all-gather.2.cloned.1.call-done, bf16[32768,512]{1,0:T(8,128)(2,1)} %param.10), kind=kOutput, calls=%fused_computation.17 | convolution fusion | flops 17179869184 | bytes 68157440 | tf_op jit(solution)/shard_map/dot_general | solution.py:36
  741.3 0.0 reduce-scatter.3.cloned.1.call-update
  741.3 0.0 reduce-scatter.5.cloned.1.call-start
  741.4 0.0 copy-done.2
  741.4 0.1 fusion
  741.5 24.8 %reduce-scatter.3.cloned.1.call-done = f32[128,512]{1,0:T(8,128)} async-done(((f32[512,512]{1,0:T(8,128)}), f32[128,512]{1,0:T(8,128)}) %reduce-scatter.3.cloned.1.call-update) | async-done | bytes 262160 | tf_op jit(solution)/shard_map/reduce_scatter | solution.py:41
  766.3 1.1 multiply_reduce_fusion
  767.4 21.3 %all-reduce = (f32[256]{0:T(256)S(1)}, f32[128]{0:T(128)S(1)}) all-reduce(f32[256]{0:T(256)S(1)} %fusion, f32[128]{0:T(128)S(1)} %multiply_reduce_fusion), channel_id=1, replica_groups=mesh['dp'=8,'fsdp'=4] {'dp'}, use_global_device_ids=true, to_apply=%region_5.0 | all-reduce | flops 384 | bytes 3072 | tf_op jit(solution)/shard_map/psum | solution.py:46
  788.7 2.3 fusion.1
  791.0 0.0 reduce-scatter.5.cloned.1.call-update
  791.0 58.0 %reduce-scatter.5.cloned.1.call-done = f32[128,32]{0,1:T(8,128)} async-done(((f32[128,256]{0,1:T(8,128)}), f32[128,32]{0,1:T(8,128)}) %reduce-scatter.5.cloned.1.call-update) | async-done | bytes 16400 | tf_op jit(solution)/shard_map/reduce_scatter | solution.py:55
  849.0 1.3 broadcast_multiply_fusion
  850.3 0.0 copy-done.1
  (2 shorter events, 0.0 us)
Async XLA Ops:
  6.5 43.6 %copy-start = (bf16[64,32,512]{2,1,0:T(8,128)(2,1)S(1)}, bf16[64,32,512]{2,1,0:T(8,128)(2,1)}, u32[]{:S(2)}) copy-start(bf16[64,32,512]{2,1,0:T(8,128)(2,1)} %param.7) | copy-start | bytes 6291460
  6.5 43.6 %all-reduce.3.cloned.1.call-start = ((), (), s32[]{:S(2)}) async-start(), calls=%async_computation.2 | async-start | bytes 2097152 | tf_op jit(solution)/shard_map/psum | solution.py:29
  6.5 4.7 copy-start.3
  11.2 702.2 %all-gather.2.cloned.1.call-start = ((), (), s32[]{:S(2)}) async-start(), calls=%async_computation.3 | async-start | bytes 37748736 | tf_op jit(solution)/shard_map/all_gather | solution.py:37
  75.2 666.2 %copy-start.2 = (bf16[256,512]{1,0:T(8,128)(2,1)S(1)}, bf16[256,512]{1,0:T(8,128)(2,1)}, u32[]{:S(2)}) copy-start(bf16[256,512]{1,0:T(8,128)(2,1)} %param.11) | copy-start | bytes 786436
  75.2 691.1 %reduce-scatter.3.cloned.1.call-start = ((), (), s32[]{:S(2)}) async-start(), calls=%async_computation.4 | async-start | bytes 1310720 | tf_op jit(solution)/shard_map/reduce_scatter | solution.py:41
  713.4 136.9 %copy-start.1 = (bf16[64,32,512]{2,1,0:T(8,128)(2,1)S(1)}, bf16[64,32,512]{2,1,0:T(8,128)(2,1)}, u32[]{:S(2)}) copy-start(bf16[64,32,512]{2,1,0:T(8,128)(2,1)} %param.7) | copy-start | bytes 6291460
  741.3 107.7 %reduce-scatter.5.cloned.1.call-start = ((), (), s32[]{:S(2)}) async-start(), calls=%async_computation.5 | async-start | bytes 147456 | tf_op jit(solution)/shard_map/reduce_scatter | solution.py:55
Sparse Core Ops, SparseCore 0:
  11.3 38.8 all-reduce.2
  75.3 638.1 all-gather.1
  741.4 24.8 reduce-scatter.2
  791.2 57.8 reduce-scatter.4
where the time goes:
time: 858 us; the launch traced here: 857 us
  waiting for transfers between devices  760 us (89%)
  matrix products  40.7 us (5%)
  blocking collectives  21.3 us (2%)
  local copies, waits for them, and re-layouts  19 us (2%)
  between operations  13.2 us (2%)
    all_gather x1, waiting for transfers between devices, per_device(): lax.all_gather(local_grads, 'dp', axis=0, tiled=True)  638 us
    reduce_scatter x1, waiting for transfers between devices, per_device(): lax.psum_scatter(partial_cos, 'dp', scatter_dimension=1, tiled=True)  58 us
    psum x1, waiting for transfers between devices, per_device(): summed = lax.psum(partial_rank, 'fsdp')  38.8 us
    dot_general x1, matrix products, per_device(): jnp.dot(lax.all_gather(local_grads, 'dp', axis=0, tiled=True), projection...  27.8 us
    reduce_scatter x1, waiting for transfers between devices, per_device(): pooled = lax.psum_scatter(features, 'fsdp', scatter_dimension=0, tiled=True)  24.8 us
    psum x1, blocking collectives, per_device(): pool_tot, target_tot = lax.psum((pool_sq, target_sq), 'dp')  21.3 us
  transfers between devices with their start and end apart: 4, of which 4 were waited for; matrix products, arithmetic and copies ran while one was open for 0% of the time, Pallas kernels for 0%

commit v1 on v0

v1 whole, which is shorter than its diff:
```python
import functools

import jax
import jax.numpy as jnp
import numpy as np
from jax import lax
from jax.experimental import pallas as pl
from jax.experimental.pallas import tpu as pltpu
from jax.sharding import PartitionSpec as P

F32 = jnp.float32
BF16 = jnp.bfloat16
LANES = 128
VMEM_LIMIT = 34 * 1024 * 1024


def ring_order(n):
    ny = 2
    while ny * ny * 4 <= n:
        ny *= 2
    nz = n // ny
    path = []
    for z in range(nz):
        ys = range(1, ny) if z % 2 == 0 else range(ny - 1, 0, -1)
        path += [z * ny + y for y in ys]
    return path + [z * ny for z in reversed(range(nz))]


def form_project_kernel(dims, meta, *refs):
    shards, parts, row, pool, rank, pairs, block, first_row = dims
    g_refs = [refs[k * parts : (k + 1) * parts] for k in range(shards)]
    a_refs = refs[shards * parts : shards * (parts + 1)]
    p_hbm, acc_hbm, out_hbm, pbuf, s_ref, held, p_sems, acc_sems = refs[shards * (parts + 1) :]
    blocks = pairs // block
    rows = block * rank
    width = 1 + 2 * pool
    stride = shards * pool + 8

    def p_copy(i, h):
        start = pl.multiple_of(first_row + (h * pairs + i * block) * rank, rank)
        return pltpu.make_async_copy(
            p_hbm.at[pl.ds(start, rows)], pbuf.at[i, h], p_sems.at[i, h]
        )

    def acc_rows(k):
        return pl.ds(pl.multiple_of(meta[(row + k) * width] * pool, pool), pool)

    def acc_load(k):
        return pltpu.make_async_copy(
            acc_hbm.at[acc_rows(k)], held.at[pl.ds(k * pool, pool)], acc_sems.at[0, k]
        )

    def acc_store(k):
        return pltpu.make_async_copy(
            held.at[pl.ds(k * pool, pool)], out_hbm.at[acc_rows(k)], acc_sems.at[1, k]
        )

    for i in range(blocks):
        for h in range(2):
            p_copy(i, h).start()
    for k in range(shards):
        acc_load(k).start()
    tiles = a_refs[0].shape[1] // LANES
    low = lax.broadcasted_iota(jnp.int32, (pairs, LANES), 1) < rank
    lane = lax.broadcasted_iota(jnp.int32, (rank, 2 * LANES), 1)

    for k in range(shards):
        first = (row + k) * width + 1

        def two_examples(p, carry, k=k, first=first):
            e = 2 * p
            tile = jnp.minimum(meta[first + e] // LANES, tiles - 2)
            base = pl.multiple_of(tile * LANES, LANES)
            g = jnp.concatenate([g_ref[:, pl.ds(base, 2 * LANES)] for g_ref in g_refs[k]], axis=0)
            a = a_refs[k][:, pl.ds(base, 2 * LANES)]
            masked = []
            for j in range(2):
                begin = meta[first + e + j] - base
                end = begin + meta[first + pool + e + j]
                part = jnp.where((lane >= begin) & (lane < end), a, jnp.zeros_like(a))
                masked += [part, part]
            formed = lax.dot_general(
                g,
                jnp.concatenate(masked, axis=0),
                (((1,), (1,)), ((), ())),
                preferred_element_type=F32,
            )
            for j in range(2):
                own = formed[:, j * LANES : (j + 1) * LANES]
                s_ref[pl.ds(k * pool + e + j, pairs, stride=stride), :] = jnp.where(
                    low, own[:pairs], own[pairs:]
                )
            return carry

        lax.fori_loop(0, pool // 2, two_examples, 0, unroll=4)
    for k in range(shards):
        acc_load(k).wait()

    def project(i, carry):
        p_copy(i, 0).wait()
        p_copy(i, 1).wait()
        left = jnp.concatenate(
            [
                s_ref[pl.ds(pl.multiple_of((i * block + o) * stride, 8), shards * pool), :].astype(BF16)
                for o in range(block)
            ],
            axis=1,
        )
        right = jnp.concatenate(
            [
                pbuf[i, h, pl.ds(o * rank, rank), :]
                for o in range(block)
                for h in range(2)
            ],
            axis=0,
        )
        held[...] += jnp.dot(left, right, preferred_element_type=F32)
        return carry

    lax.fori_loop(0, blocks, project, 0)
    for k in range(shards):
        acc_store(k).start()
    for k in range(shards):
        acc_store(k).wait()


def form_project(acc, meta, row, gs, acts, projection, half, pool):
    shards, parts = len(gs), len(gs[0])
    outs = parts * gs[0][0].shape[0]
    rank, room = acts[0].shape
    feats = projection.shape[1]
    pairs = outs // 2
    block = min(16, pairs)
    dims = (shards, parts, row, pool, rank, pairs, block, half * outs * rank)
    whole = lambda x: pl.BlockSpec(x.shape, lambda i, m: (0, 0))
    flat = [g for group in gs for g in group]
    spec = pltpu.PrefetchScalarGridSpec(
        num_scalar_prefetch=1,
        grid=(1,),
        in_specs=[whole(x) for x in flat + list(acts)]
        + [pl.BlockSpec(memory_space=pl.ANY)] * 2,
        out_specs=pl.BlockSpec(memory_space=pl.ANY),
        scratch_shapes=[
            pltpu.VMEM((pairs // block, 2, block * rank, feats), BF16),
            pltpu.VMEM((pairs * (shards * pool + 8), LANES), F32),
            pltpu.VMEM((shards * pool, feats), F32),
            pltpu.SemaphoreType.DMA((pairs // block, 2)),
            pltpu.SemaphoreType.DMA((2, shards)),
        ],
    )
    return pl.pallas_call(
        functools.partial(form_project_kernel, dims),
        out_shape=jax.ShapeDtypeStruct(acc.shape, F32),
        grid_spec=spec,
        input_output_aliases={len(flat) + shards + 2: 0},
        compiler_params=pltpu.CompilerParams(vmem_limit_bytes=VMEM_LIMIT),
        cost_estimate=pl.CostEstimate(
            flops=2 * shards * pool * outs * rank * feats,
            bytes_accessed=outs * rank * feats * 2,
            transcendentals=0,
        ),
        name="form_project",
    )(meta, *flat, *acts, projection, acc)


def exchange_sum(x, axis, n):
    me = lax.axis_index(axis)
    bit = 1
    slots = x[:, None]
    while bit < n:
        swap = [(i, i ^ bit) for i in range(n)]
        mine = (me // bit) % 2
        grouped = slots.reshape((slots.shape[0] // 2, 2) + x.shape[1:])
        keep = lax.dynamic_index_in_dim(grouped, mine, 1, keepdims=False)
        send = lax.dynamic_index_in_dim(grouped, 1 - mine, 1, keepdims=False)
        slots = keep + lax.ppermute(send, axis, swap)
        bit *= 2
    return slots.reshape(x.shape[1:])


def exchange_total(x, axis, n, bit=1):
    while bit < n:
        x = x + lax.ppermute(x, axis, [(i, i ^ bit) for i in range(n)])
        bit *= 2
    return x


def per_device(dp, fsdp, tokens, grad_rows, down, counts, projection, targets):
    pool, length, width = tokens.shape
    outs = grad_rows.shape[2]
    rank = down.shape[0]
    feats = projection.shape[1]
    half = outs // 2
    room = -(-3 * pool * length // (4 * LANES)) * LANES
    before = jnp.arange(pool)[None, :] < jnp.arange(pool)[:, None]
    starts = jnp.sum(jnp.where(before, counts[None, :], 0), axis=1)
    t = jnp.arange(length, dtype=jnp.int32)[None, :]
    place = jnp.where(t < counts[:, None], starts[:, None] + t, -1).reshape(pool * length)
    select = (place[:, None] == jnp.arange(room, dtype=jnp.int32)[None, :]).astype(BF16)
    packed = lax.dot_general(
        grad_rows.reshape(pool * length, outs),
        select,
        (((0,), (0,)), ((), ())),
        preferred_element_type=F32,
    ).astype(BF16)

    me = lax.axis_index("dp")
    order = ring_order(dp)
    ahead = [(order[i], order[(i + 1) % dp]) for i in range(dp)]
    back = [(b, a) for a, b in ahead]
    swap = [(i, i ^ 1) for i in range(fsdp)]
    core = lax.axis_index("fsdp") % 2

    acts_part = lax.dot_general(
        down,
        tokens.reshape(pool * length, width),
        (((1,), (1,)), ((), ())),
        preferred_element_type=F32,
    ).reshape(2, rank // 2, pool * length)
    keep = lax.dynamic_index_in_dim(acts_part, core, 0, keepdims=False)
    send = lax.dynamic_index_in_dim(acts_part, 1 - core, 0, keepdims=False)
    acts_half = exchange_total(keep + lax.ppermute(send, "fsdp", swap), "fsdp", fsdp, 2)
    real = (place >= 0).astype(F32)[None, :]
    acts_half = (acts_half * real).astype(BF16)

    def both_halves(mine):
        other = lax.ppermute(mine, "fsdp", swap)
        return jnp.where(
            core == 0,
            jnp.concatenate([mine, other], axis=0),
            jnp.concatenate([other, mine], axis=0),
        )

    own_acts = both_halves(
        jnp.dot(acts_half, select, preferred_element_type=F32).astype(BF16)
    )

    own = jnp.concatenate([starts, counts])
    table = lax.dynamic_update_slice(jnp.zeros((dp, 2 * pool), jnp.int32), own[None], (me, 0))
    table, packed = lax.optimization_barrier((exchange_total(table, "dp", dp), packed))
    overflow = jnp.max(jnp.sum(table[:, pool:], axis=1)) > room
    my_position = jnp.asarray(np.argsort(order), jnp.int32)[me]
    blocks = jnp.asarray(order, jnp.int32)[(my_position - jnp.arange(dp + 1)) % dp]
    meta = jnp.concatenate([blocks[:, None], table[blocks]], axis=1).reshape(-1)

    acts = {0: own_acts, dp: own_acts}
    low, high = {0: packed[:half]}, {0: packed[half:]}
    acc = jnp.zeros((dp * pool, feats), F32)
    for s in range(dp):
        if s > 0:
            keys = [k for k in (s, dp - s) if k in acts]
            low[s], high[s], acc, *fresh = lax.optimization_barrier(
                (low[s], high[s], acc, *[acts[k] for k in keys])
            )
            acts.update(zip(keys, fresh))
        if s + 1 < dp:
            low[s + 1] = lax.ppermute(low[s], "dp", ahead)
            high[s + 1] = lax.ppermute(high[s], "dp", back)
        if 2 * (s + 1) <= dp:
            acts[s + 1] = lax.ppermute(acts[s], "dp", ahead)
        if 2 * (s + 1) < dp:
            acts[dp - s - 1] = lax.ppermute(acts[dp - s], "dp", back)
        if s % 2 == 1:
            rows = [s - 1, s]
            acc = form_project(
                acc, meta, s - 1, [[low[i]] for i in rows], [acts[i] for i in rows],
                projection, 0, pool,
            )
        if s > 0 and (s % 2 == 0 or s == dp - 1):
            rows = [s - s % 2, s - s % 2 + 1] if s == dp - 1 else [s - 2, s - 1]
            rows = [dp - rows[1], dp - rows[0]]
            acc = form_project(
                acc, meta, rows[0], [[high[dp - i]] for i in rows], [acts[i] for i in rows],
                projection, 1, pool,
            )

    def padded(acc):
        mine = both_halves(acts_half).reshape(rank, pool, length)
        grads = jnp.einsum("elo,rel->eor", grad_rows, mine, preferred_element_type=F32)
        grads = grads.astype(BF16).reshape(pool, outs * rank)
        grads = lax.all_gather(grads, "dp", axis=0, tiled=True)
        return jnp.dot(grads, projection, preferred_element_type=F32)

    acc = lax.cond(overflow, padded, lambda acc: acc, acc)
    pooled = exchange_sum(acc.reshape(fsdp, dp * pool // fsdp, feats), "fsdp", fsdp)
    target_f = targets.astype(F32)
    queries = targets.shape[0]
    share = queries // dp
    rows = pooled.shape[0]
    raw = lax.dot_general(
        target_f,
        pooled,
        (((1,), (1,)), ((), ())),
        precision=lax.Precision.HIGHEST,
        preferred_element_type=F32,
    ).reshape(dp, share, rows)
    pool_sq = jnp.sum(pooled * pooled, axis=1)
    target_sq = jnp.sum(target_f * target_f, axis=1).reshape(dp, 1, share)
    sent = jnp.concatenate(
        [
            raw,
            jnp.broadcast_to(pool_sq[None, None, :], (dp, 1, rows)),
            jnp.pad(target_sq, ((0, 0), (0, 0), (0, rows - share))),
        ],
        axis=1,
    )
    got = jnp.sum(lax.all_to_all(sent, "dp", 0, 0), axis=0)
    pool_norm = jnp.sqrt(got[share] + 1e-06)
    target_norm = jnp.sqrt(got[share + 1, :share] + 1e-06)
    scale = jnp.sqrt(F32(feats * dp))
    return (got[:share].T / pool_norm[:, None]) / target_norm[None, :] * scale


def solution(mesh):
    dp, fsdp = mesh.shape["dp"], mesh.shape["fsdp"]
    return jax.shard_map(
        functools.partial(per_device, dp, fsdp),
        mesh=mesh,
        in_specs=(
            P("dp", None, "fsdp"),
            P("dp", None, "fsdp"),
            P(None, "fsdp"),
            P("dp"),
            P("fsdp", "dp"),
            P(None, "dp"),
        ),
        out_specs=P("fsdp", "dp"),
        check_vma=False,
    )
```

time: 858 us -> 229 us (0.27)
  waiting for transfers between devices: 760 us -> 54.4 us
  Pallas kernels: 0 us -> 93.5 us
  starting transfers between devices: 0.13 us -> 32 us
  matrix products: 40.7 us -> 11.9 us
  local copies, waits for them, and re-layouts: 19 us -> 7.12 us
  blocking collectives: 21.3 us -> 10.9 us
    all_gather x1 -> x0, waiting for transfers between devices: 638 us -> none  [per_device(): lax.all_gather(local_grads, 'dp', axis=0, tiled=True)]
    pallas_call x0 -> x8, Pallas kernels: none -> 93.5 us  [form_project(): pl.pallas_call(functools.partial(form_project_kernel, dims), out_shape=ja...]
    reduce_scatter x2 -> x0, waiting for transfers between devices: 82.8 us -> none  [the longest x1 58 us: per_device(): lax.psum_scatter(partial_cos, 'dp', scatter_dimension=1, tiled=True)]
    ppermute x0 -> x29, waiting for transfers between devices: none -> 54.4 us  [the longest x7 17.4 us: per_device(): low[s + 1] = lax.ppermute(low[s], 'dp', ahead)]
    psum x1 -> x0, waiting for transfers between devices: 38.8 us -> none  [per_device(): summed = lax.psum(partial_rank, 'fsdp')]
    ppermute x0 -> x29, starting transfers between devices: none -> 32 us  [the longest x7 9.81 us: per_device(): low[s + 1] = lax.ppermute(low[s], 'dp', ahead)]
    dot_general x4, matrix products: 40.7 us -> 11.9 us  [the longest x1 5.35 us: per_device(): lax.dot_general(grad_rows.reshape(pool * length, outs), select, (((0,), (...]
    psum x1 -> x0, blocking collectives: 21.3 us -> none  [per_device(): pool_tot, target_tot = lax.psum((pool_sq, target_sq), 'dp')]
  transfers between devices with their start and end apart: 4 -> 29, of which waited for: 4 -> 17; matrix products, arithmetic and copies ran while one was open for 0% -> 6% of each run, Pallas kernels for 0% -> 30%
where the time goes in v1:
time: 229 us; the launch traced here: 228 us
  Pallas kernels  93.5 us (41%)
  waiting for transfers between devices  54.4 us (24%)
  starting transfers between devices  32 us (14%)
  between operations  14.4 us (6%)
  matrix products  11.9 us (5%)
  blocking collectives  10.9 us (5%)
  local copies, waits for them, and re-layouts  7.12 us (3%)
  other arithmetic  4.12 us (2%)
    pallas_call x8, Pallas kernels, form_project(): pl.pallas_call(functools.partial(form_project_kernel, dims), out_shape=ja...  93.5 us
    ppermute x7, waiting for transfers between devices, per_device(): low[s + 1] = lax.ppermute(low[s], 'dp', ahead)  17.4 us
    ppermute x4, waiting for transfers between devices, per_device(): acts[s + 1] = lax.ppermute(acts[s], 'dp', ahead)  15.1 us
    all_to_all x1, blocking collectives, per_device(): got = jnp.sum(lax.all_to_all(sent, 'dp', 0, 0), axis=0)  10.9 us
    ppermute x7, starting transfers between devices, per_device(): low[s + 1] = lax.ppermute(low[s], 'dp', ahead)  9.81 us
    ppermute x2, waiting for transfers between devices, exchange_sum(): slots = keep + lax.ppermute(send, axis, swap)  9.6 us
    ppermute x4, starting transfers between devices, exchange_total(): x = x + lax.ppermute(x, axis, [(i, i ^ bit) for i in range(n)])  8.91 us
    ppermute x4, starting transfers between devices, per_device(): acts[s + 1] = lax.ppermute(acts[s], 'dp', ahead)  5.61 us
  transfers between devices with their start and end apart: 29, of which 17 were waited for; matrix products, arithmetic and copies ran while one was open for 6% of the time, Pallas kernels for 30%

profile of v1, /device:TPU:0, one launch (start us, length us, event | category | flops | bytes accessed | tf_op | source)
XLA Modules:
  0.0 228.4 jit_solution(6846493140401386039)
XLA Ops:
  7.4 3.6 %fusion.29 = f32[2,32,2048]{2,1,0:T(8,128)S(1)} fusion(bf16[2,32,1024]{2,1,0:T(8,128)(2,1)S(1)} %bitcast.60, bf16[2048,1024,1]{1,0,2:T(8,128)(2,1)} %bitcast.63), kind=kOutput, calls=%fused_computation.66 | convolution fusion | flops 268435456 | bytes 4849664 | tf_op jit(solution)/shard_map/dot_general | solution.py:214
  11.8 2.6 %collective-permute-start.1 = (s32[8,128]{1,0:T(8,128)S(1)}, s32[8,128]{1,0:T(8,128)S(1)}, u32[]{:S(2)}, u32[]{:S(2)}) collective-permute-start(s32[8,128]{1,0:T(8,128)S(1)} %dynamic_update_slice.5), channel_id=1, source_target_pairs={{0,4},{4,0},{8,12},{12,8},{16,20},{20,16},{24,28},{28,24},{1,5},{5... | collective-permute-start | bytes 12296 | tf_op jit(solution)/shard_map/ppermute | solution.py:183
  14.5 1.4 collective-permute-done.1
  16.1 2.1 collective-permute-start.2
  18.2 5.4 %fusion.12 = bf16[512,1536]{1,0:T(8,128)(2,1)} fusion(bf16[2048,512]{1,0:T(8,128)(2,1)S(1)} %bitcast.64, s32[2048]{0:T(1024)S(1)} %select_n.112), kind=kOutput, calls=%fused_computation.17 | convolution fusion | flops 3225157632 | bytes 3678208 | tf_op jit(solution)/shard_map/dot_general | solution.py:200
  23.6 2.6 %collective-permute-start.3 = (s32[8,128]{1,0:T(8,128)S(1)}, s32[8,128]{1,0:T(8,128)S(1)}, u32[]{:S(2)}, u32[]{:S(2)}) collective-permute-start(s32[8,128]{1,0:T(8,128)S(1)} %add.132), channel_id=1, source_target_pairs={{0,16},{4,20},{8,24},{12,28},{16,0},{20,4},{24,8},{28,12},{1,17},{... | collective-permute-start | bytes 12296 | tf_op jit(solution)/shard_map/ppermute | solution.py:183
  26.2 1.9 collective-permute-done.3
  28.1 1.6 collective-permute-start.7
  29.7 1.5 fusion.27
  31.2 1.6 collective-permute-start.4
  33.3 1.3 collective-permute-done.7
  34.6 2.5 %fusion.13 = bf16[32,1536]{1,0:T(8,128)(2,1)S(1)} fusion(bf16[32,2048]{1,0:T(8,128)(2,1)S(1)} %multiply_convert_fusion, s32[2048]{0:T(1024)S(1)} %select_n.112), kind=kOutput, calls=%fused_computation.18 | convolution fusion | flops 204521472 | bytes 237568 | tf_op jit(solution)/shard_map/dot_general | solution.py:235
  37.2 1.3 collective-permute-done.8
  38.7 1.9 collective-permute-start.9
  41.2 9.3 %collective-permute-done.4.refs_1_ = bf16[256,1536]{1,0:T(8,128)(2,1)} collective-permute-done((bf16[256,1536]{1,0:T(8,128)(2,1)S(1)}, bf16[256,1536]{1,0:T(8,128)(2,1)}, u32[]{:S(2)}, u32[]{:S(2)}) %collective-permute-start.4) | collective-permute-done | bytes 786464 | tf_op jit(solution)/shard_map/ppermute | solution.py:257
  50.5 1.2 collective-permute-done.5.refs_0_
  51.7 2.1 collective-permute-done.10.refs_2_.refs_3_
  53.8 1.4 collective-permute-start.11
  58.0 1.7 collective-permute-start.13
  60.2 12.0 %form_project.8.refs_5_ = f32[512,512]{1,0:T(8,128)S(1)} custom-call(s32[1161]{0:T(1024)S(1)} %reshape.168.meta, bf16[256,1536]{1,0:T(8,128)(2,1)S(1)} %get-tuple-element.109.refs_0_, bf16[256,1536]{1,0:T(8,128)(2,1)} %collective-permute-done.4.refs_1_, bf16[64,1536]{1,0:T(8,128)(2,1)S(1)} %maximum_select_fusion.2.refs_2_.refs_3_, ...), custom_call_target="tpu_custom_call", output_to_operand_aliasing={{}: (6, {})} | custom-call | flops 2147483648 | bytes 16777216 | tf_op jit(solution)/shard_map/form_project/pallas_call | solution.py:151
  72.3 2.5 %collective-permute-done.13.refs_2_.refs_3_ = bf16[64,1536]{1,0:T(8,128)(2,1)S(1)} collective-permute-done((bf16[64,1536]{1,0:T(8,128)(2,1)S(1)}, bf16[64,1536]{1,0:T(8,128)(2,1)S(1)}, u32[]{:S(2)}, u32[]{:S(2)}) %collective-permute-start.13) | collective-permute-done | bytes 196640 | tf_op jit(solution)/shard_map/ppermute | solution.py:260
  74.7 1.5 collective-permute-done.14.refs_3_.refs_2_
  76.2 1.0 collective-permute-start.15
  77.2 1.0 collective-permute-start.16
  79.3 1.0 collective-permute-start.18
  80.3 10.9 %form_project.9.refs_5_ = f32[512,512]{1,0:T(8,128)S(1)} custom-call(s32[1161]{0:T(1024)S(1)} %reshape.168.meta, bf16[256,1536]{1,0:T(8,128)(2,1)S(1)} %collective-permute-done.5.refs_0_, bf16[256,1536]{1,0:T(8,128)(2,1)S(1)} %get-tuple-element.108.refs_1_, ...), custom_call_target="tpu_custom_call", output_to_operand_aliasing={{}: (6, {})} | custom-call | flops 2147483648 | bytes 16777216 | tf_op jit(solution)/shard_map/form_project/pallas_call | solution.py:151
  91.2 5.8 %collective-permute-done.17.refs_3_.refs_2_ = bf16[64,1536]{1,0:T(8,128)(2,1)S(1)} collective-permute-done((bf16[64,1536]{1,0:T(8,128)(2,1)S(1)}, bf16[64,1536]{1,0:T(8,128)(2,1)S(1)}, u32[]{:S(2)}, u32[]{:S(2)}) %collective-permute-start.17) | collective-permute-done | bytes 196640 | tf_op jit(solution)/shard_map/ppermute | solution.py:260
  97.0 1.3 collective-permute-done.18.refs_2_.refs_3_
  98.3 1.0 collective-permute-start.19
  100.4 1.0 collective-permute-start.21
  101.4 12.0 %form_project.10.refs_5_ = f32[512,512]{1,0:T(8,128)S(1)} custom-call(s32[1161]{0:T(1024)S(1)} %reshape.168.meta, bf16[256,1536]{1,0:T(8,128)(2,1)} %collective-permute-done.11.refs_0_, bf16[256,1536]{1,0:T(8,128)(2,1)S(1)} %collective-permute-done.15.refs_1_, ...), custom_call_target="tpu_custom_call", output_to_operand_aliasing={{}: (6, {})} | custom-call | flops 2147483648 | bytes 16777216 | tf_op jit(solution)/shard_map/form_project/pallas_call | solution.py:151
  113.4 6.8 %collective-permute-done.21.refs_2_.refs_3_ = bf16[64,1536]{1,0:T(8,128)(2,1)S(1)} collective-permute-done((bf16[64,1536]{1,0:T(8,128)(2,1)S(1)}, bf16[64,1536]{1,0:T(8,128)(2,1)S(1)}, u32[]{:S(2)}, u32[]{:S(2)}) %collective-permute-start.21) | collective-permute-done | bytes 196640 | tf_op jit(solution)/shard_map/ppermute | solution.py:260
  120.3 1.0 collective-permute-start.22
  122.3 12.0 %form_project.11.refs_5_ = f32[512,512]{1,0:T(8,128)S(1)} custom-call(s32[1161]{0:T(1024)S(1)} %reshape.168.meta, bf16[256,1536]{1,0:T(8,128)(2,1)S(1)} %collective-permute-done.16.refs_0_, bf16[256,1536]{1,0:T(8,128)(2,1)} %collective-permute-done.12.refs_1_, ...), custom_call_target="tpu_custom_call", output_to_operand_aliasing={{}: (6, {})} | custom-call | flops 2147483648 | bytes 16777216 | tf_op jit(solution)/shard_map/form_project/pallas_call | solution.py:151
  134.3 3.6 %collective-permute-done.22.refs_1_ = bf16[256,1536]{1,0:T(8,128)(2,1)S(1)} collective-permute-done((bf16[256,1536]{1,0:T(8,128)(2,1)S(1)}, bf16[256,1536]{1,0:T(8,128)(2,1)S(1)}, u32[]{:S(2)}, u32[]{:S(2)}) %collective-permute-start.22) | collective-permute-done | bytes 786464 | tf_op jit(solution)/shard_map/ppermute | solution.py:257
  138.0 1.1 collective-permute-start.24
  140.0 10.9 %form_project.12.refs_5_ = f32[512,512]{1,0:T(8,128)S(1)} custom-call(s32[1161]{0:T(1024)S(1)} %reshape.168.meta, bf16[256,1536]{1,0:T(8,128)(2,1)S(1)} %collective-permute-done.19.refs_0_, bf16[256,1536]{1,0:T(8,128)(2,1)S(1)} %collective-permute-done.22.refs_1_, ...), custom_call_target="tpu_custom_call", output_to_operand_aliasing={{}: (6, {})} | custom-call | flops 2147483648 | bytes 16777216 | tf_op jit(solution)/shard_map/form_project/pallas_call | solution.py:151
  150.9 4.4 %collective-permute-done.24.refs_0_ = bf16[256,1536]{1,0:T(8,128)(2,1)} collective-permute-done((bf16[256,1536]{1,0:T(8,128)(2,1)S(1)}, bf16[256,1536]{1,0:T(8,128)(2,1)}, u32[]{:S(2)}, u32[]{:S(2)}) %collective-permute-start.24) | collective-permute-done | bytes 786464 | tf_op jit(solution)/shard_map/ppermute | solution.py:257
  155.7 2.6 %collective-permute-start.26 = (bf16[256,1536]{1,0:T(8,128)(2,1)}, bf16[256,1536]{1,0:T(8,128)(2,1)}, u32[]{:S(2)}, u32[]{:S(2)}) collective-permute-start(bf16[256,1536]{1,0:T(8,128)(2,1)} %collective-permute-done.24.refs_0_), channel_id=1, source_target_pairs={{4,12},{12,20},{20,28},{28,24},{24,16},{16,8},{8,0},{0,4},{5,13},{... | collective-permute-start | bytes 2359304 | tf_op jit(solution)/shard_map/ppermute | solution.py:257
  159.8 1.1 copy-done.3
  160.9 10.9 %form_project.13.refs_5_ = f32[512,512]{1,0:T(8,128)} custom-call(s32[1161]{0:T(1024)S(1)} %reshape.168.meta, bf16[256,1536]{1,0:T(8,128)(2,1)S(1)} %copy-done.3, bf16[256,1536]{1,0:T(8,128)(2,1)S(1)} %collective-permute-done.20.refs_1_, bf16[64,1536]{1,0:T(8,128)(2,1)S(1)} %collective-permute-done.17.refs_3_.refs_2_, ...), custom_call_target="tpu_custom_call", output_to_operand_aliasing={{}: (6, {})} | custom-call | flops 2147483648 | bytes 16777216 | tf_op jit(solution)/shard_map/form_project/pallas_call | solution.py:151
  171.9 12.3 %form_project.14.refs_5_ = f32[512,512]{1,0:T(8,128)} custom-call(s32[1161]{0:T(1024)S(1)} %reshape.168.meta, bf16[256,1536]{1,0:T(8,128)(2,1)} %collective-permute-done.24.refs_0_, bf16[256,1536]{1,0:T(8,128)(2,1)} %collective-permute-done.26.refs_1_, bf16[64,1536]{1,0:T(8,128)(2,1)S(1)} %collective-permute-done.14.refs_3_.refs_2_, ...), custom_call_target="tpu_custom_call", output_to_operand_aliasing={{}: (6, {})} | custom-call | flops 2147483648 | bytes 16777216 | tf_op jit(solution)/shard_map/form_project/pallas_call | solution.py:151
  184.2 12.3 %form_project.15 = f32[512,512]{1,0:T(8,128)} custom-call(s32[1161]{0:T(1024)S(1)} %reshape.168.meta, bf16[256,1536]{1,0:T(8,128)(2,1)} %collective-permute-done.27.refs_0_, bf16[256,1536]{1,0:T(8,128)(2,1)} %collective-permute-done.25.refs_1_, bf16[64,1536]{1,0:T(8,128)(2,1)S(1)} %collective-permute-done.9.refs_3_.refs_2_, ...), custom_call_target="tpu_custom_call", output_to_operand_aliasing={{}: (6, {})} | custom-call | flops 2147483648 | bytes 16777216 | tf_op jit(solution)/shard_map/form_project/pallas_call | solution.py:151
  196.6 1.1 dynamic-slice_bitcast_fusion
  197.8 1.9 collective-permute-done.28
  199.7 1.1 bitcast_add_fusion
  201.5 7.7 %collective-permute-done.29 = f32[1,128,512]{2,1,0:T(8,128)S(1)} collective-permute-done((f32[1,128,512]{2,1,0:T(8,128)S(1)}, f32[1,128,512]{2,1,0:T(8,128)S(1)}, u32[]{:S(2)}, u32[]{:S(2)}) %collective-permute-start.29) | collective-permute-done | bytes 262176 | tf_op jit(solution)/shard_map/ppermute | solution.py:176
  209.9 10.9 %all_to_all.5 = f32[8,34,128]{2,1,0:T(8,128)S(1)} all-to-all(f32[8,34,128]{2,1,0:T(8,128)S(1)} %select_maximum_fusion), channel_id=1, replica_groups=mesh['dp'=8,'fsdp'=4] {'dp'}, dimensions={0} | all-to-all | bytes 278528 | tf_op jit(solution)/shard_map/all_to_all | solution.py:307
  (90 shorter events, 13.9 us)
Async XLA Ops:
  6.5 0.9 copy-start
  6.5 5.0 %copy-start.10 = (s32[64]{0:T(128)S(1)}, s32[64]{0:T(128)}, u32[]{:S(2)}) copy-start(s32[64]{0:T(128)} %param.13) | copy-start | bytes 772
  6.5 11.7 %copy-start.6 = (bf16[64,32,512]{2,1,0:T(8,128)(2,1)S(1)}, bf16[64,32,512]{2,1,0:T(8,128)(2,1)}, u32[]{:S(2)}) copy-start(bf16[64,32,512]{2,1,0:T(8,128)(2,1)} %param.11) | copy-start | bytes 6291460
  11.0 17.0 %collective-permute-start.6 = (f32[32,2048]{1,0:T(8,128)S(1)}, f32[32,2048]{1,0:T(8,128)S(1)}, u32[]{:S(2)}, u32[]{:S(2)}) collective-permute-start(f32[32,2048]{1,0:T(8,128)S(1)} %dynamic-slice_bitcast_fusion.1), channel_id=1, source_target_pairs={{0,1},{1,0},{2,3},{3,2},{4,5},{5,4},{6,7},{7,6},{8,9},{9,8},{10,11... | collective-permute-start | bytes 786440 | tf_op jit(solution)/shard_map/ppermute | solution.py:222
  11.8 4.2 %collective-permute-start.1 = (s32[8,128]{1,0:T(8,128)S(1)}, s32[8,128]{1,0:T(8,128)S(1)}, u32[]{:S(2)}, u32[]{:S(2)}) collective-permute-start(s32[8,128]{1,0:T(8,128)S(1)} %dynamic_update_slice.5), channel_id=1, source_target_pairs={{0,4},{4,0},{8,12},{12,8},{16,20},{20,16},{24,28},{28,24},{1,5},{5... | collective-permute-start | bytes 12296 | tf_op jit(solution)/shard_map/ppermute | solution.py:183
  16.1 7.5 %collective-permute-start.2 = (s32[8,128]{1,0:T(8,128)S(1)}, s32[8,128]{1,0:T(8,128)S(1)}, u32[]{:S(2)}, u32[]{:S(2)}) collective-permute-start(s32[8,128]{1,0:T(8,128)S(1)} %add.131), channel_id=1, source_target_pairs={{0,8},{4,12},{8,0},{12,4},{16,24},{20,28},{24,16},{28,20},{1,9},{5... | collective-permute-start | bytes 12296 | tf_op jit(solution)/shard_map/ppermute | solution.py:183
  23.6 4.5 %collective-permute-start.3 = (s32[8,128]{1,0:T(8,128)S(1)}, s32[8,128]{1,0:T(8,128)S(1)}, u32[]{:S(2)}, u32[]{:S(2)}) collective-permute-start(s32[8,128]{1,0:T(8,128)S(1)} %add.132), channel_id=1, source_target_pairs={{0,16},{4,20},{8,24},{12,28},{16,0},{20,4},{24,8},{28,12},{1,17},{... | collective-permute-start | bytes 12296 | tf_op jit(solution)/shard_map/ppermute | solution.py:183
  28.1 12.5 %copy-start.11 = (s32[8]{0:T(128)S(1)}, s32[8]{0:T(128)}, u32[]{:S(2)}) copy-start(s32[8]{0:T(128)} %constant.111.clone) | copy-start | bytes 100
  28.1 28.4 %copy-start.4 = (s32[8]{0:T(128)S(1)}, s32[8]{0:T(128)}, u32[]{:S(2)}) copy-start(s32[8]{0:T(128)} %constant.112.clone) | copy-start | bytes 100
  28.1 6.4 %collective-permute-start.7 = (f32[32,2048]{1,0:T(8,128)S(1)}, f32[32,2048]{1,0:T(8,128)S(1)}, u32[]{:S(2)}, u32[]{:S(2)}) collective-permute-start(f32[32,2048]{1,0:T(8,128)S(1)} %bitcast_add_fusion.1), channel_id=1, source_target_pairs={{0,2},{1,3},{2,0},{3,1},{4,6},{5,7},{6,4},{7,5},{8,10},{9,11},{10,... | collective-permute-start | bytes 786440 | tf_op jit(solution)/shard_map/ppermute | solution.py:183
  31.2 19.3 %collective-permute-start.4 = (bf16[256,1536]{1,0:T(8,128)(2,1)S(1)}, bf16[256,1536]{1,0:T(8,128)(2,1)}, u32[]{:S(2)}, u32[]{:S(2)}) collective-permute-start(bf16[256,1536]{1,0:T(8,128)(2,1)S(1)} %get-tuple-element.109.refs_0_), channel_id=1, source_target_pairs={{4,12},{12,20},{20,28},{28,24},{24,16},{16,8},{8,0},{0,4},{5,13},{... | collective-permute-start | bytes 2359304 | tf_op jit(solution)/shard_map/ppermute | solution.py:257
  32.8 18.9 %collective-permute-start.5 = (bf16[256,1536]{1,0:T(8,128)(2,1)S(1)}, bf16[256,1536]{1,0:T(8,128)(2,1)S(1)}, u32[]{:S(2)}, u32[]{:S(2)}) collective-permute-start(bf16[256,1536]{1,0:T(8,128)(2,1)S(1)} %get-tuple-element.108.refs_1_), channel_id=1, source_target_pairs={{12,4},{20,12},{28,20},{24,28},{16,24},{8,16},{0,8},{4,0},{13,5},{... | collective-permute-start | bytes 2359304 | tf_op jit(solution)/shard_map/ppermute | solution.py:258
  34.6 23.4 %copy-start.8 = (bf16[32,2048]{1,0:T(8,128)(2,1)}, bf16[32,2048]{1,0:T(8,128)(2,1)S(1)}, u32[]{:S(2)}) copy-start(bf16[32,2048]{1,0:T(8,128)(2,1)S(1)} %multiply_convert_fusion) | copy-start | bytes 393220
  37.2 1.3 collective-permute-start.8
  38.5 15.3 %collective-permute-start.10 = (bf16[64,1536]{1,0:T(8,128)(2,1)S(1)}, bf16[64,1536]{1,0:T(8,128)(2,1)S(1)}, u32[]{:S(2)}, u32[]{:S(2)}) collective-permute-start(bf16[64,1536]{1,0:T(8,128)(2,1)S(1)} %maximum_select_fusion.2.refs_2_.refs_3_), channel_id=1, source_target_pairs={{12,4},{20,12},{28,20},{24,28},{16,24},{8,16},{0,8},{4,0},{13,5},{... | collective-permute-start | bytes 589832 | tf_op jit(solution)/shard_map/ppermute | solution.py:262
  38.7 15.0 %collective-permute-start.9 = (bf16[64,1536]{1,0:T(8,128)(2,1)S(1)}, bf16[64,1536]{1,0:T(8,128)(2,1)S(1)}, u32[]{:S(2)}, u32[]{:S(2)}) collective-permute-start(bf16[64,1536]{1,0:T(8,128)(2,1)S(1)} %maximum_select_fusion.2.refs_2_.refs_3_), channel_id=1, source_target_pairs={{4,12},{12,20},{20,28},{28,24},{24,16},{16,8},{8,0},{0,4},{5,13},{... | collective-permute-start | bytes 589832 | tf_op jit(solution)/shard_map/ppermute | solution.py:260
  53.8 22.4 %collective-permute-start.11 = (bf16[256,1536]{1,0:T(8,128)(2,1)}, bf16[256,1536]{1,0:T(8,128)(2,1)}, u32[]{:S(2)}, u32[]{:S(2)}) collective-permute-start(bf16[256,1536]{1,0:T(8,128)(2,1)} %collective-permute-done.4.refs_1_), channel_id=1, source_target_pairs={{4,12},{12,20},{20,28},{28,24},{24,16},{16,8},{8,0},{0,4},{5,13},{... | collective-permute-start | bytes 2359304 | tf_op jit(solution)/shard_map/ppermute | solution.py:257
  55.2 21.1 %collective-permute-start.12 = (bf16[256,1536]{1,0:T(8,128)(2,1)S(1)}, bf16[256,1536]{1,0:T(8,128)(2,1)}, u32[]{:S(2)}, u32[]{:S(2)}) collective-permute-start(bf16[256,1536]{1,0:T(8,128)(2,1)S(1)} %collective-permute-done.5.refs_0_), channel_id=1, source_target_pairs={{12,4},{20,12},{28,20},{24,28},{16,24},{8,16},{0,8},{4,0},{13,5},{... | collective-permute-start | bytes 2359304 | tf_op jit(solution)/shard_map/ppermute | solution.py:258
  58.0 16.7 %collective-permute-start.13 = (bf16[64,1536]{1,0:T(8,128)(2,1)S(1)}, bf16[64,1536]{1,0:T(8,128)(2,1)S(1)}, u32[]{:S(2)}, u32[]{:S(2)}) collective-permute-start(bf16[64,1536]{1,0:T(8,128)(2,1)S(1)} %collective-permute-done.9.refs_3_.refs_2_), channel_id=1, source_target_pairs={{4,12},{12,20},{20,28},{28,24},{24,16},{16,8},{8,0},{0,4},{5,13},{... | collective-permute-start | bytes 589832 | tf_op jit(solution)/shard_map/ppermute | solution.py:260
  59.7 16.5 %collective-permute-start.14 = (bf16[64,1536]{1,0:T(8,128)(2,1)S(1)}, bf16[64,1536]{1,0:T(8,128)(2,1)S(1)}, u32[]{:S(2)}, u32[]{:S(2)}) collective-permute-start(bf16[64,1536]{1,0:T(8,128)(2,1)S(1)} %collective-permute-done.10.refs_2_.refs_3_), channel_id=1, source_target_pairs={{12,4},{20,12},{28,20},{24,28},{16,24},{8,16},{0,8},{4,0},{13,5},{... | collective-permute-start | bytes 589832 | tf_op jit(solution)/shard_map/ppermute | solution.py:262
  76.2 22.1 %collective-permute-start.15 = (bf16[256,1536]{1,0:T(8,128)(2,1)}, bf16[256,1536]{1,0:T(8,128)(2,1)S(1)}, u32[]{:S(2)}, u32[]{:S(2)}) collective-permute-start(bf16[256,1536]{1,0:T(8,128)(2,1)} %collective-permute-done.11.refs_0_), channel_id=1, source_target_pairs={{4,12},{12,20},{20,28},{28,24},{24,16},{16,8},{8,0},{0,4},{5,13},{... | collective-permute-start | bytes 2359304 | tf_op jit(solution)/shard_map/ppermute | solution.py:257
  77.2 21.1 %collective-permute-start.16 = (bf16[256,1536]{1,0:T(8,128)(2,1)}, bf16[256,1536]{1,0:T(8,128)(2,1)S(1)}, u32[]{:S(2)}, u32[]{:S(2)}) collective-permute-start(bf16[256,1536]{1,0:T(8,128)(2,1)} %collective-permute-done.12.refs_1_), channel_id=1, source_target_pairs={{12,4},{20,12},{28,20},{24,28},{16,24},{8,16},{0,8},{4,0},{13,5},{... | collective-permute-start | bytes 2359304 | tf_op jit(solution)/shard_map/ppermute | solution.py:258
  78.3 18.8 %collective-permute-start.17 = (bf16[64,1536]{1,0:T(8,128)(2,1)S(1)}, bf16[64,1536]{1,0:T(8,128)(2,1)S(1)}, u32[]{:S(2)}, u32[]{:S(2)}) collective-permute-start(bf16[64,1536]{1,0:T(8,128)(2,1)S(1)} %collective-permute-done.13.refs_2_.refs_3_), channel_id=1, source_target_pairs={{4,12},{12,20},{20,28},{28,24},{24,16},{16,8},{8,0},{0,4},{5,13},{... | collective-permute-start | bytes 589832 | tf_op jit(solution)/shard_map/ppermute | solution.py:260
  79.3 19.1 %collective-permute-start.18 = (bf16[64,1536]{1,0:T(8,128)(2,1)S(1)}, bf16[64,1536]{1,0:T(8,128)(2,1)S(1)}, u32[]{:S(2)}, u32[]{:S(2)}) collective-permute-start(bf16[64,1536]{1,0:T(8,128)(2,1)S(1)} %collective-permute-done.14.refs_3_.refs_2_), channel_id=1, source_target_pairs={{12,4},{20,12},{28,20},{24,28},{16,24},{8,16},{0,8},{4,0},{13,5},{... | collective-permute-start | bytes 589832 | tf_op jit(solution)/shard_map/ppermute | solution.py:262
  98.3 21.9 %collective-permute-start.19 = (bf16[256,1536]{1,0:T(8,128)(2,1)S(1)}, bf16[256,1536]{1,0:T(8,128)(2,1)S(1)}, u32[]{:S(2)}, u32[]{:S(2)}) collective-permute-start(bf16[256,1536]{1,0:T(8,128)(2,1)S(1)} %collective-permute-done.15.refs_1_), channel_id=1, source_target_pairs={{4,12},{12,20},{20,28},{28,24},{24,16},{16,8},{8,0},{0,4},{5,13},{... | collective-permute-start | bytes 2359304 | tf_op jit(solution)/shard_map/ppermute | solution.py:257
  99.4 20.9 %collective-permute-start.20 = (bf16[256,1536]{1,0:T(8,128)(2,1)S(1)}, bf16[256,1536]{1,0:T(8,128)(2,1)S(1)}, u32[]{:S(2)}, u32[]{:S(2)}) collective-permute-start(bf16[256,1536]{1,0:T(8,128)(2,1)S(1)} %collective-permute-done.16.refs_0_), channel_id=1, source_target_pairs={{12,4},{20,12},{28,20},{24,28},{16,24},{8,16},{0,8},{4,0},{13,5},{... | collective-permute-start | bytes 2359304 | tf_op jit(solution)/shard_map/ppermute | solution.py:258
  100.4 19.9 %collective-permute-start.21 = (bf16[64,1536]{1,0:T(8,128)(2,1)S(1)}, bf16[64,1536]{1,0:T(8,128)(2,1)S(1)}, u32[]{:S(2)}, u32[]{:S(2)}) collective-permute-start(bf16[64,1536]{1,0:T(8,128)(2,1)S(1)} %collective-permute-done.17.refs_3_.refs_2_), channel_id=1, source_target_pairs={{4,12},{12,20},{20,28},{28,24},{24,16},{16,8},{8,0},{0,4},{5,13},{... | collective-permute-start | bytes 589832 | tf_op jit(solution)/shard_map/ppermute | solution.py:260
  120.3 17.7 %collective-permute-start.22 = (bf16[256,1536]{1,0:T(8,128)(2,1)S(1)}, bf16[256,1536]{1,0:T(8,128)(2,1)S(1)}, u32[]{:S(2)}, u32[]{:S(2)}) collective-permute-start(bf16[256,1536]{1,0:T(8,128)(2,1)S(1)} %collective-permute-done.19.refs_0_), channel_id=1, source_target_pairs={{4,12},{12,20},{20,28},{28,24},{24,16},{16,8},{8,0},{0,4},{5,13},{... | collective-permute-start | bytes 2359304 | tf_op jit(solution)/shard_map/ppermute | solution.py:257
  121.3 16.7 %collective-permute-start.23 = (bf16[256,1536]{1,0:T(8,128)(2,1)S(1)}, bf16[256,1536]{1,0:T(8,128)(2,1)S(1)}, u32[]{:S(2)}, u32[]{:S(2)}) collective-permute-start(bf16[256,1536]{1,0:T(8,128)(2,1)S(1)} %collective-permute-done.20.refs_1_), channel_id=1, source_target_pairs={{12,4},{20,12},{28,20},{24,28},{16,24},{8,16},{0,8},{4,0},{13,5},{... | collective-permute-start | bytes 2359304 | tf_op jit(solution)/shard_map/ppermute | solution.py:258
  138.0 13.0 %copy-start.2 = (bf16[256,1536]{1,0:T(8,128)(2,1)}, bf16[256,1536]{1,0:T(8,128)(2,1)S(1)}, u32[]{:S(2)}) copy-start(bf16[256,1536]{1,0:T(8,128)(2,1)S(1)} %collective-permute-done.23.refs_0_) | copy-start | bytes 2359300
  138.0 17.4 %collective-permute-start.24 = (bf16[256,1536]{1,0:T(8,128)(2,1)S(1)}, bf16[256,1536]{1,0:T(8,128)(2,1)}, u32[]{:S(2)}, u32[]{:S(2)}) collective-permute-start(bf16[256,1536]{1,0:T(8,128)(2,1)S(1)} %collective-permute-done.22.refs_1_), channel_id=1, source_target_pairs={{4,12},{12,20},{20,28},{28,24},{24,16},{16,8},{8,0},{0,4},{5,13},{... | collective-permute-start | bytes 2359304 | tf_op jit(solution)/shard_map/ppermute | solution.py:257
  139.1 16.6 %collective-permute-start.25 = (bf16[256,1536]{1,0:T(8,128)(2,1)S(1)}, bf16[256,1536]{1,0:T(8,128)(2,1)}, u32[]{:S(2)}, u32[]{:S(2)}) collective-permute-start(bf16[256,1536]{1,0:T(8,128)(2,1)S(1)} %collective-permute-done.23.refs_0_), channel_id=1, source_target_pairs={{12,4},{20,12},{28,20},{24,28},{16,24},{8,16},{0,8},{4,0},{13,5},{... | collective-permute-start | bytes 2359304 | tf_op jit(solution)/shard_map/ppermute | solution.py:258
  150.9 4.7 %copy-start.5 = (f32[512,512]{1,0:T(8,128)}, f32[512,512]{1,0:T(8,128)S(1)}, u32[]{:S(2)}) copy-start(f32[512,512]{1,0:T(8,128)S(1)} %form_project.12.refs_5_) | copy-start | bytes 3145732
  155.7 16.2 %collective-permute-start.26 = (bf16[256,1536]{1,0:T(8,128)(2,1)}, bf16[256,1536]{1,0:T(8,128)(2,1)}, u32[]{:S(2)}, u32[]{:S(2)}) collective-permute-start(bf16[256,1536]{1,0:T(8,128)(2,1)} %collective-permute-done.24.refs_0_), channel_id=1, source_target_pairs={{4,12},{12,20},{20,28},{28,24},{24,16},{16,8},{8,0},{0,4},{5,13},{... | collective-permute-start | bytes 2359304 | tf_op jit(solution)/shard_map/ppermute | solution.py:257
  158.3 13.6 %collective-permute-start.27 = (bf16[256,1536]{1,0:T(8,128)(2,1)}, bf16[256,1536]{1,0:T(8,128)(2,1)}, u32[]{:S(2)}, u32[]{:S(2)}) collective-permute-start(bf16[256,1536]{1,0:T(8,128)(2,1)} %collective-permute-done.25.refs_1_), channel_id=1, source_target_pairs={{12,4},{20,12},{28,20},{24,28},{16,24},{8,16},{0,8},{4,0},{13,5},{... | collective-permute-start | bytes 2359304 | tf_op jit(solution)/shard_map/ppermute | solution.py:258
  159.8 1.1 copy-start.3
  171.9 12.3 %copy-start.9 = (bf16[32,2048]{1,0:T(8,128)(2,1)S(1)}, bf16[32,2048]{1,0:T(8,128)(2,1)}, u32[]{:S(2)}) copy-start(bf16[32,2048]{1,0:T(8,128)(2,1)} %copy-done.8) | copy-start | bytes 393220
  196.6 4.8 %copy-start.7 = (bf16[256,512]{1,0:T(8,128)(2,1)S(1)}, bf16[256,512]{1,0:T(8,128)(2,1)}, u32[]{:S(2)}) copy-start(bf16[256,512]{1,0:T(8,128)(2,1)} %param.15) | copy-start | bytes 786436
  196.6 25.0 %copy-start.1 = (bf16[64,1024]{1,0:T(8,128)(2,1)S(1)}, bf16[64,1024]{1,0:T(8,128)(2,1)}, u32[]{:S(2)}) copy-start(bf16[64,1024]{1,0:T(8,128)(2,1)} %param.12) | copy-start | bytes 393220
  197.7 2.0 collective-permute-start.28
  200.9 8.4 %collective-permute-start.29 = (f32[1,128,512]{2,1,0:T(8,128)S(1)}, f32[1,128,512]{2,1,0:T(8,128)S(1)}, u32[]{:S(2)}, u32[]{:S(2)}) collective-permute-start(f32[1,128,512]{2,1,0:T(8,128)S(1)} %constant_dynamic-slice_fusion), channel_id=1, source_target_pairs={{0,2},{1,3},{2,0},{3,1},{4,6},{5,7},{6,4},{7,5},{8,10},{9,11},{10,... | collective-permute-start | bytes 786440 | tf_op jit(solution)/shard_map/ppermute | solution.py:176

commit v2 on v1

--- a/solution.py
+++ b/solution.py
@@ -26,15 +26,14 @@
     return path + [z * ny for z in reversed(range(nz))]
 
 
-def form_project_kernel(dims, meta, *refs):
-    shards, parts, row, pool, rank, pairs, block, first_row = dims
-    g_refs = [refs[k * parts : (k + 1) * parts] for k in range(shards)]
-    a_refs = refs[shards * parts : shards * (parts + 1)]
-    p_hbm, acc_hbm, out_hbm, pbuf, s_ref, held, p_sems, acc_sems = refs[shards * (parts + 1) :]
+def form_project_kernel(dims, blocks_ref, *refs):
+    shards, row, pool, rank, pairs, block, first_row = dims
+    g_refs, a_refs = refs[:shards], refs[shards : 2 * shards]
+    p_hbm, acc_hbm, out_hbm, pbuf, s_ref, held, words, meta, p_sems, acc_sems = refs[2 * shards :]
     blocks = pairs // block
     rows = block * rank
-    width = 1 + 2 * pool
     stride = shards * pool + 8
+    room = g_refs[0].shape[1]
 
     def p_copy(i, h):
         start = pl.multiple_of(first_row + (h * pairs + i * block) * rank, rank)
@@ -43,7 +42,7 @@
         )
 
     def acc_rows(k):
-        return pl.ds(pl.multiple_of(meta[(row + k) * width] * pool, pool), pool)
+        return pl.ds(pl.multiple_of(blocks_ref[row + k] * pool, pool), pool)
 
     def acc_load(k):
         return pltpu.make_async_copy(
@@ -60,23 +59,30 @@
             p_copy(i, h).start()
     for k in range(shards):
         acc_load(k).start()
-    tiles = a_refs[0].shape[1] // LANES
+        words[k] = a_refs[k][: 2 * 8, room:].astype(F32).astype(jnp.int32)
+    to_scalars = [
+        pltpu.make_async_copy(words.at[k, pl.ds(0, 8)], meta.at[k], acc_sems.at[2, k])
+        for k in range(shards)
+    ]
+    for copy in to_scalars:
+        copy.start()
+    tiles = room // LANES
     low = lax.broadcasted_iota(jnp.int32, (pairs, LANES), 1) < rank
     lane = lax.broadcasted_iota(jnp.int32, (rank, 2 * LANES), 1)
 
     for k in range(shards):
-        first = (row + k) * width + 1
-
-        def two_examples(p, carry, k=k, first=first):
+        to_scalars[k].wait()
+
+        def two_examples(p, carry, k=k):
             e = 2 * p
-            tile = jnp.minimum(meta[first + e] // LANES, tiles - 2)
+            tile = jnp.minimum(meta[k, 1, e], tiles - 2)
             base = pl.multiple_of(tile * LANES, LANES)
-            g = jnp.concatenate([g_ref[:, pl.ds(base, 2 * LANES)] for g_ref in g_refs[k]], axis=0)
+            g = g_refs[k][:, pl.ds(base, 2 * LANES)]
             a = a_refs[k][:, pl.ds(base, 2 * LANES)]
             masked = []
             for j in range(2):
-                begin = meta[first + e + j] - base
-                end = begin + meta[first + pool + e + j]
+                begin = meta[k, 1, e + j] * LANES + meta[k, 2, e + j] - base
+                end = begin + meta[k, 0, e + j]
                 part = jnp.where((lane >= begin) & (lane < end), a, jnp.zeros_like(a))
                 masked += [part, part]
             formed = lax.dot_general(
@@ -124,16 +130,16 @@
         acc_store(k).wait()
 
 
-def form_project(acc, meta, row, gs, acts, projection, half, pool):
-    shards, parts = len(gs), len(gs[0])
-    outs = parts * gs[0][0].shape[0]
-    rank, room = acts[0].shape
+def form_project(acc, blocks, row, gs, acts, projection, half, pool):
+    shards = len(gs)
+    outs = gs[0].shape[0]
+    rank = acts[0].shape[0]
     feats = projection.shape[1]
     pairs = outs // 2
     block = min(16, pairs)
-    dims = (shards, parts, row, pool, rank, pairs, block, half * outs * rank)
+    dims = (shards, row, pool, rank, pairs, block, half * outs * rank)
     whole = lambda x: pl.BlockSpec(x.shape, lambda i, m: (0, 0))
-    flat = [g for group in gs for g in group]
+    flat = list(gs)
     spec = pltpu.PrefetchScalarGridSpec(
         num_scalar_prefetch=1,
         grid=(1,),
@@ -142,10 +148,12 @@
         out_specs=pl.BlockSpec(memory_space=pl.ANY),
         scratch_shapes=[
             pltpu.VMEM((pairs // block, 2, block * rank, feats), BF16),
-            pltpu.VMEM((pairs * (shards * pool + 8), LANES), F32),
+            pltpu.VMEM(((pairs + 1) * (shards * pool + 8), LANES), F32),
             pltpu.VMEM((shards * pool, feats), F32),
+            pltpu.VMEM((shards, 16, LANES), jnp.int32),
+            pltpu.SMEM((shards, 8, LANES), jnp.int32),
             pltpu.SemaphoreType.DMA((pairs // block, 2)),
-            pltpu.SemaphoreType.DMA((2, shards)),
+            pltpu.SemaphoreType.DMA((3, shards)),
         ],
     )
     return pl.pallas_call(
@@ -160,7 +168,7 @@
             transcendentals=0,
         ),
         name="form_project",
-    )(meta, *flat, *acts, projection, acc)
+    )(blocks, *flat, *acts, projection, acc)
 
 
 def exchange_sum(x, axis, n):
@@ -231,55 +239,60 @@
             jnp.concatenate([other, mine], axis=0),
         )
 
-    own_acts = both_halves(
-        jnp.dot(acts_half, select, preferred_element_type=F32).astype(BF16)
-    )
-
-    own = jnp.concatenate([starts, counts])
-    table = lax.dynamic_update_slice(jnp.zeros((dp, 2 * pool), jnp.int32), own[None], (me, 0))
-    table, packed = lax.optimization_barrier((exchange_total(table, "dp", dp), packed))
-    overflow = jnp.max(jnp.sum(table[:, pool:], axis=1)) > room
+    words = jnp.stack([counts, starts // LANES, starts % LANES]).astype(BF16)
+    words = jnp.pad(words, ((0, rank // 2 - 3), (0, -pool % LANES)))
+    own_half = jnp.dot(acts_half, select, preferred_element_type=F32).astype(BF16)
+    own_acts = both_halves(jnp.concatenate([own_half, words], axis=1))
     my_position = jnp.asarray(np.argsort(order), jnp.int32)[me]
     blocks = jnp.asarray(order, jnp.int32)[(my_position - jnp.arange(dp + 1)) % dp]
-    meta = jnp.concatenate([blocks[:, None], table[blocks]], axis=1).reshape(-1)
 
     acts = {0: own_acts, dp: own_acts}
-    low, high = {0: packed[:half]}, {0: packed[half:]}
+    low, high = {0: packed[:half]}, {dp: packed[half:]}
     acc = jnp.zeros((dp * pool, feats), F32)
+
+    def add(acc, first, gs, which):
+        return form_project(
+            acc, blocks, first, [gs[first], gs[first + 1]], [acts[first], acts[first + 1]],
+            projection, which, pool,
+        )
+
     for s in range(dp):
         if s > 0:
-            keys = [k for k in (s, dp - s) if k in acts]
-            low[s], high[s], acc, *fresh = lax.optimization_barrier(
-                (low[s], high[s], acc, *[acts[k] for k in keys])
+            keys = [k for k in dict.fromkeys((s, dp - s)) if k in acts]
+            low[s], high[dp - s], acc, *fresh = lax.optimization_barrier(
+                (low[s], high[dp - s], acc, *[acts[k] for k in keys])
             )
             acts.update(zip(keys, fresh))
         if s + 1 < dp:
             low[s + 1] = lax.ppermute(low[s], "dp", ahead)
-            high[s + 1] = lax.ppermute(high[s], "dp", back)
+            high[dp - s - 1] = lax.ppermute(high[dp - s], "dp", back)
         if 2 * (s + 1) <= dp:
             acts[s + 1] = lax.ppermute(acts[s], "dp", ahead)
         if 2 * (s + 1) < dp:
             acts[dp - s - 1] = lax.ppermute(acts[dp - s], "dp", back)
         if s % 2 == 1:
-            rows = [s - 1, s]
-            acc = form_project(
-                acc, meta, s - 1, [[low[i]] for i in rows], [acts[i] for i in rows],
-                projection, 0, pool,
-            )
-        if s > 0 and (s % 2 == 0 or s == dp - 1):
-            rows = [s - s % 2, s - s % 2 + 1] if s == dp - 1 else [s - 2, s - 1]
-            rows = [dp - rows[1], dp - rows[0]]
-            acc = form_project(
-                acc, meta, rows[0], [[high[dp - i]] for i in rows], [acts[i] for i in rows],
-                projection, 1, pool,
-            )
+            acc = add(acc, s - 1, low, 0)
+        if s > 0 and s % 2 == 0:
+            acc = add(acc, dp - s + 1, high, 1)
+        if s == dp - 1:
+            acc = add(acc, 1, high, 1)
+
+    used = jnp.stack([acts[i][0, room : room + pool] for i in range(dp)]).astype(jnp.int32)
+    overflow = jnp.max(jnp.sum(used, axis=1)) > room
 
     def padded(acc):
         mine = both_halves(acts_half).reshape(rank, pool, length)
         grads = jnp.einsum("elo,rel->eor", grad_rows, mine, preferred_element_type=F32)
         grads = grads.astype(BF16).reshape(pool, outs * rank)
-        grads = lax.all_gather(grads, "dp", axis=0, tiled=True)
-        return jnp.dot(grads, projection, preferred_element_type=F32)
+
+        def step(s, state):
+            acc, grads = state
+            part = jnp.dot(grads, projection, preferred_element_type=F32)
+            block = lax.dynamic_index_in_dim(blocks, s, 0, keepdims=False)
+            acc = lax.dynamic_update_slice(acc, part, (block * pool, 0))
+            return acc, lax.ppermute(grads, "dp", ahead)
+
+        return lax.fori_loop(0, dp, step, (acc, grads))[0]
 
     acc = lax.cond(overflow, padded, lambda acc: acc, acc)
     pooled = exchange_sum(acc.reshape(fsdp, dp * pool // fsdp, feats), "fsdp", fsdp)

time: 229 us -> 209 us (0.913)
  between operations: 14.4 us -> 0.98 us
  starting transfers between devices: 32 us -> 26.9 us
    ppermute x4 -> x1, starting transfers between devices: 8.91 us -> 1.92 us  [exchange_total(): x = x + lax.ppermute(x, axis, [(i, i ^ bit) for i in range(n)])]
    ppermute x7, waiting for transfers between devices: 17.4 us -> 10.7 us  [per_device(): low[s + 1] = lax.ppermute(low[s], 'dp', ahead)]
    ppermute x4, waiting for transfers between devices: 15.1 us -> 21.3 us  [per_device(): acts[s + 1] = lax.ppermute(acts[s], 'dp', ahead)]
    ppermute x3, waiting for transfers between devices: 4.9 us -> 2.11 us  [per_device(): acts[dp - s - 1] = lax.ppermute(acts[dp - s], 'dp', back)]
    ppermute x4 -> x1, waiting for transfers between devices: 4.63 us -> 6.54 us  [exchange_total(): x = x + lax.ppermute(x, axis, [(i, i ^ bit) for i in range(n)])]
  transfers between devices with their start and end apart: 29 -> 26, of which waited for: 17 -> 15; matrix products, arithmetic and copies ran while one was open for 6% -> 5% of each run, Pallas kernels for 30% -> 34%
where the time goes in v2:
time: 209 us; the launch traced here: 208 us
  Pallas kernels  94.3 us (45%)
  waiting for transfers between devices  52.2 us (25%)
  starting transfers between devices  26.9 us (13%)
  blocking collectives  12.4 us (6%)
  matrix products  10.7 us (5%)
  local copies, waits for them, and re-layouts  5.74 us (3%)
  other arithmetic  4.9 us (2%)
    pallas_call x8, Pallas kernels, form_project(): pl.pallas_call(functools.partial(form_project_kernel, dims), out_shape=ja...  94.3 us
    ppermute x4, waiting for transfers between devices, per_device(): acts[s + 1] = lax.ppermute(acts[s], 'dp', ahead)  21.3 us
    all_to_all x1, blocking collectives, per_device(): got = jnp.sum(lax.all_to_all(sent, 'dp', 0, 0), axis=0)  12.4 us
    ppermute x7, starting transfers between devices, per_device(): low[s + 1] = lax.ppermute(low[s], 'dp', ahead)  11.9 us
    ppermute x7, waiting for transfers between devices, per_device(): low[s + 1] = lax.ppermute(low[s], 'dp', ahead)  10.7 us
    ppermute x2, waiting for transfers between devices, exchange_sum(): slots = keep + lax.ppermute(send, axis, swap)  8.47 us
    ppermute x1, waiting for transfers between devices, exchange_total(): x = x + lax.ppermute(x, axis, [(i, i ^ bit) for i in range(n)])  6.54 us
    ppermute x4, starting transfers between devices, per_device(): acts[s + 1] = lax.ppermute(acts[s], 'dp', ahead)  6.18 us
  transfers between devices with their start and end apart: 26, of which 15 were waited for; matrix products, arithmetic and copies ran while one was open for 5% of the time, Pallas kernels for 34%

profile of v2, /device:TPU:0, one launch (start us, length us, event | category | flops | bytes accessed | tf_op | source)
XLA Modules:
  0.0 208.4 jit_solution(515617578243925819)
XLA Ops:
  0.0 0.9 copy-done
  0.9 3.6 %fusion.37 = f32[2,32,2048]{2,1,0:T(8,128)S(1)} fusion(bf16[2,32,1024]{2,1,0:T(8,128)(2,1)S(1)} %bitcast.78, bf16[2048,1024,1]{1,0,2:T(8,128)(2,1)} %bitcast.81), kind=kOutput, calls=%fused_computation.79 | convolution fusion | flops 268435456 | bytes 4849664 | tf_op jit(solution)/shard_map/dot_general | solution.py:222
  4.5 0.8 copy-done.4
  6.2 4.2 %fusion.12 = bf16[512,1536]{1,0:T(8,128)(2,1)S(1)} fusion(bf16[2048,512]{1,0:T(8,128)(2,1)S(1)} %bitcast.82, s32[2048]{0:T(1024)S(1)} %select_n.142), kind=kOutput, calls=%fused_computation.17 | convolution fusion | flops 3225157632 | bytes 3678208 | tf_op jit(solution)/shard_map/dot_general | solution.py:208
  10.4 2.6 %collective-permute-start.5 = (bf16[256,1536]{1,0:T(8,128)(2,1)S(1)}, bf16[256,1536]{1,0:T(8,128)(2,1)}, u32[]{:S(2)}, u32[]{:S(2)}) collective-permute-start(bf16[256,1536]{1,0:T(8,128)(2,1)S(1)} %get-tuple-element.219.refs_0_), channel_id=1, source_target_pairs={{4,12},{12,20},{20,28},{28,24},{24,16},{16,8},{8,0},{0,4},{5,13},{... | collective-permute-start | bytes 2359304 | tf_op jit(solution)/shard_map/ppermute | solution.py:267
  13.2 1.1 bitcast_add_fusion.1
  14.3 1.9 collective-permute-start.3
  16.2 6.5 %collective-permute-done.3 = f32[32,2048]{1,0:T(8,128)S(1)} collective-permute-done((f32[32,2048]{1,0:T(8,128)S(1)}, f32[32,2048]{1,0:T(8,128)S(1)}, u32[]{:S(2)}, u32[]{:S(2)}) %collective-permute-start.3) | collective-permute-done | bytes 262176 | tf_op jit(solution)/shard_map/ppermute | solution.py:191
  22.8 2.5 %fusion.13 = bf16[32,1536]{1,0:T(8,128)(2,1)S(1)} fusion(bf16[32,2048]{1,0:T(8,128)(2,1)S(1)} %multiply_convert_fusion, s32[2048]{0:T(1024)S(1)} %select_n.142), kind=kOutput, calls=%fused_computation.18 | convolution fusion | flops 204521472 | bytes 237568 | tf_op jit(solution)/shard_map/dot_general | solution.py:244
  25.5 1.3 collective-permute-done.4
  26.8 1.7 collective-permute-start.7
  28.9 2.7 %collective-permute-done.5.refs_1_ = bf16[256,1536]{1,0:T(8,128)(2,1)} collective-permute-done((bf16[256,1536]{1,0:T(8,128)(2,1)S(1)}, bf16[256,1536]{1,0:T(8,128)(2,1)}, u32[]{:S(2)}, u32[]{:S(2)}) %collective-permute-start.5) | collective-permute-done | bytes 786464 | tf_op jit(solution)/shard_map/ppermute | solution.py:267
  31.6 1.8 collective-permute-done.6.refs_0_
  33.4 2.4 %collective-permute-done.7.refs_3_.refs_2_ = bf16[64,1664]{1,0:T(8,128)(2,1)S(1)} collective-permute-done((bf16[64,1664]{1,0:T(8,128)(2,1)S(1)}, bf16[64,1664]{1,0:T(8,128)(2,1)S(1)}, u32[]{:S(2)}, u32[]{:S(2)}) %collective-permute-start.7) | collective-permute-done | bytes 213024 | tf_op jit(solution)/shard_map/ppermute | solution.py:270
  35.9 1.4 collective-permute-done.8.refs_2_.refs_3_
  37.7 1.6 collective-permute-start.9
  40.6 1.6 collective-permute-start.11
  43.4 12.5 %form_project.8.refs_5_ = f32[512,512]{1,0:T(8,128)S(1)} custom-call(s32[9]{0:T(128)S(1)} %gather_fusion, bf16[256,1536]{1,0:T(8,128)(2,1)S(1)} %get-tuple-element.219.refs_0_, bf16[256,1536]{1,0:T(8,128)(2,1)} %collective-permute-done.5.refs_1_, bf16[64,1664]{1,0:T(8,128)(2,1)S(1)} %maximum_select_fusion.2.refs_2_.refs_3_, ...), custom_call_target="tpu_custom_call", output_to_operand_aliasing={{}: (6, {})} | custom-call | flops 2147483648 | bytes 16777216 | tf_op jit(solution)/shard_map/form_project/pallas_call | solution.py:159
  55.9 5.4 %collective-permute-done.11.refs_2_.refs_3_ = bf16[64,1664]{1,0:T(8,128)(2,1)S(1)} collective-permute-done((bf16[64,1664]{1,0:T(8,128)(2,1)S(1)}, bf16[64,1664]{1,0:T(8,128)(2,1)S(1)}, u32[]{:S(2)}, u32[]{:S(2)}) %collective-permute-start.11) | collective-permute-done | bytes 213024 | tf_op jit(solution)/shard_map/ppermute | solution.py:270
  61.3 1.4 collective-permute-start.13
  62.7 0.7 collective-permute-start.14
  63.4 1.3 collective-permute-start.15
  64.7 0.7 collective-permute-start.16
  65.4 11.4 %form_project.9.refs_5_ = f32[512,512]{1,0:T(8,128)S(1)} custom-call(s32[9]{0:T(128)S(1)} %gather_fusion, bf16[256,1536]{1,0:T(8,128)(2,1)S(1)} %collective-permute-done.6.refs_0_, bf16[256,1536]{1,0:T(8,128)(2,1)S(1)} %get-tuple-element.218.refs_1_, bf16[64,1664]{1,0:T(8,128)(2,1)S(1)} %collective-permute-done.8.refs_2_.refs_3_, ...), custom_call_target="tpu_custom_call", output_to_operand_aliasing={{}: (6, {})} | custom-call | flops 2147483648 | bytes 16777216 | tf_op jit(solution)/shard_map/form_project/pallas_call | solution.py:159
  76.8 7.3 %collective-permute-done.15.refs_3_.refs_2_ = bf16[64,1664]{1,0:T(8,128)(2,1)S(1)} collective-permute-done((bf16[64,1664]{1,0:T(8,128)(2,1)S(1)}, bf16[64,1664]{1,0:T(8,128)(2,1)S(1)}, u32[]{:S(2)}, u32[]{:S(2)}) %collective-permute-start.15) | collective-permute-done | bytes 213024 | tf_op jit(solution)/shard_map/ppermute | solution.py:270
  84.1 0.7 collective-permute-done.16.refs_2_.refs_3_
  84.8 1.6 collective-permute-start.17
  86.9 1.6 collective-permute-start.19
  88.4 12.5 %form_project.10.refs_5_ = f32[512,512]{1,0:T(8,128)S(1)} custom-call(s32[9]{0:T(128)S(1)} %gather_fusion, bf16[256,1536]{1,0:T(8,128)(2,1)} %collective-permute-done.9.refs_0_, bf16[256,1536]{1,0:T(8,128)(2,1)S(1)} %collective-permute-done.13.refs_1_, bf16[64,1664]{1,0:T(8,128)(2,1)S(1)} %collective-permute-done.11.refs_2_.refs_3_, ...), custom_call_target="tpu_custom_call", output_to_operand_aliasing={{}: (6, {})} | custom-call | flops 2147483648 | bytes 16777216 | tf_op jit(solution)/shard_map/form_project/pallas_call | solution.py:159
  100.9 6.2 %collective-permute-done.19.refs_2_.refs_3_ = bf16[64,1664]{1,0:T(8,128)(2,1)S(1)} collective-permute-done((bf16[64,1664]{1,0:T(8,128)(2,1)S(1)}, bf16[64,1664]{1,0:T(8,128)(2,1)S(1)}, u32[]{:S(2)}, u32[]{:S(2)}) %collective-permute-start.19) | collective-permute-done | bytes 213024 | tf_op jit(solution)/shard_map/ppermute | solution.py:270
  107.1 1.6 collective-permute-start.20
  109.1 12.5 %form_project.11.refs_5_ = f32[512,512]{1,0:T(8,128)S(1)} custom-call(s32[9]{0:T(128)S(1)} %gather_fusion, bf16[256,1536]{1,0:T(8,128)(2,1)S(1)} %collective-permute-done.14.refs_0_, bf16[256,1536]{1,0:T(8,128)(2,1)} %collective-permute-done.10.refs_1_, bf16[64,1664]{1,0:T(8,128)(2,1)S(1)} %collective-permute-done.16.refs_2_.refs_3_, ...), custom_call_target="tpu_custom_call", output_to_operand_aliasing={{}: (6, {})} | custom-call | flops 2147483648 | bytes 16777216 | tf_op jit(solution)/shard_map/form_project/pallas_call | solution.py:159
  121.6 3.2 %collective-permute-done.20.refs_1_ = bf16[256,1536]{1,0:T(8,128)(2,1)S(1)} collective-permute-done((bf16[256,1536]{1,0:T(8,128)(2,1)S(1)}, bf16[256,1536]{1,0:T(8,128)(2,1)S(1)}, u32[]{:S(2)}, u32[]{:S(2)}) %collective-permute-start.20) | collective-permute-done | bytes 786464 | tf_op jit(solution)/shard_map/ppermute | solution.py:267
  124.8 1.6 collective-permute-start.22
  126.8 11.4 %form_project.12.refs_5_ = f32[512,512]{1,0:T(8,128)S(1)} custom-call(s32[9]{0:T(128)S(1)} %gather_fusion, bf16[256,1536]{1,0:T(8,128)(2,1)S(1)} %collective-permute-done.17.refs_0_, bf16[256,1536]{1,0:T(8,128)(2,1)S(1)} %collective-permute-done.20.refs_1_, ...), custom_call_target="tpu_custom_call", output_to_operand_aliasing={{}: (6, {})} | custom-call | flops 2147483648 | bytes 16777216 | tf_op jit(solution)/shard_map/form_project/pallas_call | solution.py:159
  138.2 4.3 %collective-permute-done.22.refs_0_ = bf16[256,1536]{1,0:T(8,128)(2,1)S(1)} collective-permute-done((bf16[256,1536]{1,0:T(8,128)(2,1)S(1)}, bf16[256,1536]{1,0:T(8,128)(2,1)S(1)}, u32[]{:S(2)}, u32[]{:S(2)}) %collective-permute-start.22) | collective-permute-done | bytes 786464 | tf_op jit(solution)/shard_map/ppermute | solution.py:267
  142.5 1.6 collective-permute-start.24
  144.6 11.4 %form_project.13.refs_5_ = f32[512,512]{1,0:T(8,128)S(1)} custom-call(s32[9]{0:T(128)S(1)} %gather_fusion, bf16[256,1536]{1,0:T(8,128)(2,1)S(1)} %collective-permute-done.21.refs_0_, bf16[256,1536]{1,0:T(8,128)(2,1)S(1)} %collective-permute-done.18.refs_1_, ...), custom_call_target="tpu_custom_call", output_to_operand_aliasing={{}: (6, {})} | custom-call | flops 2147483648 | bytes 16777216 | tf_op jit(solution)/shard_map/form_project/pallas_call | solution.py:159
  156.4 11.4 %form_project.14.refs_5_ = f32[512,512]{1,0:T(8,128)S(1)} custom-call(s32[9]{0:T(128)S(1)} %gather_fusion, bf16[256,1536]{1,0:T(8,128)(2,1)S(1)} %collective-permute-done.22.refs_0_, bf16[256,1536]{1,0:T(8,128)(2,1)S(1)} %collective-permute-done.24.refs_1_, ...), custom_call_target="tpu_custom_call", output_to_operand_aliasing={{}: (6, {})} | custom-call | flops 2147483648 | bytes 16777216 | tf_op jit(solution)/shard_map/form_project/pallas_call | solution.py:159
  167.8 11.4 %form_project.15 = f32[512,512]{1,0:T(8,128)S(1)} custom-call(s32[9]{0:T(128)S(1)} %gather_fusion, bf16[256,1536]{1,0:T(8,128)(2,1)S(1)} %collective-permute-done.25.refs_0_, bf16[256,1536]{1,0:T(8,128)(2,1)S(1)} %collective-permute-done.23.refs_1_, bf16[64,1664]{1,0:T(8,128)(2,1)S(1)} %collective-permute-done.7.refs_3_.refs_2_, ...), custom_call_target="tpu_custom_call", output_to_operand_aliasing={{}: (6, {})} | custom-call | flops 2147483648 | bytes 16777216 | tf_op jit(solution)/shard_map/form_project/pallas_call | solution.py:159
  179.2 1.0 copy-done.3
  181.9 1.1 dynamic-slice_bitcast_fusion
  183.1 1.9 collective-permute-done.26
  185.0 1.1 bitcast_add_fusion
  186.1 1.6 collective-permute-start.27
  187.9 6.6 %collective-permute-done.27 = f32[1,128,512]{2,1,0:T(8,128)S(1)} collective-permute-done((f32[1,128,512]{2,1,0:T(8,128)S(1)}, f32[1,128,512]{2,1,0:T(8,128)S(1)}, u32[]{:S(2)}, u32[]{:S(2)}) %collective-permute-start.27) | collective-permute-done | bytes 262176 | tf_op jit(solution)/shard_map/ppermute | solution.py:184
  195.2 12.4 %all_to_all.5 = f32[8,34,128]{2,1,0:T(8,128)S(1)} all-to-all(f32[8,34,128]{2,1,0:T(8,128)S(1)} %select_maximum_fusion), channel_id=1, replica_groups=mesh['dp'=8,'fsdp'=4] {'dp'}, dimensions={0} | all-to-all | bytes 278528 | tf_op jit(solution)/shard_map/all_to_all | solution.py:320
  207.7 0.7 fusion.17
  (82 shorter events, 8.8 us)
Async XLA Ops:
  0.0 0.9 copy-start
  0.0 5.9 %copy-start.9 = (s32[64]{0:T(128)S(1)}, s32[64]{0:T(128)}, u32[]{:S(2)}) copy-start(s32[64]{0:T(128)} %param.15) | copy-start | bytes 772
  0.0 6.1 %copy-start.5 = (bf16[64,32,512]{2,1,0:T(8,128)(2,1)S(1)}, bf16[64,32,512]{2,1,0:T(8,128)(2,1)}, u32[]{:S(2)}) copy-start(bf16[64,32,512]{2,1,0:T(8,128)(2,1)} %param.13) | copy-start | bytes 6291460
  4.5 0.8 copy-start.4
  5.3 7.8 %collective-permute-start.2 = (f32[32,2048]{1,0:T(8,128)S(1)}, f32[32,2048]{1,0:T(8,128)}, u32[]{:S(2)}, u32[]{:S(2)}) collective-permute-start(f32[32,2048]{1,0:T(8,128)S(1)} %dynamic-slice_bitcast_fusion.1), channel_id=1, source_target_pairs={{0,1},{1,0},{2,3},{3,2},{4,5},{5,4},{6,7},{7,6},{8,9},{9,8},{10,11... | collective-permute-start | bytes 786440 | tf_op jit(solution)/shard_map/ppermute | solution.py:230
  10.3 29.0 %copy-start.10 = (s32[8]{0:T(128)S(1)}, s32[8]{0:T(128)}, u32[]{:S(2)}) copy-start(s32[8]{0:T(128)} %constant.174.clone) | copy-start | bytes 100
  10.3 32.3 %copy-start.2 = (s32[8]{0:T(128)S(1)}, s32[8]{0:T(128)}, u32[]{:S(2)}) copy-start(s32[8]{0:T(128)} %constant.175.clone) | copy-start | bytes 100
  10.4 21.2 %collective-permute-start.5 = (bf16[256,1536]{1,0:T(8,128)(2,1)S(1)}, bf16[256,1536]{1,0:T(8,128)(2,1)}, u32[]{:S(2)}, u32[]{:S(2)}) collective-permute-start(bf16[256,1536]{1,0:T(8,128)(2,1)S(1)} %get-tuple-element.219.refs_0_), channel_id=1, source_target_pairs={{4,12},{12,20},{20,28},{28,24},{24,16},{16,8},{8,0},{0,4},{5,13},{... | collective-permute-start | bytes 2359304 | tf_op jit(solution)/shard_map/ppermute | solution.py:267
  13.0 20.4 %collective-permute-start.6 = (bf16[256,1536]{1,0:T(8,128)(2,1)S(1)}, bf16[256,1536]{1,0:T(8,128)(2,1)S(1)}, u32[]{:S(2)}, u32[]{:S(2)}) collective-permute-start(bf16[256,1536]{1,0:T(8,128)(2,1)S(1)} %get-tuple-element.218.refs_1_), channel_id=1, source_target_pairs={{12,4},{20,12},{28,20},{24,28},{16,24},{8,16},{0,8},{4,0},{13,5},{... | collective-permute-start | bytes 2359304 | tf_op jit(solution)/shard_map/ppermute | solution.py:268
  14.3 8.5 %collective-permute-start.3 = (f32[32,2048]{1,0:T(8,128)S(1)}, f32[32,2048]{1,0:T(8,128)S(1)}, u32[]{:S(2)}, u32[]{:S(2)}) collective-permute-start(f32[32,2048]{1,0:T(8,128)S(1)} %bitcast_add_fusion.1), channel_id=1, source_target_pairs={{0,2},{1,3},{2,0},{3,1},{4,6},{5,7},{6,4},{7,5},{8,10},{9,11},{10,... | collective-permute-start | bytes 786440 | tf_op jit(solution)/shard_map/ppermute | solution.py:191
  22.8 17.7 %copy-start.7 = (bf16[32,2048]{1,0:T(8,128)(2,1)}, bf16[32,2048]{1,0:T(8,128)(2,1)S(1)}, u32[]{:S(2)}) copy-start(bf16[32,2048]{1,0:T(8,128)(2,1)S(1)} %multiply_convert_fusion) | copy-start | bytes 393220
  25.4 1.4 collective-permute-start.4
  26.8 9.1 %collective-permute-start.7 = (bf16[64,1664]{1,0:T(8,128)(2,1)S(1)}, bf16[64,1664]{1,0:T(8,128)(2,1)S(1)}, u32[]{:S(2)}, u32[]{:S(2)}) collective-permute-start(bf16[64,1664]{1,0:T(8,128)(2,1)S(1)} %maximum_select_fusion.2.refs_2_.refs_3_), channel_id=1, source_target_pairs={{4,12},{12,20},{20,28},{28,24},{24,16},{16,8},{8,0},{0,4},{5,13},{... | collective-permute-start | bytes 638984 | tf_op jit(solution)/shard_map/ppermute | solution.py:270
  28.5 8.8 %collective-permute-start.8 = (bf16[64,1664]{1,0:T(8,128)(2,1)S(1)}, bf16[64,1664]{1,0:T(8,128)(2,1)S(1)}, u32[]{:S(2)}, u32[]{:S(2)}) collective-permute-start(bf16[64,1664]{1,0:T(8,128)(2,1)S(1)} %maximum_select_fusion.2.refs_2_.refs_3_), channel_id=1, source_target_pairs={{12,4},{20,12},{28,20},{24,28},{16,24},{8,16},{0,8},{4,0},{13,5},{... | collective-permute-start | bytes 638984 | tf_op jit(solution)/shard_map/ppermute | solution.py:272
  37.3 24.1 %collective-permute-start.10 = (bf16[256,1536]{1,0:T(8,128)(2,1)S(1)}, bf16[256,1536]{1,0:T(8,128)(2,1)}, u32[]{:S(2)}, u32[]{:S(2)}) collective-permute-start(bf16[256,1536]{1,0:T(8,128)(2,1)S(1)} %collective-permute-done.6.refs_0_), channel_id=1, source_target_pairs={{12,4},{20,12},{28,20},{24,28},{16,24},{8,16},{0,8},{4,0},{13,5},{... | collective-permute-start | bytes 2359304 | tf_op jit(solution)/shard_map/ppermute | solution.py:268
  37.7 23.7 %collective-permute-start.9 = (bf16[256,1536]{1,0:T(8,128)(2,1)}, bf16[256,1536]{1,0:T(8,128)(2,1)}, u32[]{:S(2)}, u32[]{:S(2)}) collective-permute-start(bf16[256,1536]{1,0:T(8,128)(2,1)} %collective-permute-done.5.refs_1_), channel_id=1, source_target_pairs={{4,12},{12,20},{20,28},{28,24},{24,16},{16,8},{8,0},{0,4},{5,13},{... | collective-permute-start | bytes 2359304 | tf_op jit(solution)/shard_map/ppermute | solution.py:267
  40.6 20.8 %collective-permute-start.11 = (bf16[64,1664]{1,0:T(8,128)(2,1)S(1)}, bf16[64,1664]{1,0:T(8,128)(2,1)S(1)}, u32[]{:S(2)}, u32[]{:S(2)}) collective-permute-start(bf16[64,1664]{1,0:T(8,128)(2,1)S(1)} %collective-permute-done.7.refs_3_.refs_2_), channel_id=1, source_target_pairs={{4,12},{12,20},{20,28},{28,24},{24,16},{16,8},{8,0},{0,4},{5,13},{... | collective-permute-start | bytes 638984 | tf_op jit(solution)/shard_map/ppermute | solution.py:270
  42.2 19.1 %collective-permute-start.12 = (bf16[64,1664]{1,0:T(8,128)(2,1)S(1)}, bf16[64,1664]{1,0:T(8,128)(2,1)S(1)}, u32[]{:S(2)}, u32[]{:S(2)}) collective-permute-start(bf16[64,1664]{1,0:T(8,128)(2,1)S(1)} %collective-permute-done.8.refs_2_.refs_3_), channel_id=1, source_target_pairs={{12,4},{20,12},{28,20},{24,28},{16,24},{8,16},{0,8},{4,0},{13,5},{... | collective-permute-start | bytes 638984 | tf_op jit(solution)/shard_map/ppermute | solution.py:272
  61.3 23.5 %collective-permute-start.13 = (bf16[256,1536]{1,0:T(8,128)(2,1)}, bf16[256,1536]{1,0:T(8,128)(2,1)S(1)}, u32[]{:S(2)}, u32[]{:S(2)}) collective-permute-start(bf16[256,1536]{1,0:T(8,128)(2,1)} %collective-permute-done.9.refs_0_), channel_id=1, source_target_pairs={{4,12},{12,20},{20,28},{28,24},{24,16},{16,8},{8,0},{0,4},{5,13},{... | collective-permute-start | bytes 2359304 | tf_op jit(solution)/shard_map/ppermute | solution.py:267
  62.7 22.1 %collective-permute-start.14 = (bf16[256,1536]{1,0:T(8,128)(2,1)}, bf16[256,1536]{1,0:T(8,128)(2,1)S(1)}, u32[]{:S(2)}, u32[]{:S(2)}) collective-permute-start(bf16[256,1536]{1,0:T(8,128)(2,1)} %collective-permute-done.10.refs_1_), channel_id=1, source_target_pairs={{12,4},{20,12},{28,20},{24,28},{16,24},{8,16},{0,8},{4,0},{13,5},{... | collective-permute-start | bytes 2359304 | tf_op jit(solution)/shard_map/ppermute | solution.py:268
  63.4 20.7 %collective-permute-start.15 = (bf16[64,1664]{1,0:T(8,128)(2,1)S(1)}, bf16[64,1664]{1,0:T(8,128)(2,1)S(1)}, u32[]{:S(2)}, u32[]{:S(2)}) collective-permute-start(bf16[64,1664]{1,0:T(8,128)(2,1)S(1)} %collective-permute-done.11.refs_2_.refs_3_), channel_id=1, source_target_pairs={{4,12},{12,20},{20,28},{28,24},{24,16},{16,8},{8,0},{0,4},{5,13},{... | collective-permute-start | bytes 638984 | tf_op jit(solution)/shard_map/ppermute | solution.py:270
  64.7 20.1 %collective-permute-start.16 = (bf16[64,1664]{1,0:T(8,128)(2,1)S(1)}, bf16[64,1664]{1,0:T(8,128)(2,1)S(1)}, u32[]{:S(2)}, u32[]{:S(2)}) collective-permute-start(bf16[64,1664]{1,0:T(8,128)(2,1)S(1)} %collective-permute-done.12.refs_3_.refs_2_), channel_id=1, source_target_pairs={{12,4},{20,12},{28,20},{24,28},{16,24},{8,16},{0,8},{4,0},{13,5},{... | collective-permute-start | bytes 638984 | tf_op jit(solution)/shard_map/ppermute | solution.py:272
  84.8 22.3 %collective-permute-start.17 = (bf16[256,1536]{1,0:T(8,128)(2,1)S(1)}, bf16[256,1536]{1,0:T(8,128)(2,1)S(1)}, u32[]{:S(2)}, u32[]{:S(2)}) collective-permute-start(bf16[256,1536]{1,0:T(8,128)(2,1)S(1)} %collective-permute-done.13.refs_1_), channel_id=1, source_target_pairs={{4,12},{12,20},{20,28},{28,24},{24,16},{16,8},{8,0},{0,4},{5,13},{... | collective-permute-start | bytes 2359304 | tf_op jit(solution)/shard_map/ppermute | solution.py:267
  86.4 20.7 %collective-permute-start.18 = (bf16[256,1536]{1,0:T(8,128)(2,1)S(1)}, bf16[256,1536]{1,0:T(8,128)(2,1)S(1)}, u32[]{:S(2)}, u32[]{:S(2)}) collective-permute-start(bf16[256,1536]{1,0:T(8,128)(2,1)S(1)} %collective-permute-done.14.refs_0_), channel_id=1, source_target_pairs={{12,4},{20,12},{28,20},{24,28},{16,24},{8,16},{0,8},{4,0},{13,5},{... | collective-permute-start | bytes 2359304 | tf_op jit(solution)/shard_map/ppermute | solution.py:268
  86.9 20.2 %collective-permute-start.19 = (bf16[64,1664]{1,0:T(8,128)(2,1)S(1)}, bf16[64,1664]{1,0:T(8,128)(2,1)S(1)}, u32[]{:S(2)}, u32[]{:S(2)}) collective-permute-start(bf16[64,1664]{1,0:T(8,128)(2,1)S(1)} %collective-permute-done.15.refs_3_.refs_2_), channel_id=1, source_target_pairs={{4,12},{12,20},{20,28},{28,24},{24,16},{16,8},{8,0},{0,4},{5,13},{... | collective-permute-start | bytes 638984 | tf_op jit(solution)/shard_map/ppermute | solution.py:270
  107.1 17.7 %collective-permute-start.20 = (bf16[256,1536]{1,0:T(8,128)(2,1)S(1)}, bf16[256,1536]{1,0:T(8,128)(2,1)S(1)}, u32[]{:S(2)}, u32[]{:S(2)}) collective-permute-start(bf16[256,1536]{1,0:T(8,128)(2,1)S(1)} %collective-permute-done.17.refs_0_), channel_id=1, source_target_pairs={{4,12},{12,20},{20,28},{28,24},{24,16},{16,8},{8,0},{0,4},{5,13},{... | collective-permute-start | bytes 2359304 | tf_op jit(solution)/shard_map/ppermute | solution.py:267
  108.7 16.1 %collective-permute-start.21 = (bf16[256,1536]{1,0:T(8,128)(2,1)S(1)}, bf16[256,1536]{1,0:T(8,128)(2,1)S(1)}, u32[]{:S(2)}, u32[]{:S(2)}) collective-permute-start(bf16[256,1536]{1,0:T(8,128)(2,1)S(1)} %collective-permute-done.18.refs_1_), channel_id=1, source_target_pairs={{12,4},{20,12},{28,20},{24,28},{16,24},{8,16},{0,8},{4,0},{13,5},{... | collective-permute-start | bytes 2359304 | tf_op jit(solution)/shard_map/ppermute | solution.py:268
  124.8 17.7 %collective-permute-start.22 = (bf16[256,1536]{1,0:T(8,128)(2,1)S(1)}, bf16[256,1536]{1,0:T(8,128)(2,1)S(1)}, u32[]{:S(2)}, u32[]{:S(2)}) collective-permute-start(bf16[256,1536]{1,0:T(8,128)(2,1)S(1)} %collective-permute-done.20.refs_1_), channel_id=1, source_target_pairs={{4,12},{12,20},{20,28},{28,24},{24,16},{16,8},{8,0},{0,4},{5,13},{... | collective-permute-start | bytes 2359304 | tf_op jit(solution)/shard_map/ppermute | solution.py:267
  126.4 16.1 %collective-permute-start.23 = (bf16[256,1536]{1,0:T(8,128)(2,1)S(1)}, bf16[256,1536]{1,0:T(8,128)(2,1)S(1)}, u32[]{:S(2)}, u32[]{:S(2)}) collective-permute-start(bf16[256,1536]{1,0:T(8,128)(2,1)S(1)} %collective-permute-done.21.refs_0_), channel_id=1, source_target_pairs={{12,4},{20,12},{28,20},{24,28},{16,24},{8,16},{0,8},{4,0},{13,5},{... | collective-permute-start | bytes 2359304 | tf_op jit(solution)/shard_map/ppermute | solution.py:268
  142.5 13.9 %collective-permute-start.24 = (bf16[256,1536]{1,0:T(8,128)(2,1)S(1)}, bf16[256,1536]{1,0:T(8,128)(2,1)S(1)}, u32[]{:S(2)}, u32[]{:S(2)}) collective-permute-start(bf16[256,1536]{1,0:T(8,128)(2,1)S(1)} %collective-permute-done.22.refs_0_), channel_id=1, source_target_pairs={{4,12},{12,20},{20,28},{28,24},{24,16},{16,8},{8,0},{0,4},{5,13},{... | collective-permute-start | bytes 2359304 | tf_op jit(solution)/shard_map/ppermute | solution.py:267
  144.1 12.3 %collective-permute-start.25 = (bf16[256,1536]{1,0:T(8,128)(2,1)S(1)}, bf16[256,1536]{1,0:T(8,128)(2,1)S(1)}, u32[]{:S(2)}, u32[]{:S(2)}) collective-permute-start(bf16[256,1536]{1,0:T(8,128)(2,1)S(1)} %collective-permute-done.23.refs_1_), channel_id=1, source_target_pairs={{12,4},{20,12},{28,20},{24,28},{16,24},{8,16},{0,8},{4,0},{13,5},{... | collective-permute-start | bytes 2359304 | tf_op jit(solution)/shard_map/ppermute | solution.py:268
  167.8 13.8 %copy-start.8 = (bf16[32,2048]{1,0:T(8,128)(2,1)S(1)}, bf16[32,2048]{1,0:T(8,128)(2,1)}, u32[]{:S(2)}) copy-start(bf16[32,2048]{1,0:T(8,128)(2,1)} %copy-done.7) | copy-start | bytes 393220
  179.2 1.0 copy-start.3
  181.6 6.1 %copy-start.6 = (bf16[256,512]{1,0:T(8,128)(2,1)S(1)}, bf16[256,512]{1,0:T(8,128)(2,1)}, u32[]{:S(2)}) copy-start(bf16[256,512]{1,0:T(8,128)(2,1)} %param.17) | copy-start | bytes 786436
  181.9 26.5 %copy-start.1 = (bf16[64,1024]{1,0:T(8,128)(2,1)S(1)}, bf16[64,1024]{1,0:T(8,128)(2,1)}, u32[]{:S(2)}) copy-start(bf16[64,1024]{1,0:T(8,128)(2,1)} %param.14) | copy-start | bytes 393220
  183.0 2.0 collective-permute-start.26
  186.1 8.4 %collective-permute-start.27 = (f32[1,128,512]{2,1,0:T(8,128)S(1)}, f32[1,128,512]{2,1,0:T(8,128)S(1)}, u32[]{:S(2)}, u32[]{:S(2)}) collective-permute-start(f32[1,128,512]{2,1,0:T(8,128)S(1)} %constant_dynamic-slice_fusion), channel_id=1, source_target_pairs={{0,2},{1,3},{2,0},{3,1},{4,6},{5,7},{6,4},{7,5},{8,10},{9,11},{10,... | collective-permute-start | bytes 786440 | tf_op jit(solution)/shard_map/ppermute | solution.py:184

commit v3 on v2

--- a/solution.py
+++ b/solution.py
@@ -27,9 +27,9 @@
 
 
 def form_project_kernel(dims, blocks_ref, *refs):
-    shards, row, pool, rank, pairs, block, first_row = dims
-    g_refs, a_refs = refs[:shards], refs[shards : 2 * shards]
-    p_hbm, acc_hbm, out_hbm, pbuf, s_ref, held, words, meta, p_sems, acc_sems = refs[2 * shards :]
+    shards, row, pool, rank, pairs, block, first_row, last = dims
+    g_refs, own_refs, other_refs = (refs[i * shards : (i + 1) * shards] for i in range(3))
+    p_hbm, acc_hbm, out_hbm, pbuf, s_ref, held, words, meta, p_sems, acc_sems = refs[3 * shards :]
     blocks = pairs // block
     rows = block * rank
     stride = shards * pool + 8
@@ -59,7 +59,7 @@
             p_copy(i, h).start()
     for k in range(shards):
         acc_load(k).start()
-        words[k] = a_refs[k][: 2 * 8, room:].astype(F32).astype(jnp.int32)
+        words[k] = own_refs[k][: 2 * 8, room:].astype(F32).astype(jnp.int32)
     to_scalars = [
         pltpu.make_async_copy(words.at[k, pl.ds(0, 8)], meta.at[k], acc_sems.at[2, k])
         for k in range(shards)
@@ -69,6 +69,7 @@
     tiles = room // LANES
     low = lax.broadcasted_iota(jnp.int32, (pairs, LANES), 1) < rank
     lane = lax.broadcasted_iota(jnp.int32, (rank, 2 * LANES), 1)
+    first_core = jnp.full((rank // 2, 2 * LANES), blocks_ref[blocks_ref.shape[0] - 1]) == 0
 
     for k in range(shards):
         to_scalars[k].wait()
@@ -78,7 +79,11 @@
             tile = jnp.minimum(meta[k, 1, e], tiles - 2)
             base = pl.multiple_of(tile * LANES, LANES)
             g = g_refs[k][:, pl.ds(base, 2 * LANES)]
-            a = a_refs[k][:, pl.ds(base, 2 * LANES)]
+            own = own_refs[k][:, pl.ds(base, 2 * LANES)]
+            other = other_refs[k][:, pl.ds(base, 2 * LANES)]
+            a = jnp.concatenate(
+                [jnp.where(first_core, own, other), jnp.where(first_core, other, own)], axis=0
+            )
             masked = []
             for j in range(2):
                 begin = meta[k, 1, e + j] * LANES + meta[k, 2, e + j] - base
@@ -98,7 +103,7 @@
                 )
             return carry
 
-        lax.fori_loop(0, pool // 2, two_examples, 0, unroll=4)
+        lax.fori_loop(0, pool // 2, two_examples, 0, unroll=8 if last else 4)
     for k in range(shards):
         acc_load(k).wait()
 
@@ -107,7 +112,9 @@
         p_copy(i, 1).wait()
         left = jnp.concatenate(
             [
-                s_ref[pl.ds(pl.multiple_of((i * block + o) * stride, 8), shards * pool), :].astype(BF16)
+                s_ref[
+                    pl.ds(pl.multiple_of((i * block + o) * stride, 8), shards * pool), :
+                ].astype(BF16)
                 for o in range(block)
             ],
             axis=1,
@@ -123,27 +130,27 @@
         held[...] += jnp.dot(left, right, preferred_element_type=F32)
         return carry
 
-    lax.fori_loop(0, blocks, project, 0)
+    lax.fori_loop(0, blocks, project, 0, unroll=blocks if last else 1)
     for k in range(shards):
         acc_store(k).start()
     for k in range(shards):
         acc_store(k).wait()
 
 
-def form_project(acc, blocks, row, gs, acts, projection, half, pool):
+def form_project(acc, blocks, row, gs, acts, projection, half, pool, last):
     shards = len(gs)
     outs = gs[0].shape[0]
-    rank = acts[0].shape[0]
+    rank = 2 * acts[0][0].shape[0]
     feats = projection.shape[1]
     pairs = outs // 2
-    block = min(16, pairs)
-    dims = (shards, row, pool, rank, pairs, block, half * outs * rank)
+    block = min(32, pairs)
+    dims = (shards, row, pool, rank, pairs, block, half * outs * rank, last)
     whole = lambda x: pl.BlockSpec(x.shape, lambda i, m: (0, 0))
-    flat = list(gs)
+    flat = list(gs) + [a[0] for a in acts] + [a[1] for a in acts]
     spec = pltpu.PrefetchScalarGridSpec(
         num_scalar_prefetch=1,
         grid=(1,),
-        in_specs=[whole(x) for x in flat + list(acts)]
+        in_specs=[whole(x) for x in flat]
         + [pl.BlockSpec(memory_space=pl.ANY)] * 2,
         out_specs=pl.BlockSpec(memory_space=pl.ANY),
         scratch_shapes=[
@@ -160,7 +167,7 @@
         functools.partial(form_project_kernel, dims),
         out_shape=jax.ShapeDtypeStruct(acc.shape, F32),
         grid_spec=spec,
-        input_output_aliases={len(flat) + shards + 2: 0},
+        input_output_aliases={len(flat) + 2: 0},
         compiler_params=pltpu.CompilerParams(vmem_limit_bytes=VMEM_LIMIT),
         cost_estimate=pl.CostEstimate(
             flops=2 * shards * pool * outs * rank * feats,
@@ -168,7 +175,7 @@
             transcendentals=0,
         ),
         name="form_project",
-    )(blocks, *flat, *acts, projection, acc)
+    )(blocks, *flat, projection, acc)
 
 
 def exchange_sum(x, axis, n):
@@ -181,7 +188,9 @@
         grouped = slots.reshape((slots.shape[0] // 2, 2) + x.shape[1:])
         keep = lax.dynamic_index_in_dim(grouped, mine, 1, keepdims=False)
         send = lax.dynamic_index_in_dim(grouped, 1 - mine, 1, keepdims=False)
-        slots = keep + lax.ppermute(send, axis, swap)
+        if bit > 1:
+            send = send.astype(BF16)
+        slots = keep + lax.ppermute(send, axis, swap).astype(F32)
         bit *= 2
     return slots.reshape(x.shape[1:])
 
@@ -242,43 +251,53 @@
     words = jnp.stack([counts, starts // LANES, starts % LANES]).astype(BF16)
     words = jnp.pad(words, ((0, rank // 2 - 3), (0, -pool % LANES)))
     own_half = jnp.dot(acts_half, select, preferred_element_type=F32).astype(BF16)
-    own_acts = both_halves(jnp.concatenate([own_half, words], axis=1))
+    own_half = jnp.concatenate([own_half, words], axis=1)
     my_position = jnp.asarray(np.argsort(order), jnp.int32)[me]
     blocks = jnp.asarray(order, jnp.int32)[(my_position - jnp.arange(dp + 1)) % dp]
-
-    acts = {0: own_acts, dp: own_acts}
+    blocks = jnp.concatenate([blocks, core[None].astype(jnp.int32)])
+
+    halves = {0: own_half, dp: own_half}
+    acts = {}
     low, high = {0: packed[:half]}, {dp: packed[half:]}
     acc = jnp.zeros((dp * pool, feats), F32)
-
-    def add(acc, first, gs, which):
+    overflow = None
+
+    blocks, acc = lax.optimization_barrier((blocks, acc))
+
+    def add(acc, blocks, first, gs, which):
         return form_project(
             acc, blocks, first, [gs[first], gs[first + 1]], [acts[first], acts[first + 1]],
-            projection, which, pool,
+            projection, which, pool, first in (1, dp - 2),
         )
 
     for s in range(dp):
-        if s > 0:
-            keys = [k for k in dict.fromkeys((s, dp - s)) if k in acts]
-            low[s], high[dp - s], acc, *fresh = lax.optimization_barrier(
-                (low[s], high[dp - s], acc, *[acts[k] for k in keys])
+        keys = [k for k in dict.fromkeys((s, dp - s)) if k in halves]
+        if s == dp // 2 + 1:
+            used = jnp.stack([halves[i][0, room : room + pool] for i in range(dp)])
+            overflow = jnp.max(jnp.sum(used.astype(jnp.int32), axis=1)) > room
+            low[s], high[dp - s], acc, overflow = lax.optimization_barrier(
+                (low[s], high[dp - s], acc, overflow)
             )
-            acts.update(zip(keys, fresh))
+        elif s > 0:
+            low[s], high[dp - s], acc, blocks, *fresh = lax.optimization_barrier(
+                (low[s], high[dp - s], acc, blocks, *[halves[k] for k in keys])
+            )
+            halves.update(zip(keys, fresh))
         if s + 1 < dp:
             low[s + 1] = lax.ppermute(low[s], "dp", ahead)
             high[dp - s - 1] = lax.ppermute(high[dp - s], "dp", back)
         if 2 * (s + 1) <= dp:
-            acts[s + 1] = lax.ppermute(acts[s], "dp", ahead)
+            halves[s + 1] = lax.ppermute(halves[s], "dp", ahead)
         if 2 * (s + 1) < dp:
-            acts[dp - s - 1] = lax.ppermute(acts[dp - s], "dp", back)
+            halves[dp - s - 1] = lax.ppermute(halves[dp - s], "dp", back)
+        for k in keys:
+            acts[k] = acts[0] if k == dp else (halves[k], lax.ppermute(halves[k], "fsdp", swap))
         if s % 2 == 1:
-            acc = add(acc, s - 1, low, 0)
+            acc = add(acc, blocks, s - 1, low, 0)
         if s > 0 and s % 2 == 0:
-            acc = add(acc, dp - s + 1, high, 1)
+            acc = add(acc, blocks, dp - s + 1, high, 1)
         if s == dp - 1:
-            acc = add(acc, 1, high, 1)
-
-    used = jnp.stack([acts[i][0, room : room + pool] for i in range(dp)]).astype(jnp.int32)
-    overflow = jnp.max(jnp.sum(used, axis=1)) > room
+            acc = add(acc, blocks, 1, high, 1)
 
     def padded(acc):
         mine = both_halves(acts_half).reshape(rank, pool, length)

time: 209 us -> 200 us (0.957)
  Pallas kernels: 94.3 us -> 86.6 us
  waiting for transfers between devices: 52.2 us -> 47.9 us
  blocking collectives: 12.4 us -> 9.98 us
    pallas_call x8, Pallas kernels: 94.3 us -> 86.6 us  [form_project(): pl.pallas_call(functools.partial(form_project_kernel, dims), out_shape=ja...]
    all_to_all x1, blocking collectives: 12.4 us -> 9.98 us  [per_device(): got = jnp.sum(lax.all_to_all(sent, 'dp', 0, 0), axis=0)]
    ppermute x10 -> x21, starting transfers between devices: 9.5 us -> 11.5 us  [the longest x4 6.39 us: per_device(): halves[s + 1] = lax.ppermute(halves[s], 'dp', ahead)]
    ppermute x10 -> x21, waiting for transfers between devices: 33.2 us -> 31.6 us  [the longest x4 19.9 us: per_device(): halves[s + 1] = lax.ppermute(halves[s], 'dp', ahead)]
  transfers between devices with their start and end apart: 26 -> 37, of which waited for: 15 -> 15; matrix products, arithmetic and copies ran while one was open for 5% -> 7% of each run, Pallas kernels for 34% -> 39%
where the time goes in v3:
time: 200 us; the launch traced here: 199 us
  Pallas kernels  86.6 us (43%)
  waiting for transfers between devices  47.9 us (24%)
  starting transfers between devices  28.9 us (14%)
  matrix products  12.3 us (6%)
  blocking collectives  9.98 us (5%)
  local copies, waits for them, and re-layouts  7.28 us (4%)
  other arithmetic  4.91 us (2%)
    pallas_call x8, Pallas kernels, form_project(): pl.pallas_call(functools.partial(form_project_kernel, dims), out_shape=ja...  86.6 us
    ppermute x4, waiting for transfers between devices, per_device(): halves[s + 1] = lax.ppermute(halves[s], 'dp', ahead)  19.9 us
    ppermute x7, starting transfers between devices, per_device(): low[s + 1] = lax.ppermute(low[s], 'dp', ahead)  11.5 us
    all_to_all x1, blocking collectives, per_device(): got = jnp.sum(lax.all_to_all(sent, 'dp', 0, 0), axis=0)  9.98 us
    ppermute x7, waiting for transfers between devices, per_device(): low[s + 1] = lax.ppermute(low[s], 'dp', ahead)  9.14 us
    ppermute x4, starting transfers between devices, per_device(): halves[s + 1] = lax.ppermute(halves[s], 'dp', ahead)  6.39 us
    ppermute x1, waiting for transfers between devices, exchange_total(): x = x + lax.ppermute(x, axis, [(i, i ^ bit) for i in range(n)])  5.87 us
    dot_general x1, matrix products, per_device(): lax.dot_general(grad_rows.reshape(pool * length, outs), select, (((0,), (...  5.76 us
  transfers between devices with their start and end apart: 37, of which 15 were waited for; matrix products, arithmetic and copies ran while one was open for 7% of the time, Pallas kernels for 39%

profile of v3, /device:TPU:0, one launch (start us, length us, event | category | flops | bytes accessed | tf_op | source)
XLA Modules:
  0.0 199.2 jit_solution(1757762368022708481)
XLA Ops:
  0.0 0.9 copy-done
  0.9 3.6 %fusion.37 = f32[2,32,2048]{2,1,0:T(8,128)S(1)} fusion(bf16[2,32,1024]{2,1,0:T(8,128)(2,1)S(1)} %bitcast.79, bf16[2048,1024,1]{1,0,2:T(8,128)(2,1)} %bitcast.82), kind=kOutput, calls=%fused_computation.79 | convolution fusion | flops 268435456 | bytes 4849664 | tf_op jit(solution)/shard_map/dot_general | solution.py:231
  5.3 5.8 %fusion.12 = bf16[512,1536]{1,0:T(8,128)(2,1)S(1)} fusion(bf16[2048,512]{1,0:T(8,128)(2,1)} %bitcast.83, s32[2048]{0:T(1024)S(1)} %select_n.130), kind=kOutput, calls=%fused_computation.17 | convolution fusion | flops 3225157632 | bytes 3678208 | tf_op jit(solution)/shard_map/dot_general | solution.py:217
  11.2 2.6 %collective-permute-start.2 = (bf16[256,1536]{1,0:T(8,128)(2,1)S(1)}, bf16[256,1536]{1,0:T(8,128)(2,1)}, u32[]{:S(2)}, u32[]{:S(2)}) collective-permute-start(bf16[256,1536]{1,0:T(8,128)(2,1)S(1)} %get-tuple-element.233.refs_0_), channel_id=1, source_target_pairs={{4,12},{12,20},{20,28},{28,24},{24,16},{16,8},{8,0},{0,4},{5,13},{... | collective-permute-start | bytes 2359304 | tf_op jit(solution)/shard_map/ppermute | solution.py:287
  15.2 1.0 bitcast_add_fusion.1
  16.2 1.9 collective-permute-start.5
  18.9 5.9 %collective-permute-done.5 = f32[32,2048]{1,0:T(8,128)S(1)} collective-permute-done((f32[32,2048]{1,0:T(8,128)S(1)}, f32[32,2048]{1,0:T(8,128)S(1)}, u32[]{:S(2)}, u32[]{:S(2)}) %collective-permute-start.5) | collective-permute-done | bytes 262176 | tf_op jit(solution)/shard_map/ppermute | solution.py:200
  24.8 2.5 %fusion.13 = bf16[32,1536]{1,0:T(8,128)(2,1)S(1)} fusion(bf16[32,2048]{1,0:T(8,128)(2,1)S(1)} %multiply_convert_fusion, s32[2048]{0:T(1024)S(1)} %select_n.130), kind=kOutput, calls=%fused_computation.18 | convolution fusion | flops 204521472 | bytes 237568 | tf_op jit(solution)/shard_map/dot_general | solution.py:253
  27.3 1.7 collective-permute-start.6
  29.5 4.8 %collective-permute-done.6.refs_3_.refs_2_ = bf16[32,1664]{1,0:T(8,128)(2,1)S(1)} collective-permute-done((bf16[32,1664]{1,0:T(8,128)(2,1)S(1)}, bf16[32,1664]{1,0:T(8,128)(2,1)S(1)}, u32[]{:S(2)}, u32[]{:S(2)}) %collective-permute-start.6) | collective-permute-done | bytes 106528 | tf_op jit(solution)/shard_map/ppermute | solution.py:290
  34.3 1.4 collective-permute-done.7.refs_2_.refs_3_
  35.7 1.6 collective-permute-start.8
  38.3 1.6 collective-permute-start.12
  40.4 11.7 %form_project.8.refs_7_ = f32[512,512]{1,0:T(8,128)S(1)} custom-call(s32[10]{0:T(128)S(1)} %pad_add_fusion.blocks_ref, bf16[256,1536]{1,0:T(8,128)(2,1)S(1)} %get-tuple-element.233.refs_0_, bf16[256,1536]{1,0:T(8,128)(2,1)} %collective-permute-done.2.refs_1_, bf16[32,1664]{1,0:T(8,128)(2,1)S(1)} %pad_maximum_fusion.refs_2_.refs_3_, ...), custom_call_target="tpu_custom_call", output_to_operand_aliasing={{}: (8, {})} | custom-call | flops 2147483648 | bytes 16777216 | tf_op jit(solution)/shard_map/form_project/pallas_call | solution.py:166
  52.2 4.9 %collective-permute-done.12.refs_2_.refs_3_ = bf16[32,1664]{1,0:T(8,128)(2,1)S(1)} collective-permute-done((bf16[32,1664]{1,0:T(8,128)(2,1)S(1)}, bf16[32,1664]{1,0:T(8,128)(2,1)S(1)}, u32[]{:S(2)}, u32[]{:S(2)}) %collective-permute-start.12) | collective-permute-done | bytes 106528 | tf_op jit(solution)/shard_map/ppermute | solution.py:290
  57.1 1.2 collective-permute-done.13.refs_3_.refs_2_
  58.3 1.6 collective-permute-start.14
  60.3 1.6 collective-permute-start.17
  62.3 10.6 %form_project.9.refs_7_ = f32[512,512]{1,0:T(8,128)S(1)} custom-call(s32[10]{0:T(128)S(1)} %pad_add_fusion.blocks_ref, bf16[256,1536]{1,0:T(8,128)(2,1)S(1)} %collective-permute-done.3.refs_0_, bf16[256,1536]{1,0:T(8,128)(2,1)S(1)} %get-tuple-element.232.refs_1_, ...), custom_call_target="tpu_custom_call", output_to_operand_aliasing={{}: (8, {})} | custom-call | flops 2147483648 | bytes 16777216 | tf_op jit(solution)/shard_map/form_project/pallas_call | solution.py:166
  72.9 5.1 %collective-permute-done.17.refs_3_.refs_2_ = bf16[32,1664]{1,0:T(8,128)(2,1)S(1)} collective-permute-done((bf16[32,1664]{1,0:T(8,128)(2,1)S(1)}, bf16[32,1664]{1,0:T(8,128)(2,1)S(1)}, u32[]{:S(2)}, u32[]{:S(2)}) %collective-permute-start.17) | collective-permute-done | bytes 106528 | tf_op jit(solution)/shard_map/ppermute | solution.py:290
  78.1 1.4 collective-permute-done.18.refs_2_.refs_3_
  79.5 1.6 collective-permute-start.19
  82.0 1.6 collective-permute-start.23
  83.6 10.6 %form_project.10.refs_7_ = f32[512,512]{1,0:T(8,128)S(1)} custom-call(s32[10]{0:T(128)S(1)} %pad_add_fusion.blocks_ref, bf16[256,1536]{1,0:T(8,128)(2,1)S(1)} %collective-permute-done.8.refs_0_, bf16[256,1536]{1,0:T(8,128)(2,1)S(1)} %collective-permute-done.14.refs_1_, ...), custom_call_target="tpu_custom_call", output_to_operand_aliasing={{}: (8, {})} | custom-call | flops 2147483648 | bytes 16777216 | tf_op jit(solution)/shard_map/form_project/pallas_call | solution.py:166
  94.2 5.0 %collective-permute-done.23.refs_2_.refs_3_ = bf16[32,1664]{1,0:T(8,128)(2,1)S(1)} collective-permute-done((bf16[32,1664]{1,0:T(8,128)(2,1)S(1)}, bf16[32,1664]{1,0:T(8,128)(2,1)S(1)}, u32[]{:S(2)}, u32[]{:S(2)}) %collective-permute-start.23) | collective-permute-done | bytes 106528 | tf_op jit(solution)/shard_map/ppermute | solution.py:290
  99.3 1.6 collective-permute-start.24
  103.3 0.7 reduce_max.9
  104.8 11.7 %form_project.11.refs_7_ = f32[512,512]{1,0:T(8,128)} custom-call(s32[10]{0:T(128)S(1)} %pad_add_fusion.blocks_ref, bf16[256,1536]{1,0:T(8,128)(2,1)S(1)} %collective-permute-done.15.refs_0_, bf16[256,1536]{1,0:T(8,128)(2,1)S(1)} %collective-permute-done.9.refs_1_, ...), custom_call_target="tpu_custom_call", output_to_operand_aliasing={{}: (8, {})} | custom-call | flops 2147483648 | bytes 16777216 | tf_op jit(solution)/shard_map/form_project/pallas_call | solution.py:166
  116.5 1.6 collective-permute-start.28
  118.6 1.3 collective-permute-done.30.refs_4_.refs_5_
  119.9 11.8 %form_project.12.refs_7_ = f32[512,512]{1,0:T(8,128)} custom-call(s32[10]{0:T(128)S(1)} %pad_add_fusion.blocks_ref, bf16[256,1536]{1,0:T(8,128)(2,1)S(1)} %collective-permute-done.19.refs_0_, bf16[256,1536]{1,0:T(8,128)(2,1)} %collective-permute-done.24.refs_1_, bf16[32,1664]{1,0:T(8,128)(2,1)S(1)} %copy-done.9, ...), custom_call_target="tpu_custom_call", output_to_operand_aliasing={{}: (8, {})} | custom-call | flops 2147483648 | bytes 16777216 | tf_op jit(solution)/shard_map/form_project/pallas_call | solution.py:166
  131.7 4.6 %collective-permute-done.28.refs_0_ = bf16[256,1536]{1,0:T(8,128)(2,1)S(1)} collective-permute-done((bf16[256,1536]{1,0:T(8,128)(2,1)}, bf16[256,1536]{1,0:T(8,128)(2,1)S(1)}, u32[]{:S(2)}, u32[]{:S(2)}) %collective-permute-start.28) | collective-permute-done | bytes 786464 | tf_op jit(solution)/shard_map/ppermute | solution.py:287
  136.3 1.2 collective-permute-done.29.refs_1_
  137.5 1.0 collective-permute-start.31
  138.6 1.0 collective-permute-start.32
  139.6 11.8 %form_project.13.refs_7_ = f32[512,512]{1,0:T(8,128)} custom-call(s32[10]{0:T(128)S(1)} %pad_add_fusion.blocks_ref, bf16[256,1536]{1,0:T(8,128)(2,1)} %collective-permute-done.25.refs_0_, bf16[256,1536]{1,0:T(8,128)(2,1)S(1)} %collective-permute-done.20.refs_1_, bf16[32,1664]{1,0:T(8,128)(2,1)S(1)} %copy-done.5, ...), custom_call_target="tpu_custom_call", output_to_operand_aliasing={{}: (8, {})} | custom-call | flops 2147483648 | bytes 16777216 | tf_op jit(solution)/shard_map/form_project/pallas_call | solution.py:166
  151.3 4.5 %collective-permute-done.31.refs_1_ = bf16[256,1536]{1,0:T(8,128)(2,1)S(1)} collective-permute-done((bf16[256,1536]{1,0:T(8,128)(2,1)S(1)}, bf16[256,1536]{1,0:T(8,128)(2,1)S(1)}, u32[]{:S(2)}, u32[]{:S(2)}) %collective-permute-start.31) | collective-permute-done | bytes 786464 | tf_op jit(solution)/shard_map/ppermute | solution.py:287
  155.9 0.9 copy-done.2
  157.3 0.8 collective-permute-done.36.refs_5_
  158.1 1.1 copy-done.3
  159.2 9.7 %form_project.14.refs_7_ = f32[512,512]{1,0:T(8,128)} custom-call(s32[10]{0:T(128)S(1)} %pad_add_fusion.blocks_ref, bf16[256,1536]{1,0:T(8,128)(2,1)S(1)} %collective-permute-done.28.refs_0_, bf16[256,1536]{1,0:T(8,128)(2,1)S(1)} %copy-done.3, bf16[32,1664]{1,0:T(8,128)(2,1)} %collective-permute-done.13.refs_3_.refs_2_, ...), custom_call_target="tpu_custom_call", output_to_operand_aliasing={{}: (8, {})} | custom-call | flops 2147483648 | bytes 16777216 | tf_op jit(solution)/shard_map/form_project/pallas_call | solution.py:166
  168.9 8.7 %form_project.15 = f32[512,512]{1,0:T(8,128)} custom-call(s32[10]{0:T(128)S(1)} %pad_add_fusion.blocks_ref, bf16[256,1536]{1,0:T(8,128)(2,1)S(1)} %collective-permute-done.32.refs_0_, bf16[256,1536]{1,0:T(8,128)(2,1)S(1)} %collective-permute-done.29.refs_1_, ...), custom_call_target="tpu_custom_call", output_to_operand_aliasing={{}: (8, {})} | custom-call | flops 2147483648 | bytes 16777216 | tf_op jit(solution)/shard_map/form_project/pallas_call | solution.py:166
  178.0 1.1 dynamic-slice_bitcast_fusion
  179.3 1.8 collective-permute-done.37
  181.1 1.1 bitcast_add_fusion
  182.2 1.5 collective-permute-start.38
  184.0 3.9 %collective-permute-done.38 = bf16[1,128,512]{2,1,0:T(8,128)(2,1)S(1)} collective-permute-done((bf16[1,128,512]{2,1,0:T(8,128)(2,1)S(1)}, bf16[1,128,512]{2,1,0:T(8,128)(2,1)S(1)}, u32[]{:S(2)}, u32[]{:S(2)}) %collective-permute-start.38) | collective-permute-done | bytes 131104 | tf_op jit(solution)/shard_map/ppermute | solution.py:193
  188.5 10.0 %all_to_all.5 = f32[8,34,128]{2,1,0:T(8,128)S(1)} all-to-all(f32[8,34,128]{2,1,0:T(8,128)S(1)} %select_maximum_fusion), channel_id=1, replica_groups=mesh['dp'=8,'fsdp'=4] {'dp'}, dimensions={0} | all-to-all | bytes 278528 | tf_op jit(solution)/shard_map/all_to_all | solution.py:339
  (115 shorter events, 12.6 us)
Async XLA Ops:
  4.5 10.7 %collective-permute-start.4 = (f32[32,2048]{1,0:T(8,128)S(1)}, f32[32,2048]{1,0:T(8,128)}, u32[]{:S(2)}, u32[]{:S(2)}) collective-permute-start(f32[32,2048]{1,0:T(8,128)S(1)} %dynamic-slice_bitcast_fusion.1), channel_id=1, source_target_pairs={{0,1},{1,0},{2,3},{3,2},{4,5},{5,4},{6,7},{7,6},{8,9},{9,8},{10,11... | collective-permute-start | bytes 786440 | tf_op jit(solution)/shard_map/ppermute | solution.py:239
  5.3 8.6 %copy-start.16 = (s32[8]{0:T(128)S(1)}, s32[8]{0:T(128)}, u32[]{:S(2)}) copy-start(s32[8]{0:T(128)} %constant.174.clone) | copy-start | bytes 100
  11.1 7.1 %copy-start.10 = (s32[8]{0:T(128)S(1)}, s32[8]{0:T(128)}, u32[]{:S(2)}) copy-start(s32[8]{0:T(128)} %constant.175.clone) | copy-start | bytes 100
  11.2 24.5 %collective-permute-start.2 = (bf16[256,1536]{1,0:T(8,128)(2,1)S(1)}, bf16[256,1536]{1,0:T(8,128)(2,1)}, u32[]{:S(2)}, u32[]{:S(2)}) collective-permute-start(bf16[256,1536]{1,0:T(8,128)(2,1)S(1)} %get-tuple-element.233.refs_0_), channel_id=1, source_target_pairs={{4,12},{12,20},{20,28},{28,24},{24,16},{16,8},{8,0},{0,4},{5,13},{... | collective-permute-start | bytes 2359304 | tf_op jit(solution)/shard_map/ppermute | solution.py:287
  13.8 21.9 %collective-permute-start.3 = (bf16[256,1536]{1,0:T(8,128)(2,1)S(1)}, bf16[256,1536]{1,0:T(8,128)(2,1)S(1)}, u32[]{:S(2)}, u32[]{:S(2)}) collective-permute-start(bf16[256,1536]{1,0:T(8,128)(2,1)S(1)} %get-tuple-element.232.refs_1_), channel_id=1, source_target_pairs={{12,4},{20,12},{28,20},{24,28},{16,24},{8,16},{0,8},{4,0},{13,5},{... | collective-permute-start | bytes 2359304 | tf_op jit(solution)/shard_map/ppermute | solution.py:288
  16.2 8.5 %collective-permute-start.5 = (f32[32,2048]{1,0:T(8,128)S(1)}, f32[32,2048]{1,0:T(8,128)S(1)}, u32[]{:S(2)}, u32[]{:S(2)}) collective-permute-start(f32[32,2048]{1,0:T(8,128)S(1)} %bitcast_add_fusion.1), channel_id=1, source_target_pairs={{0,2},{1,3},{2,0},{3,1},{4,6},{5,7},{6,4},{7,5},{8,10},{9,11},{10,... | collective-permute-start | bytes 786440 | tf_op jit(solution)/shard_map/ppermute | solution.py:200
  27.3 7.0 %collective-permute-start.6 = (bf16[32,1664]{1,0:T(8,128)(2,1)S(1)}, bf16[32,1664]{1,0:T(8,128)(2,1)S(1)}, u32[]{:S(2)}, u32[]{:S(2)}) collective-permute-start(bf16[32,1664]{1,0:T(8,128)(2,1)S(1)} %pad_maximum_fusion.refs_2_.refs_3_), channel_id=1, source_target_pairs={{4,12},{12,20},{20,28},{28,24},{24,16},{16,8},{8,0},{0,4},{5,13},{... | collective-permute-start | bytes 319496 | tf_op jit(solution)/shard_map/ppermute | solution.py:290
  29.0 6.7 %collective-permute-start.7 = (bf16[32,1664]{1,0:T(8,128)(2,1)S(1)}, bf16[32,1664]{1,0:T(8,128)(2,1)S(1)}, u32[]{:S(2)}, u32[]{:S(2)}) collective-permute-start(bf16[32,1664]{1,0:T(8,128)(2,1)S(1)} %pad_maximum_fusion.refs_2_.refs_3_), channel_id=1, source_target_pairs={{12,4},{20,12},{28,20},{24,28},{16,24},{8,16},{0,8},{4,0},{13,5},{... | collective-permute-start | bytes 319496 | tf_op jit(solution)/shard_map/ppermute | solution.py:292
  35.7 22.5 %collective-permute-start.8 = (bf16[256,1536]{1,0:T(8,128)(2,1)}, bf16[256,1536]{1,0:T(8,128)(2,1)S(1)}, u32[]{:S(2)}, u32[]{:S(2)}) collective-permute-start(bf16[256,1536]{1,0:T(8,128)(2,1)} %collective-permute-done.2.refs_1_), channel_id=1, source_target_pairs={{4,12},{12,20},{20,28},{28,24},{24,16},{16,8},{8,0},{0,4},{5,13},{... | collective-permute-start | bytes 2359304 | tf_op jit(solution)/shard_map/ppermute | solution.py:287
  37.3 20.9 %collective-permute-start.9 = (bf16[256,1536]{1,0:T(8,128)(2,1)S(1)}, bf16[256,1536]{1,0:T(8,128)(2,1)S(1)}, u32[]{:S(2)}, u32[]{:S(2)}) collective-permute-start(bf16[256,1536]{1,0:T(8,128)(2,1)S(1)} %collective-permute-done.3.refs_0_), channel_id=1, source_target_pairs={{12,4},{20,12},{28,20},{24,28},{16,24},{8,16},{0,8},{4,0},{13,5},{... | collective-permute-start | bytes 2359304 | tf_op jit(solution)/shard_map/ppermute | solution.py:288
  37.8 2.1 %collective-permute-start.10 = (bf16[32,1664]{1,0:T(8,128)(2,1)S(1)}, bf16[32,1664]{1,0:T(8,128)(2,1)S(1)}, u32[]{:S(2)}, u32[]{:S(2)}) collective-permute-start(bf16[32,1664]{1,0:T(8,128)(2,1)S(1)} %pad_maximum_fusion.refs_2_.refs_3_), channel_id=1, source_target_pairs={{0,1},{1,0},{2,3},{3,2},{4,5},{5,4},{6,7},{7,6},{8,9},{9,8},{10,11... | collective-permute-start | bytes 319496 | tf_op jit(solution)/shard_map/ppermute | solution.py:294
  37.8 2.5 %collective-permute-start.11 = (bf16[32,1664]{1,0:T(8,128)(2,1)S(1)}, bf16[32,1664]{1,0:T(8,128)(2,1)S(1)}, u32[]{:S(2)}, u32[]{:S(2)}) collective-permute-start(bf16[32,1664]{1,0:T(8,128)(2,1)S(1)} %collective-permute-done.6.refs_3_.refs_2_), channel_id=1, source_target_pairs={{0,1},{1,0},{2,3},{3,2},{4,5},{5,4},{6,7},{7,6},{8,9},{9,8},{10,11... | collective-permute-start | bytes 319496 | tf_op jit(solution)/shard_map/ppermute | solution.py:294
  38.3 18.8 %collective-permute-start.12 = (bf16[32,1664]{1,0:T(8,128)(2,1)S(1)}, bf16[32,1664]{1,0:T(8,128)(2,1)S(1)}, u32[]{:S(2)}, u32[]{:S(2)}) collective-permute-start(bf16[32,1664]{1,0:T(8,128)(2,1)S(1)} %collective-permute-done.6.refs_3_.refs_2_), channel_id=1, source_target_pairs={{4,12},{12,20},{20,28},{28,24},{24,16},{16,8},{8,0},{0,4},{5,13},{... | collective-permute-start | bytes 319496 | tf_op jit(solution)/shard_map/ppermute | solution.py:290
  39.9 18.4 %collective-permute-start.13 = (bf16[32,1664]{1,0:T(8,128)(2,1)S(1)}, bf16[32,1664]{1,0:T(8,128)(2,1)}, u32[]{:S(2)}, u32[]{:S(2)}) collective-permute-start(bf16[32,1664]{1,0:T(8,128)(2,1)S(1)} %collective-permute-done.7.refs_2_.refs_3_), channel_id=1, source_target_pairs={{12,4},{20,12},{28,20},{24,28},{16,24},{8,16},{0,8},{4,0},{13,5},{... | collective-permute-start | bytes 319496 | tf_op jit(solution)/shard_map/ppermute | solution.py:292
  58.3 21.2 %collective-permute-start.14 = (bf16[256,1536]{1,0:T(8,128)(2,1)S(1)}, bf16[256,1536]{1,0:T(8,128)(2,1)S(1)}, u32[]{:S(2)}, u32[]{:S(2)}) collective-permute-start(bf16[256,1536]{1,0:T(8,128)(2,1)S(1)} %collective-permute-done.8.refs_0_), channel_id=1, source_target_pairs={{4,12},{12,20},{20,28},{28,24},{24,16},{16,8},{8,0},{0,4},{5,13},{... | collective-permute-start | bytes 2359304 | tf_op jit(solution)/shard_map/ppermute | solution.py:287
  59.8 19.6 %collective-permute-start.15 = (bf16[256,1536]{1,0:T(8,128)(2,1)S(1)}, bf16[256,1536]{1,0:T(8,128)(2,1)S(1)}, u32[]{:S(2)}, u32[]{:S(2)}) collective-permute-start(bf16[256,1536]{1,0:T(8,128)(2,1)S(1)} %collective-permute-done.9.refs_1_), channel_id=1, source_target_pairs={{12,4},{20,12},{28,20},{24,28},{16,24},{8,16},{0,8},{4,0},{13,5},{... | collective-permute-start | bytes 2359304 | tf_op jit(solution)/shard_map/ppermute | solution.py:288
  60.3 2.0 %collective-permute-start.16 = (bf16[32,1664]{1,0:T(8,128)(2,1)S(1)}, bf16[32,1664]{1,0:T(8,128)(2,1)S(1)}, u32[]{:S(2)}, u32[]{:S(2)}) collective-permute-start(bf16[32,1664]{1,0:T(8,128)(2,1)S(1)} %collective-permute-done.7.refs_2_.refs_3_), channel_id=1, source_target_pairs={{0,1},{1,0},{2,3},{3,2},{4,5},{5,4},{6,7},{7,6},{8,9},{9,8},{10,11... | collective-permute-start | bytes 319496 | tf_op jit(solution)/shard_map/ppermute | solution.py:294
  60.3 17.8 %collective-permute-start.17 = (bf16[32,1664]{1,0:T(8,128)(2,1)S(1)}, bf16[32,1664]{1,0:T(8,128)(2,1)S(1)}, u32[]{:S(2)}, u32[]{:S(2)}) collective-permute-start(bf16[32,1664]{1,0:T(8,128)(2,1)S(1)} %collective-permute-done.12.refs_2_.refs_3_), channel_id=1, source_target_pairs={{4,12},{12,20},{20,28},{28,24},{24,16},{16,8},{8,0},{0,4},{5,13},{... | collective-permute-start | bytes 319496 | tf_op jit(solution)/shard_map/ppermute | solution.py:290
  61.9 17.6 %collective-permute-start.18 = (bf16[32,1664]{1,0:T(8,128)(2,1)}, bf16[32,1664]{1,0:T(8,128)(2,1)}, u32[]{:S(2)}, u32[]{:S(2)}) collective-permute-start(bf16[32,1664]{1,0:T(8,128)(2,1)} %collective-permute-done.13.refs_3_.refs_2_), channel_id=1, source_target_pairs={{12,4},{20,12},{28,20},{24,28},{16,24},{8,16},{0,8},{4,0},{13,5},{... | collective-permute-start | bytes 319496 | tf_op jit(solution)/shard_map/ppermute | solution.py:292
  78.1 24.0 %copy-start.4 = (bf16[32,1664]{1,0:T(8,128)(2,1)}, bf16[32,1664]{1,0:T(8,128)(2,1)S(1)}, u32[]{:S(2)}) copy-start(bf16[32,1664]{1,0:T(8,128)(2,1)S(1)} %collective-permute-done.17.refs_3_.refs_2_) | copy-start | bytes 319492
  79.5 19.8 %collective-permute-start.19 = (bf16[256,1536]{1,0:T(8,128)(2,1)S(1)}, bf16[256,1536]{1,0:T(8,128)(2,1)S(1)}, u32[]{:S(2)}, u32[]{:S(2)}) collective-permute-start(bf16[256,1536]{1,0:T(8,128)(2,1)S(1)} %collective-permute-done.14.refs_1_), channel_id=1, source_target_pairs={{4,12},{12,20},{20,28},{28,24},{24,16},{16,8},{8,0},{0,4},{5,13},{... | collective-permute-start | bytes 2359304 | tf_op jit(solution)/shard_map/ppermute | solution.py:287
  81.0 18.2 %collective-permute-start.20 = (bf16[256,1536]{1,0:T(8,128)(2,1)S(1)}, bf16[256,1536]{1,0:T(8,128)(2,1)S(1)}, u32[]{:S(2)}, u32[]{:S(2)}) collective-permute-start(bf16[256,1536]{1,0:T(8,128)(2,1)S(1)} %collective-permute-done.15.refs_0_), channel_id=1, source_target_pairs={{12,4},{20,12},{28,20},{24,28},{16,24},{8,16},{0,8},{4,0},{13,5},{... | collective-permute-start | bytes 2359304 | tf_op jit(solution)/shard_map/ppermute | solution.py:288
  81.5 2.1 %collective-permute-start.21 = (bf16[32,1664]{1,0:T(8,128)(2,1)S(1)}, bf16[32,1664]{1,0:T(8,128)(2,1)S(1)}, u32[]{:S(2)}, u32[]{:S(2)}) collective-permute-start(bf16[32,1664]{1,0:T(8,128)(2,1)S(1)} %collective-permute-done.12.refs_2_.refs_3_), channel_id=1, source_target_pairs={{0,1},{1,0},{2,3},{3,2},{4,5},{5,4},{6,7},{7,6},{8,9},{9,8},{10,11... | collective-permute-start | bytes 319496 | tf_op jit(solution)/shard_map/ppermute | solution.py:294
  81.5 2.1 %collective-permute-start.22 = (bf16[32,1664]{1,0:T(8,128)(2,1)S(1)}, bf16[32,1664]{1,0:T(8,128)(2,1)S(1)}, u32[]{:S(2)}, u32[]{:S(2)}) collective-permute-start(bf16[32,1664]{1,0:T(8,128)(2,1)S(1)} %collective-permute-done.17.refs_3_.refs_2_), channel_id=1, source_target_pairs={{0,1},{1,0},{2,3},{3,2},{4,5},{5,4},{6,7},{7,6},{8,9},{9,8},{10,11... | collective-permute-start | bytes 319496 | tf_op jit(solution)/shard_map/ppermute | solution.py:294
  82.0 17.2 %collective-permute-start.23 = (bf16[32,1664]{1,0:T(8,128)(2,1)S(1)}, bf16[32,1664]{1,0:T(8,128)(2,1)S(1)}, u32[]{:S(2)}, u32[]{:S(2)}) collective-permute-start(bf16[32,1664]{1,0:T(8,128)(2,1)S(1)} %collective-permute-done.17.refs_3_.refs_2_), channel_id=1, source_target_pairs={{4,12},{12,20},{20,28},{28,24},{24,16},{16,8},{8,0},{0,4},{5,13},{... | collective-permute-start | bytes 319496 | tf_op jit(solution)/shard_map/ppermute | solution.py:290
  83.6 10.6 %copy-start.6 = (bf16[32,1664]{1,0:T(8,128)(2,1)}, bf16[32,1664]{1,0:T(8,128)(2,1)S(1)}, u32[]{:S(2)}) copy-start(bf16[32,1664]{1,0:T(8,128)(2,1)S(1)} %collective-permute-done.22.refs_5_.refs_4_) | copy-start | bytes 319492
  94.2 7.8 %copy-start.11 = (f32[512,512]{1,0:T(8,128)}, f32[512,512]{1,0:T(8,128)S(1)}, u32[]{:S(2)}) copy-start(f32[512,512]{1,0:T(8,128)S(1)} %form_project.10.refs_7_) | copy-start | bytes 3145732
  99.3 17.2 %collective-permute-start.24 = (bf16[256,1536]{1,0:T(8,128)(2,1)S(1)}, bf16[256,1536]{1,0:T(8,128)(2,1)}, u32[]{:S(2)}, u32[]{:S(2)}) collective-permute-start(bf16[256,1536]{1,0:T(8,128)(2,1)S(1)} %collective-permute-done.19.refs_0_), channel_id=1, source_target_pairs={{4,12},{12,20},{20,28},{28,24},{24,16},{16,8},{8,0},{0,4},{5,13},{... | collective-permute-start | bytes 2359304 | tf_op jit(solution)/shard_map/ppermute | solution.py:287
  100.8 15.6 %collective-permute-start.25 = (bf16[256,1536]{1,0:T(8,128)(2,1)S(1)}, bf16[256,1536]{1,0:T(8,128)(2,1)}, u32[]{:S(2)}, u32[]{:S(2)}) collective-permute-start(bf16[256,1536]{1,0:T(8,128)(2,1)S(1)} %collective-permute-done.20.refs_1_), channel_id=1, source_target_pairs={{12,4},{20,12},{28,20},{24,28},{16,24},{8,16},{0,8},{4,0},{13,5},{... | collective-permute-start | bytes 2359304 | tf_op jit(solution)/shard_map/ppermute | solution.py:288
  102.0 2.7 %collective-permute-start.27 = (bf16[32,1664]{1,0:T(8,128)(2,1)}, bf16[32,1664]{1,0:T(8,128)(2,1)}, u32[]{:S(2)}, u32[]{:S(2)}) collective-permute-start(bf16[32,1664]{1,0:T(8,128)(2,1)} %collective-permute-done.13.refs_3_.refs_2_), channel_id=1, source_target_pairs={{0,1},{1,0},{2,3},{3,2},{4,5},{5,4},{6,7},{7,6},{8,9},{9,8},{10,11... | collective-permute-start | bytes 319496 | tf_op jit(solution)/shard_map/ppermute | solution.py:294
  102.7 2.1 %collective-permute-start.26 = (bf16[32,1664]{1,0:T(8,128)(2,1)}, bf16[32,1664]{1,0:T(8,128)(2,1)}, u32[]{:S(2)}, u32[]{:S(2)}) collective-permute-start(bf16[32,1664]{1,0:T(8,128)(2,1)} %collective-permute-done.18.refs_2_.refs_3_), channel_id=1, source_target_pairs={{0,1},{1,0},{2,3},{3,2},{4,5},{5,4},{6,7},{7,6},{8,9},{9,8},{10,11... | collective-permute-start | bytes 319496 | tf_op jit(solution)/shard_map/ppermute | solution.py:294
  104.7 13.8 %copy-start.9 = (bf16[32,1664]{1,0:T(8,128)(2,1)S(1)}, bf16[32,1664]{1,0:T(8,128)(2,1)}, u32[]{:S(2)}) copy-start(bf16[32,1664]{1,0:T(8,128)(2,1)} %copy-done.8) | copy-start | bytes 319492
  116.4 23.1 %copy-start.5 = (bf16[32,1664]{1,0:T(8,128)(2,1)S(1)}, bf16[32,1664]{1,0:T(8,128)(2,1)}, u32[]{:S(2)}) copy-start(bf16[32,1664]{1,0:T(8,128)(2,1)} %copy-done.4) | copy-start | bytes 319492
  116.4 23.1 %copy-start.7 = (bf16[32,1664]{1,0:T(8,128)(2,1)S(1)}, bf16[32,1664]{1,0:T(8,128)(2,1)}, u32[]{:S(2)}) copy-start(bf16[32,1664]{1,0:T(8,128)(2,1)} %copy-done.6) | copy-start | bytes 319492
  116.5 19.8 %collective-permute-start.28 = (bf16[256,1536]{1,0:T(8,128)(2,1)}, bf16[256,1536]{1,0:T(8,128)(2,1)S(1)}, u32[]{:S(2)}, u32[]{:S(2)}) collective-permute-start(bf16[256,1536]{1,0:T(8,128)(2,1)} %collective-permute-done.24.refs_1_), channel_id=1, source_target_pairs={{4,12},{12,20},{20,28},{28,24},{24,16},{16,8},{8,0},{0,4},{5,13},{... | collective-permute-start | bytes 2359304 | tf_op jit(solution)/shard_map/ppermute | solution.py:287
  118.1 19.5 %collective-permute-start.29 = (bf16[256,1536]{1,0:T(8,128)(2,1)}, bf16[256,1536]{1,0:T(8,128)(2,1)S(1)}, u32[]{:S(2)}, u32[]{:S(2)}) collective-permute-start(bf16[256,1536]{1,0:T(8,128)(2,1)} %collective-permute-done.25.refs_0_), channel_id=1, source_target_pairs={{12,4},{20,12},{28,20},{24,28},{16,24},{8,16},{0,8},{4,0},{13,5},{... | collective-permute-start | bytes 2359304 | tf_op jit(solution)/shard_map/ppermute | solution.py:288
  118.6 1.3 collective-permute-start.30
  137.5 18.4 %collective-permute-start.31 = (bf16[256,1536]{1,0:T(8,128)(2,1)S(1)}, bf16[256,1536]{1,0:T(8,128)(2,1)S(1)}, u32[]{:S(2)}, u32[]{:S(2)}) collective-permute-start(bf16[256,1536]{1,0:T(8,128)(2,1)S(1)} %collective-permute-done.28.refs_0_), channel_id=1, source_target_pairs={{4,12},{12,20},{20,28},{28,24},{24,16},{16,8},{8,0},{0,4},{5,13},{... | collective-permute-start | bytes 2359304 | tf_op jit(solution)/shard_map/ppermute | solution.py:287
  138.6 18.2 %collective-permute-start.32 = (bf16[256,1536]{1,0:T(8,128)(2,1)S(1)}, bf16[256,1536]{1,0:T(8,128)(2,1)S(1)}, u32[]{:S(2)}, u32[]{:S(2)}) collective-permute-start(bf16[256,1536]{1,0:T(8,128)(2,1)S(1)} %collective-permute-done.29.refs_1_), channel_id=1, source_target_pairs={{12,4},{20,12},{28,20},{24,28},{16,24},{8,16},{0,8},{4,0},{13,5},{... | collective-permute-start | bytes 2359304 | tf_op jit(solution)/shard_map/ppermute | solution.py:288
  139.5 17.8 %collective-permute-start.35 = (bf16[32,1664]{1,0:T(8,128)(2,1)}, bf16[32,1664]{1,0:T(8,128)(2,1)}, u32[]{:S(2)}, u32[]{:S(2)}) collective-permute-start(bf16[32,1664]{1,0:T(8,128)(2,1)} %collective-permute-done.13.refs_3_.refs_2_), channel_id=1, source_target_pairs={{0,1},{1,0},{2,3},{3,2},{4,5},{5,4},{6,7},{7,6},{8,9},{9,8},{10,11... | collective-permute-start | bytes 319496 | tf_op jit(solution)/shard_map/ppermute | solution.py:294
  156.8 1.3 collective-permute-start.36
  156.8 12.1 %collective-permute-start.34 = (bf16[32,1664]{1,0:T(8,128)(2,1)S(1)}, bf16[32,1664]{1,0:T(8,128)(2,1)S(1)}, u32[]{:S(2)}, u32[]{:S(2)}) collective-permute-start(bf16[32,1664]{1,0:T(8,128)(2,1)S(1)} %collective-permute-done.12.refs_2_.refs_3_), channel_id=1, source_target_pairs={{0,1},{1,0},{2,3},{3,2},{4,5},{5,4},{6,7},{7,6},{8,9},{9,8},{10,11... | collective-permute-start | bytes 319496 | tf_op jit(solution)/shard_map/ppermute | solution.py:294
  157.3 11.6 %collective-permute-start.33 = (bf16[32,1664]{1,0:T(8,128)(2,1)S(1)}, bf16[32,1664]{1,0:T(8,128)(2,1)S(1)}, u32[]{:S(2)}, u32[]{:S(2)}) collective-permute-start(bf16[32,1664]{1,0:T(8,128)(2,1)S(1)} %collective-permute-done.6.refs_3_.refs_2_), channel_id=1, source_target_pairs={{0,1},{1,0},{2,3},{3,2},{4,5},{5,4},{6,7},{7,6},{8,9},{9,8},{10,11... | collective-permute-start | bytes 319496 | tf_op jit(solution)/shard_map/ppermute | solution.py:294
  168.9 8.8 %copy-start.14 = (bf16[32,2048]{1,0:T(8,128)(2,1)S(1)}, bf16[32,2048]{1,0:T(8,128)(2,1)}, u32[]{:S(2)}) copy-start(bf16[32,2048]{1,0:T(8,128)(2,1)} %copy-done.13) | copy-start | bytes 393220
  177.7 6.1 %copy-start.12 = (bf16[256,512]{1,0:T(8,128)(2,1)S(1)}, bf16[256,512]{1,0:T(8,128)(2,1)}, u32[]{:S(2)}) copy-start(bf16[256,512]{1,0:T(8,128)(2,1)} %param.17) | copy-start | bytes 786436
  178.0 21.3 %copy-start.1 = (bf16[64,1024]{1,0:T(8,128)(2,1)S(1)}, bf16[64,1024]{1,0:T(8,128)(2,1)}, u32[]{:S(2)}) copy-start(bf16[64,1024]{1,0:T(8,128)(2,1)} %param.14) | copy-start | bytes 393220
  179.1 2.0 collective-permute-start.37
  182.2 5.6 %collective-permute-start.38 = (bf16[1,128,512]{2,1,0:T(8,128)(2,1)S(1)}, bf16[1,128,512]{2,1,0:T(8,128)(2,1)S(1)}, u32[]{:S(2)}, u32[]{:S(2)}) collective-permute-start(bf16[1,128,512]{2,1,0:T(8,128)(2,1)S(1)} %dynamic-slice_convert_fusion), channel_id=1, source_target_pairs={{0,2},{1,3},{2,0},{3,1},{4,6},{5,7},{6,4},{7,5},{8,10},{9,11},{10,... | collective-permute-start | bytes 393224 | tf_op jit(solution)/shard_map/ppermute | solution.py:193
  (6 other events, 14.5 us)

commit v4 on v3

--- a/solution.py
+++ b/solution.py
@@ -271,7 +271,7 @@
         )
 
     for s in range(dp):
-        keys = [k for k in dict.fromkeys((s, dp - s)) if k in halves]
+        keys = [k for k in dict.fromkeys((s, dp - s)) if k in halves and k not in acts]
         if s == dp // 2 + 1:
             used = jnp.stack([halves[i][0, room : room + pool] for i in range(dp)])
             overflow = jnp.max(jnp.sum(used.astype(jnp.int32), axis=1)) > room

time: 200 us -> 198 us (0.990)
  waiting for transfers between devices: 47.9 us -> 44.4 us
    ppermute x7, waiting for transfers between devices: 9.14 us -> 5.69 us  [per_device(): low[s + 1] = lax.ppermute(low[s], 'dp', ahead)]
    unnamed x34 -> x48, local copies, waits for them, and re-layouts: 3 us -> 4.57 us
  transfers between devices with their start and end apart: 37 -> 33, of which waited for: 15 -> 15; matrix products, arithmetic and copies ran while one was open for 7% -> 7% of each run, Pallas kernels for 39% -> 35%
where the time goes in v4:
time: 198 us; the launch traced here: 197 us
  Pallas kernels  86.8 us (44%)
  waiting for transfers between devices  44.4 us (22%)
  starting transfers between devices  28.3 us (14%)
  matrix products  12.3 us (6%)
  blocking collectives  9.96 us (5%)
  local copies, waits for them, and re-layouts  8.82 us (4%)
  other arithmetic  4.85 us (2%)
    pallas_call x8, Pallas kernels, form_project(): pl.pallas_call(functools.partial(form_project_kernel, dims), out_shape=ja...  86.8 us
    ppermute x4, waiting for transfers between devices, per_device(): halves[s + 1] = lax.ppermute(halves[s], 'dp', ahead)  19.9 us
    ppermute x7, starting transfers between devices, per_device(): low[s + 1] = lax.ppermute(low[s], 'dp', ahead)  11.5 us
    all_to_all x1, blocking collectives, per_device(): got = jnp.sum(lax.all_to_all(sent, 'dp', 0, 0), axis=0)  9.96 us
    ppermute x4, starting transfers between devices, per_device(): halves[s + 1] = lax.ppermute(halves[s], 'dp', ahead)  6.4 us
    ppermute x1, waiting for transfers between devices, exchange_total(): x = x + lax.ppermute(x, axis, [(i, i ^ bit) for i in range(n)])  5.87 us
    dot_general x1, matrix products, per_device(): lax.dot_general(grad_rows.reshape(pool * length, outs), select, (((0,), (...  5.76 us
    ppermute x2, waiting for transfers between devices, exchange_sum(): slots = keep + lax.ppermute(send, axis, swap).astype(F32)  5.7 us
  transfers between devices with their start and end apart: 33, of which 15 were waited for; matrix products, arithmetic and copies ran while one was open for 7% of the time, Pallas kernels for 35%

profile of v4, /device:TPU:0, one launch (start us, length us, event | category | flops | bytes accessed | tf_op | source)
XLA Modules:
  0.0 196.9 jit_solution(10208430239495840101)
XLA Ops:
  0.0 0.9 copy-done
  0.9 3.6 %fusion.37 = f32[2,32,2048]{2,1,0:T(8,128)S(1)} fusion(bf16[2,32,1024]{2,1,0:T(8,128)(2,1)S(1)} %bitcast.79, bf16[2048,1024,1]{1,0,2:T(8,128)(2,1)} %bitcast.82), kind=kOutput, calls=%fused_computation.79 | convolution fusion | flops 268435456 | bytes 4849664 | tf_op jit(solution)/shard_map/dot_general | solution.py:231
  5.3 5.8 %fusion.12 = bf16[512,1536]{1,0:T(8,128)(2,1)S(1)} fusion(bf16[2048,512]{1,0:T(8,128)(2,1)} %bitcast.83, s32[2048]{0:T(1024)S(1)} %select_n.130), kind=kOutput, calls=%fused_computation.17 | convolution fusion | flops 3225157632 | bytes 3678208 | tf_op jit(solution)/shard_map/dot_general | solution.py:217
  11.2 2.6 %collective-permute-start.2 = (bf16[256,1536]{1,0:T(8,128)(2,1)S(1)}, bf16[256,1536]{1,0:T(8,128)(2,1)}, u32[]{:S(2)}, u32[]{:S(2)}) collective-permute-start(bf16[256,1536]{1,0:T(8,128)(2,1)S(1)} %get-tuple-element.225.refs_0_), channel_id=1, source_target_pairs={{4,12},{12,20},{20,28},{28,24},{24,16},{16,8},{8,0},{0,4},{5,13},{... | collective-permute-start | bytes 2359304 | tf_op jit(solution)/shard_map/ppermute | solution.py:287
  15.2 1.0 bitcast_add_fusion.1
  16.1 1.9 collective-permute-start.5
  18.8 5.9 %collective-permute-done.5 = f32[32,2048]{1,0:T(8,128)S(1)} collective-permute-done((f32[32,2048]{1,0:T(8,128)S(1)}, f32[32,2048]{1,0:T(8,128)S(1)}, u32[]{:S(2)}, u32[]{:S(2)}) %collective-permute-start.5) | collective-permute-done | bytes 262176 | tf_op jit(solution)/shard_map/ppermute | solution.py:200
  24.7 2.5 %fusion.13 = bf16[32,1536]{1,0:T(8,128)(2,1)S(1)} fusion(bf16[32,2048]{1,0:T(8,128)(2,1)S(1)} %multiply_convert_fusion, s32[2048]{0:T(1024)S(1)} %select_n.130), kind=kOutput, calls=%fused_computation.18 | convolution fusion | flops 204521472 | bytes 237568 | tf_op jit(solution)/shard_map/dot_general | solution.py:253
  27.2 1.7 collective-permute-start.6
  29.4 4.9 %collective-permute-done.6.refs_3_.refs_2_ = bf16[32,1664]{1,0:T(8,128)(2,1)S(1)} collective-permute-done((bf16[32,1664]{1,0:T(8,128)(2,1)S(1)}, bf16[32,1664]{1,0:T(8,128)(2,1)S(1)}, u32[]{:S(2)}, u32[]{:S(2)}) %collective-permute-start.6) | collective-permute-done | bytes 106528 | tf_op jit(solution)/shard_map/ppermute | solution.py:290
  34.3 1.4 collective-permute-done.7.refs_2_.refs_3_
  35.7 1.6 collective-permute-start.8
  38.3 1.6 collective-permute-start.12
  40.4 11.7 %form_project.8.refs_7_ = f32[512,512]{1,0:T(8,128)S(1)} custom-call(s32[10]{0:T(128)S(1)} %pad_add_fusion.blocks_ref, bf16[256,1536]{1,0:T(8,128)(2,1)S(1)} %get-tuple-element.225.refs_0_, bf16[256,1536]{1,0:T(8,128)(2,1)} %collective-permute-done.2.refs_1_, bf16[32,1664]{1,0:T(8,128)(2,1)S(1)} %pad_maximum_fusion.refs_2_.refs_3_, ...), custom_call_target="tpu_custom_call", output_to_operand_aliasing={{}: (8, {})} | custom-call | flops 2147483648 | bytes 16777216 | tf_op jit(solution)/shard_map/form_project/pallas_call | solution.py:166
  52.2 4.9 %collective-permute-done.12.refs_2_.refs_3_ = bf16[32,1664]{1,0:T(8,128)(2,1)S(1)} collective-permute-done((bf16[32,1664]{1,0:T(8,128)(2,1)S(1)}, bf16[32,1664]{1,0:T(8,128)(2,1)S(1)}, u32[]{:S(2)}, u32[]{:S(2)}) %collective-permute-start.12) | collective-permute-done | bytes 106528 | tf_op jit(solution)/shard_map/ppermute | solution.py:290
  57.1 1.2 collective-permute-done.13.refs_3_.refs_2_
  58.3 1.6 collective-permute-start.14
  60.3 1.6 collective-permute-start.17
  62.3 10.6 %form_project.9.refs_7_ = f32[512,512]{1,0:T(8,128)S(1)} custom-call(s32[10]{0:T(128)S(1)} %pad_add_fusion.blocks_ref, bf16[256,1536]{1,0:T(8,128)(2,1)S(1)} %collective-permute-done.3.refs_0_, bf16[256,1536]{1,0:T(8,128)(2,1)S(1)} %get-tuple-element.224.refs_1_, ...), custom_call_target="tpu_custom_call", output_to_operand_aliasing={{}: (8, {})} | custom-call | flops 2147483648 | bytes 16777216 | tf_op jit(solution)/shard_map/form_project/pallas_call | solution.py:166
  72.9 5.1 %collective-permute-done.17.refs_3_.refs_2_ = bf16[32,1664]{1,0:T(8,128)(2,1)S(1)} collective-permute-done((bf16[32,1664]{1,0:T(8,128)(2,1)S(1)}, bf16[32,1664]{1,0:T(8,128)(2,1)S(1)}, u32[]{:S(2)}, u32[]{:S(2)}) %collective-permute-start.17) | collective-permute-done | bytes 106528 | tf_op jit(solution)/shard_map/ppermute | solution.py:290
  78.1 1.4 collective-permute-done.18.refs_2_.refs_3_
  79.5 1.6 collective-permute-start.19
  82.0 1.6 collective-permute-start.23
  83.6 10.6 %form_project.10.refs_7_ = f32[512,512]{1,0:T(8,128)S(1)} custom-call(s32[10]{0:T(128)S(1)} %pad_add_fusion.blocks_ref, bf16[256,1536]{1,0:T(8,128)(2,1)S(1)} %collective-permute-done.8.refs_0_, bf16[256,1536]{1,0:T(8,128)(2,1)S(1)} %collective-permute-done.14.refs_1_, ...), custom_call_target="tpu_custom_call", output_to_operand_aliasing={{}: (8, {})} | custom-call | flops 2147483648 | bytes 16777216 | tf_op jit(solution)/shard_map/form_project/pallas_call | solution.py:166
  94.3 5.0 %collective-permute-done.23.refs_2_.refs_3_ = bf16[32,1664]{1,0:T(8,128)(2,1)S(1)} collective-permute-done((bf16[32,1664]{1,0:T(8,128)(2,1)S(1)}, bf16[32,1664]{1,0:T(8,128)(2,1)S(1)}, u32[]{:S(2)}, u32[]{:S(2)}) %collective-permute-start.23) | collective-permute-done | bytes 106528 | tf_op jit(solution)/shard_map/ppermute | solution.py:290
  99.2 1.6 collective-permute-start.24
  104.7 11.7 %form_project.11.refs_7_ = f32[512,512]{1,0:T(8,128)} custom-call(s32[10]{0:T(128)S(1)} %pad_add_fusion.blocks_ref, bf16[256,1536]{1,0:T(8,128)(2,1)S(1)} %collective-permute-done.15.refs_0_, bf16[256,1536]{1,0:T(8,128)(2,1)S(1)} %collective-permute-done.9.refs_1_, ...), custom_call_target="tpu_custom_call", output_to_operand_aliasing={{}: (8, {})} | custom-call | flops 2147483648 | bytes 16777216 | tf_op jit(solution)/shard_map/form_project/pallas_call | solution.py:166
  116.4 1.6 collective-permute-start.28
  118.5 1.3 collective-permute-done.30.refs_4_.refs_5_
  119.8 11.8 %form_project.12.refs_7_ = f32[512,512]{1,0:T(8,128)} custom-call(s32[10]{0:T(128)S(1)} %pad_add_fusion.blocks_ref, bf16[256,1536]{1,0:T(8,128)(2,1)S(1)} %collective-permute-done.19.refs_0_, bf16[256,1536]{1,0:T(8,128)(2,1)} %collective-permute-done.24.refs_1_, bf16[32,1664]{1,0:T(8,128)(2,1)S(1)} %copy-done.13, ...), custom_call_target="tpu_custom_call", output_to_operand_aliasing={{}: (8, {})} | custom-call | flops 2147483648 | bytes 16777216 | tf_op jit(solution)/shard_map/form_project/pallas_call | solution.py:166
  131.7 4.6 %collective-permute-done.28.refs_0_ = bf16[256,1536]{1,0:T(8,128)(2,1)S(1)} collective-permute-done((bf16[256,1536]{1,0:T(8,128)(2,1)}, bf16[256,1536]{1,0:T(8,128)(2,1)S(1)}, u32[]{:S(2)}, u32[]{:S(2)}) %collective-permute-start.28) | collective-permute-done | bytes 786464 | tf_op jit(solution)/shard_map/ppermute | solution.py:287
  136.2 1.3 collective-permute-done.29.refs_1_
  137.5 1.0 collective-permute-start.31
  138.5 1.0 collective-permute-start.32
  139.6 0.9 copy-done.7
  140.4 0.9 copy-done.11
  141.3 0.9 copy-done.14
  142.2 0.9 copy-done.16
  143.1 11.8 %form_project.13.refs_7_ = f32[512,512]{1,0:T(8,128)} custom-call(s32[10]{0:T(128)S(1)} %pad_add_fusion.blocks_ref, bf16[256,1536]{1,0:T(8,128)(2,1)} %collective-permute-done.25.refs_0_, bf16[256,1536]{1,0:T(8,128)(2,1)S(1)} %collective-permute-done.20.refs_1_, bf16[32,1664]{1,0:T(8,128)(2,1)S(1)} %copy-done.7, ...), custom_call_target="tpu_custom_call", output_to_operand_aliasing={{}: (8, {})} | custom-call | flops 2147483648 | bytes 16777216 | tf_op jit(solution)/shard_map/form_project/pallas_call | solution.py:166
  154.9 1.1 collective-permute-done.31.refs_1_
  156.7 9.9 %form_project.14.refs_7_ = f32[512,512]{1,0:T(8,128)} custom-call(s32[10]{0:T(128)S(1)} %pad_add_fusion.blocks_ref, bf16[256,1536]{1,0:T(8,128)(2,1)S(1)} %collective-permute-done.28.refs_0_, bf16[256,1536]{1,0:T(8,128)(2,1)} %collective-permute-done.31.refs_1_, ...), custom_call_target="tpu_custom_call", output_to_operand_aliasing={{}: (8, {})} | custom-call | flops 2147483648 | bytes 16777216 | tf_op jit(solution)/shard_map/form_project/pallas_call | solution.py:166
  166.6 8.7 %form_project.15 = f32[512,512]{1,0:T(8,128)} custom-call(s32[10]{0:T(128)S(1)} %pad_add_fusion.blocks_ref, bf16[256,1536]{1,0:T(8,128)(2,1)S(1)} %collective-permute-done.32.refs_0_, bf16[256,1536]{1,0:T(8,128)(2,1)S(1)} %collective-permute-done.29.refs_1_, ...), custom_call_target="tpu_custom_call", output_to_operand_aliasing={{}: (8, {})} | custom-call | flops 2147483648 | bytes 16777216 | tf_op jit(solution)/shard_map/form_project/pallas_call | solution.py:166
  175.7 1.1 dynamic-slice_bitcast_fusion
  176.9 1.9 collective-permute-done.33
  178.8 1.1 bitcast_add_fusion
  179.9 1.6 collective-permute-start.34
  181.7 3.8 %collective-permute-done.34 = bf16[1,128,512]{2,1,0:T(8,128)(2,1)S(1)} collective-permute-done((bf16[1,128,512]{2,1,0:T(8,128)(2,1)S(1)}, bf16[1,128,512]{2,1,0:T(8,128)(2,1)S(1)}, u32[]{:S(2)}, u32[]{:S(2)}) %collective-permute-start.34) | collective-permute-done | bytes 131104 | tf_op jit(solution)/shard_map/ppermute | solution.py:193
  186.2 10.0 %all_to_all.5 = f32[8,34,128]{2,1,0:T(8,128)S(1)} all-to-all(f32[8,34,128]{2,1,0:T(8,128)S(1)} %select_maximum_fusion), channel_id=1, replica_groups=mesh['dp'=8,'fsdp'=4] {'dp'}, dimensions={0} | all-to-all | bytes 278528 | tf_op jit(solution)/shard_map/all_to_all | solution.py:339
  (121 shorter events, 13.2 us)
Async XLA Ops:
  4.5 10.6 %collective-permute-start.4 = (f32[32,2048]{1,0:T(8,128)S(1)}, f32[32,2048]{1,0:T(8,128)}, u32[]{:S(2)}, u32[]{:S(2)}) collective-permute-start(f32[32,2048]{1,0:T(8,128)S(1)} %dynamic-slice_bitcast_fusion.1), channel_id=1, source_target_pairs={{0,1},{1,0},{2,3},{3,2},{4,5},{5,4},{6,7},{7,6},{8,9},{9,8},{10,11... | collective-permute-start | bytes 786440 | tf_op jit(solution)/shard_map/ppermute | solution.py:239
  5.3 8.6 %copy-start.23 = (s32[8]{0:T(128)S(1)}, s32[8]{0:T(128)}, u32[]{:S(2)}) copy-start(s32[8]{0:T(128)} %constant.174.clone) | copy-start | bytes 100
  11.1 7.0 %copy-start.17 = (s32[8]{0:T(128)S(1)}, s32[8]{0:T(128)}, u32[]{:S(2)}) copy-start(s32[8]{0:T(128)} %constant.175.clone) | copy-start | bytes 100
  11.2 24.5 %collective-permute-start.2 = (bf16[256,1536]{1,0:T(8,128)(2,1)S(1)}, bf16[256,1536]{1,0:T(8,128)(2,1)}, u32[]{:S(2)}, u32[]{:S(2)}) collective-permute-start(bf16[256,1536]{1,0:T(8,128)(2,1)S(1)} %get-tuple-element.225.refs_0_), channel_id=1, source_target_pairs={{4,12},{12,20},{20,28},{28,24},{24,16},{16,8},{8,0},{0,4},{5,13},{... | collective-permute-start | bytes 2359304 | tf_op jit(solution)/shard_map/ppermute | solution.py:287
  13.8 21.9 %collective-permute-start.3 = (bf16[256,1536]{1,0:T(8,128)(2,1)S(1)}, bf16[256,1536]{1,0:T(8,128)(2,1)S(1)}, u32[]{:S(2)}, u32[]{:S(2)}) collective-permute-start(bf16[256,1536]{1,0:T(8,128)(2,1)S(1)} %get-tuple-element.224.refs_1_), channel_id=1, source_target_pairs={{12,4},{20,12},{28,20},{24,28},{16,24},{8,16},{0,8},{4,0},{13,5},{... | collective-permute-start | bytes 2359304 | tf_op jit(solution)/shard_map/ppermute | solution.py:288
  16.1 8.5 %collective-permute-start.5 = (f32[32,2048]{1,0:T(8,128)S(1)}, f32[32,2048]{1,0:T(8,128)S(1)}, u32[]{:S(2)}, u32[]{:S(2)}) collective-permute-start(f32[32,2048]{1,0:T(8,128)S(1)} %bitcast_add_fusion.1), channel_id=1, source_target_pairs={{0,2},{1,3},{2,0},{3,1},{4,6},{5,7},{6,4},{7,5},{8,10},{9,11},{10,... | collective-permute-start | bytes 786440 | tf_op jit(solution)/shard_map/ppermute | solution.py:200
  27.2 7.1 %collective-permute-start.6 = (bf16[32,1664]{1,0:T(8,128)(2,1)S(1)}, bf16[32,1664]{1,0:T(8,128)(2,1)S(1)}, u32[]{:S(2)}, u32[]{:S(2)}) collective-permute-start(bf16[32,1664]{1,0:T(8,128)(2,1)S(1)} %pad_maximum_fusion.refs_2_.refs_3_), channel_id=1, source_target_pairs={{4,12},{12,20},{20,28},{28,24},{24,16},{16,8},{8,0},{0,4},{5,13},{... | collective-permute-start | bytes 319496 | tf_op jit(solution)/shard_map/ppermute | solution.py:290
  28.9 6.8 %collective-permute-start.7 = (bf16[32,1664]{1,0:T(8,128)(2,1)S(1)}, bf16[32,1664]{1,0:T(8,128)(2,1)S(1)}, u32[]{:S(2)}, u32[]{:S(2)}) collective-permute-start(bf16[32,1664]{1,0:T(8,128)(2,1)S(1)} %pad_maximum_fusion.refs_2_.refs_3_), channel_id=1, source_target_pairs={{12,4},{20,12},{28,20},{24,28},{16,24},{8,16},{0,8},{4,0},{13,5},{... | collective-permute-start | bytes 319496 | tf_op jit(solution)/shard_map/ppermute | solution.py:292
  35.7 22.5 %collective-permute-start.8 = (bf16[256,1536]{1,0:T(8,128)(2,1)}, bf16[256,1536]{1,0:T(8,128)(2,1)S(1)}, u32[]{:S(2)}, u32[]{:S(2)}) collective-permute-start(bf16[256,1536]{1,0:T(8,128)(2,1)} %collective-permute-done.2.refs_1_), channel_id=1, source_target_pairs={{4,12},{12,20},{20,28},{28,24},{24,16},{16,8},{8,0},{0,4},{5,13},{... | collective-permute-start | bytes 2359304 | tf_op jit(solution)/shard_map/ppermute | solution.py:287
  37.3 20.9 %collective-permute-start.9 = (bf16[256,1536]{1,0:T(8,128)(2,1)S(1)}, bf16[256,1536]{1,0:T(8,128)(2,1)S(1)}, u32[]{:S(2)}, u32[]{:S(2)}) collective-permute-start(bf16[256,1536]{1,0:T(8,128)(2,1)S(1)} %collective-permute-done.3.refs_0_), channel_id=1, source_target_pairs={{12,4},{20,12},{28,20},{24,28},{16,24},{8,16},{0,8},{4,0},{13,5},{... | collective-permute-start | bytes 2359304 | tf_op jit(solution)/shard_map/ppermute | solution.py:288
  37.8 2.1 %collective-permute-start.10 = (bf16[32,1664]{1,0:T(8,128)(2,1)S(1)}, bf16[32,1664]{1,0:T(8,128)(2,1)S(1)}, u32[]{:S(2)}, u32[]{:S(2)}) collective-permute-start(bf16[32,1664]{1,0:T(8,128)(2,1)S(1)} %pad_maximum_fusion.refs_2_.refs_3_), channel_id=1, source_target_pairs={{0,1},{1,0},{2,3},{3,2},{4,5},{5,4},{6,7},{7,6},{8,9},{9,8},{10,11... | collective-permute-start | bytes 319496 | tf_op jit(solution)/shard_map/ppermute | solution.py:294
  37.8 2.5 %collective-permute-start.11 = (bf16[32,1664]{1,0:T(8,128)(2,1)S(1)}, bf16[32,1664]{1,0:T(8,128)(2,1)S(1)}, u32[]{:S(2)}, u32[]{:S(2)}) collective-permute-start(bf16[32,1664]{1,0:T(8,128)(2,1)S(1)} %collective-permute-done.6.refs_3_.refs_2_), channel_id=1, source_target_pairs={{0,1},{1,0},{2,3},{3,2},{4,5},{5,4},{6,7},{7,6},{8,9},{9,8},{10,11... | collective-permute-start | bytes 319496 | tf_op jit(solution)/shard_map/ppermute | solution.py:294
  38.3 18.8 %collective-permute-start.12 = (bf16[32,1664]{1,0:T(8,128)(2,1)S(1)}, bf16[32,1664]{1,0:T(8,128)(2,1)S(1)}, u32[]{:S(2)}, u32[]{:S(2)}) collective-permute-start(bf16[32,1664]{1,0:T(8,128)(2,1)S(1)} %collective-permute-done.6.refs_3_.refs_2_), channel_id=1, source_target_pairs={{4,12},{12,20},{20,28},{28,24},{24,16},{16,8},{8,0},{0,4},{5,13},{... | collective-permute-start | bytes 319496 | tf_op jit(solution)/shard_map/ppermute | solution.py:290
  39.9 18.4 %collective-permute-start.13 = (bf16[32,1664]{1,0:T(8,128)(2,1)S(1)}, bf16[32,1664]{1,0:T(8,128)(2,1)}, u32[]{:S(2)}, u32[]{:S(2)}) collective-permute-start(bf16[32,1664]{1,0:T(8,128)(2,1)S(1)} %collective-permute-done.7.refs_2_.refs_3_), channel_id=1, source_target_pairs={{12,4},{20,12},{28,20},{24,28},{16,24},{8,16},{0,8},{4,0},{13,5},{... | collective-permute-start | bytes 319496 | tf_op jit(solution)/shard_map/ppermute | solution.py:292
  57.1 44.3 %copy-start.2 = (bf16[32,1664]{1,0:T(8,128)(2,1)}, bf16[32,1664]{1,0:T(8,128)(2,1)S(1)}, u32[]{:S(2)}) copy-start(bf16[32,1664]{1,0:T(8,128)(2,1)S(1)} %collective-permute-done.12.refs_2_.refs_3_) | copy-start | bytes 319492
  58.3 21.2 %collective-permute-start.14 = (bf16[256,1536]{1,0:T(8,128)(2,1)S(1)}, bf16[256,1536]{1,0:T(8,128)(2,1)S(1)}, u32[]{:S(2)}, u32[]{:S(2)}) collective-permute-start(bf16[256,1536]{1,0:T(8,128)(2,1)S(1)} %collective-permute-done.8.refs_0_), channel_id=1, source_target_pairs={{4,12},{12,20},{20,28},{28,24},{24,16},{16,8},{8,0},{0,4},{5,13},{... | collective-permute-start | bytes 2359304 | tf_op jit(solution)/shard_map/ppermute | solution.py:287
  59.8 19.6 %collective-permute-start.15 = (bf16[256,1536]{1,0:T(8,128)(2,1)S(1)}, bf16[256,1536]{1,0:T(8,128)(2,1)S(1)}, u32[]{:S(2)}, u32[]{:S(2)}) collective-permute-start(bf16[256,1536]{1,0:T(8,128)(2,1)S(1)} %collective-permute-done.9.refs_1_), channel_id=1, source_target_pairs={{12,4},{20,12},{28,20},{24,28},{16,24},{8,16},{0,8},{4,0},{13,5},{... | collective-permute-start | bytes 2359304 | tf_op jit(solution)/shard_map/ppermute | solution.py:288
  60.3 2.0 %collective-permute-start.16 = (bf16[32,1664]{1,0:T(8,128)(2,1)S(1)}, bf16[32,1664]{1,0:T(8,128)(2,1)S(1)}, u32[]{:S(2)}, u32[]{:S(2)}) collective-permute-start(bf16[32,1664]{1,0:T(8,128)(2,1)S(1)} %collective-permute-done.7.refs_2_.refs_3_), channel_id=1, source_target_pairs={{0,1},{1,0},{2,3},{3,2},{4,5},{5,4},{6,7},{7,6},{8,9},{9,8},{10,11... | collective-permute-start | bytes 319496 | tf_op jit(solution)/shard_map/ppermute | solution.py:294
  60.3 17.8 %collective-permute-start.17 = (bf16[32,1664]{1,0:T(8,128)(2,1)S(1)}, bf16[32,1664]{1,0:T(8,128)(2,1)S(1)}, u32[]{:S(2)}, u32[]{:S(2)}) collective-permute-start(bf16[32,1664]{1,0:T(8,128)(2,1)S(1)} %collective-permute-done.12.refs_2_.refs_3_), channel_id=1, source_target_pairs={{4,12},{12,20},{20,28},{28,24},{24,16},{16,8},{8,0},{0,4},{5,13},{... | collective-permute-start | bytes 319496 | tf_op jit(solution)/shard_map/ppermute | solution.py:290
  61.9 17.6 %collective-permute-start.18 = (bf16[32,1664]{1,0:T(8,128)(2,1)}, bf16[32,1664]{1,0:T(8,128)(2,1)}, u32[]{:S(2)}, u32[]{:S(2)}) collective-permute-start(bf16[32,1664]{1,0:T(8,128)(2,1)} %collective-permute-done.13.refs_3_.refs_2_), channel_id=1, source_target_pairs={{12,4},{20,12},{28,20},{24,28},{16,24},{8,16},{0,8},{4,0},{13,5},{... | collective-permute-start | bytes 319496 | tf_op jit(solution)/shard_map/ppermute | solution.py:292
  62.3 10.6 %copy-start.4 = (bf16[32,1664]{1,0:T(8,128)(2,1)}, bf16[32,1664]{1,0:T(8,128)(2,1)S(1)}, u32[]{:S(2)}) copy-start(bf16[32,1664]{1,0:T(8,128)(2,1)S(1)} %collective-permute-done.16.refs_4_.refs_5_) | copy-start | bytes 319492
  78.1 23.9 %copy-start.6 = (bf16[32,1664]{1,0:T(8,128)(2,1)}, bf16[32,1664]{1,0:T(8,128)(2,1)S(1)}, u32[]{:S(2)}) copy-start(bf16[32,1664]{1,0:T(8,128)(2,1)S(1)} %collective-permute-done.17.refs_3_.refs_2_) | copy-start | bytes 319492
  79.5 19.7 %collective-permute-start.19 = (bf16[256,1536]{1,0:T(8,128)(2,1)S(1)}, bf16[256,1536]{1,0:T(8,128)(2,1)S(1)}, u32[]{:S(2)}, u32[]{:S(2)}) collective-permute-start(bf16[256,1536]{1,0:T(8,128)(2,1)S(1)} %collective-permute-done.14.refs_1_), channel_id=1, source_target_pairs={{4,12},{12,20},{20,28},{28,24},{24,16},{16,8},{8,0},{0,4},{5,13},{... | collective-permute-start | bytes 2359304 | tf_op jit(solution)/shard_map/ppermute | solution.py:287
  81.0 18.2 %collective-permute-start.20 = (bf16[256,1536]{1,0:T(8,128)(2,1)S(1)}, bf16[256,1536]{1,0:T(8,128)(2,1)S(1)}, u32[]{:S(2)}, u32[]{:S(2)}) collective-permute-start(bf16[256,1536]{1,0:T(8,128)(2,1)S(1)} %collective-permute-done.15.refs_0_), channel_id=1, source_target_pairs={{12,4},{20,12},{28,20},{24,28},{16,24},{8,16},{0,8},{4,0},{13,5},{... | collective-permute-start | bytes 2359304 | tf_op jit(solution)/shard_map/ppermute | solution.py:288
  81.5 2.1 %collective-permute-start.21 = (bf16[32,1664]{1,0:T(8,128)(2,1)S(1)}, bf16[32,1664]{1,0:T(8,128)(2,1)S(1)}, u32[]{:S(2)}, u32[]{:S(2)}) collective-permute-start(bf16[32,1664]{1,0:T(8,128)(2,1)S(1)} %collective-permute-done.12.refs_2_.refs_3_), channel_id=1, source_target_pairs={{0,1},{1,0},{2,3},{3,2},{4,5},{5,4},{6,7},{7,6},{8,9},{9,8},{10,11... | collective-permute-start | bytes 319496 | tf_op jit(solution)/shard_map/ppermute | solution.py:294
  81.5 2.1 %collective-permute-start.22 = (bf16[32,1664]{1,0:T(8,128)(2,1)S(1)}, bf16[32,1664]{1,0:T(8,128)(2,1)S(1)}, u32[]{:S(2)}, u32[]{:S(2)}) collective-permute-start(bf16[32,1664]{1,0:T(8,128)(2,1)S(1)} %collective-permute-done.17.refs_3_.refs_2_), channel_id=1, source_target_pairs={{0,1},{1,0},{2,3},{3,2},{4,5},{5,4},{6,7},{7,6},{8,9},{9,8},{10,11... | collective-permute-start | bytes 319496 | tf_op jit(solution)/shard_map/ppermute | solution.py:294
  82.0 17.2 %collective-permute-start.23 = (bf16[32,1664]{1,0:T(8,128)(2,1)S(1)}, bf16[32,1664]{1,0:T(8,128)(2,1)S(1)}, u32[]{:S(2)}, u32[]{:S(2)}) collective-permute-start(bf16[32,1664]{1,0:T(8,128)(2,1)S(1)} %collective-permute-done.17.refs_3_.refs_2_), channel_id=1, source_target_pairs={{4,12},{12,20},{20,28},{28,24},{24,16},{16,8},{8,0},{0,4},{5,13},{... | collective-permute-start | bytes 319496 | tf_op jit(solution)/shard_map/ppermute | solution.py:290
  83.6 10.6 %copy-start.8 = (bf16[32,1664]{1,0:T(8,128)(2,1)}, bf16[32,1664]{1,0:T(8,128)(2,1)S(1)}, u32[]{:S(2)}) copy-start(bf16[32,1664]{1,0:T(8,128)(2,1)S(1)} %collective-permute-done.21.refs_4_.refs_5_) | copy-start | bytes 319492
  83.6 10.6 %copy-start.10 = (bf16[32,1664]{1,0:T(8,128)(2,1)}, bf16[32,1664]{1,0:T(8,128)(2,1)S(1)}, u32[]{:S(2)}) copy-start(bf16[32,1664]{1,0:T(8,128)(2,1)S(1)} %collective-permute-done.22.refs_5_.refs_4_) | copy-start | bytes 319492
  94.3 7.8 %copy-start.18 = (f32[512,512]{1,0:T(8,128)}, f32[512,512]{1,0:T(8,128)S(1)}, u32[]{:S(2)}) copy-start(f32[512,512]{1,0:T(8,128)S(1)} %form_project.10.refs_7_) | copy-start | bytes 3145732
  99.2 17.2 %collective-permute-start.24 = (bf16[256,1536]{1,0:T(8,128)(2,1)S(1)}, bf16[256,1536]{1,0:T(8,128)(2,1)}, u32[]{:S(2)}, u32[]{:S(2)}) collective-permute-start(bf16[256,1536]{1,0:T(8,128)(2,1)S(1)} %collective-permute-done.19.refs_0_), channel_id=1, source_target_pairs={{4,12},{12,20},{20,28},{28,24},{24,16},{16,8},{8,0},{0,4},{5,13},{... | collective-permute-start | bytes 2359304 | tf_op jit(solution)/shard_map/ppermute | solution.py:287
  100.8 15.6 %collective-permute-start.25 = (bf16[256,1536]{1,0:T(8,128)(2,1)S(1)}, bf16[256,1536]{1,0:T(8,128)(2,1)}, u32[]{:S(2)}, u32[]{:S(2)}) collective-permute-start(bf16[256,1536]{1,0:T(8,128)(2,1)S(1)} %collective-permute-done.20.refs_1_), channel_id=1, source_target_pairs={{12,4},{20,12},{28,20},{24,28},{16,24},{8,16},{0,8},{4,0},{13,5},{... | collective-permute-start | bytes 2359304 | tf_op jit(solution)/shard_map/ppermute | solution.py:288
  102.0 2.7 %collective-permute-start.27 = (bf16[32,1664]{1,0:T(8,128)(2,1)}, bf16[32,1664]{1,0:T(8,128)(2,1)}, u32[]{:S(2)}, u32[]{:S(2)}) collective-permute-start(bf16[32,1664]{1,0:T(8,128)(2,1)} %collective-permute-done.13.refs_3_.refs_2_), channel_id=1, source_target_pairs={{0,1},{1,0},{2,3},{3,2},{4,5},{5,4},{6,7},{7,6},{8,9},{9,8},{10,11... | collective-permute-start | bytes 319496 | tf_op jit(solution)/shard_map/ppermute | solution.py:294
  102.7 2.0 %collective-permute-start.26 = (bf16[32,1664]{1,0:T(8,128)(2,1)}, bf16[32,1664]{1,0:T(8,128)(2,1)}, u32[]{:S(2)}, u32[]{:S(2)}) collective-permute-start(bf16[32,1664]{1,0:T(8,128)(2,1)} %collective-permute-done.18.refs_2_.refs_3_), channel_id=1, source_target_pairs={{0,1},{1,0},{2,3},{3,2},{4,5},{5,4},{6,7},{7,6},{8,9},{9,8},{10,11... | collective-permute-start | bytes 319496 | tf_op jit(solution)/shard_map/ppermute | solution.py:294
  104.7 13.8 %copy-start.13 = (bf16[32,1664]{1,0:T(8,128)(2,1)S(1)}, bf16[32,1664]{1,0:T(8,128)(2,1)}, u32[]{:S(2)}) copy-start(bf16[32,1664]{1,0:T(8,128)(2,1)} %copy-done.12) | copy-start | bytes 319492
  116.4 19.8 %collective-permute-start.28 = (bf16[256,1536]{1,0:T(8,128)(2,1)}, bf16[256,1536]{1,0:T(8,128)(2,1)S(1)}, u32[]{:S(2)}, u32[]{:S(2)}) collective-permute-start(bf16[256,1536]{1,0:T(8,128)(2,1)} %collective-permute-done.24.refs_1_), channel_id=1, source_target_pairs={{4,12},{12,20},{20,28},{28,24},{24,16},{16,8},{8,0},{0,4},{5,13},{... | collective-permute-start | bytes 2359304 | tf_op jit(solution)/shard_map/ppermute | solution.py:287
  118.0 19.5 %collective-permute-start.29 = (bf16[256,1536]{1,0:T(8,128)(2,1)}, bf16[256,1536]{1,0:T(8,128)(2,1)S(1)}, u32[]{:S(2)}, u32[]{:S(2)}) collective-permute-start(bf16[256,1536]{1,0:T(8,128)(2,1)} %collective-permute-done.25.refs_0_), channel_id=1, source_target_pairs={{12,4},{20,12},{28,20},{24,28},{16,24},{8,16},{0,8},{4,0},{13,5},{... | collective-permute-start | bytes 2359304 | tf_op jit(solution)/shard_map/ppermute | solution.py:288
  118.5 1.3 collective-permute-start.30
  119.8 11.9 %copy-start.15 = (bf16[32,1664]{1,0:T(8,128)(2,1)}, bf16[32,1664]{1,0:T(8,128)(2,1)S(1)}, u32[]{:S(2)}) copy-start(bf16[32,1664]{1,0:T(8,128)(2,1)S(1)} %collective-permute-done.30.refs_4_.refs_5_) | copy-start | bytes 319492
  137.5 18.5 %collective-permute-start.31 = (bf16[256,1536]{1,0:T(8,128)(2,1)S(1)}, bf16[256,1536]{1,0:T(8,128)(2,1)}, u32[]{:S(2)}, u32[]{:S(2)}) collective-permute-start(bf16[256,1536]{1,0:T(8,128)(2,1)S(1)} %collective-permute-done.28.refs_0_), channel_id=1, source_target_pairs={{4,12},{12,20},{20,28},{28,24},{24,16},{16,8},{8,0},{0,4},{5,13},{... | collective-permute-start | bytes 2359304 | tf_op jit(solution)/shard_map/ppermute | solution.py:287
  138.5 18.1 %collective-permute-start.32 = (bf16[256,1536]{1,0:T(8,128)(2,1)S(1)}, bf16[256,1536]{1,0:T(8,128)(2,1)S(1)}, u32[]{:S(2)}, u32[]{:S(2)}) collective-permute-start(bf16[256,1536]{1,0:T(8,128)(2,1)S(1)} %collective-permute-done.29.refs_1_), channel_id=1, source_target_pairs={{12,4},{20,12},{28,20},{24,28},{16,24},{8,16},{0,8},{4,0},{13,5},{... | collective-permute-start | bytes 2359304 | tf_op jit(solution)/shard_map/ppermute | solution.py:288
  143.1 13.5 %copy-start.5 = (bf16[32,1664]{1,0:T(8,128)(2,1)S(1)}, bf16[32,1664]{1,0:T(8,128)(2,1)}, u32[]{:S(2)}) copy-start(bf16[32,1664]{1,0:T(8,128)(2,1)} %copy-done.4) | copy-start | bytes 319492
  154.9 11.7 %copy-start.3 = (bf16[32,1664]{1,0:T(8,128)(2,1)S(1)}, bf16[32,1664]{1,0:T(8,128)(2,1)}, u32[]{:S(2)}) copy-start(bf16[32,1664]{1,0:T(8,128)(2,1)} %copy-done.2) | copy-start | bytes 319492
  154.9 11.7 %copy-start.9 = (bf16[32,1664]{1,0:T(8,128)(2,1)S(1)}, bf16[32,1664]{1,0:T(8,128)(2,1)}, u32[]{:S(2)}) copy-start(bf16[32,1664]{1,0:T(8,128)(2,1)} %copy-done.8) | copy-start | bytes 319492
  166.6 8.7 %copy-start.21 = (bf16[32,2048]{1,0:T(8,128)(2,1)S(1)}, bf16[32,2048]{1,0:T(8,128)(2,1)}, u32[]{:S(2)}) copy-start(bf16[32,2048]{1,0:T(8,128)(2,1)} %copy-done.20) | copy-start | bytes 393220
  175.6 21.2 %copy-start.1 = (bf16[64,1024]{1,0:T(8,128)(2,1)S(1)}, bf16[64,1024]{1,0:T(8,128)(2,1)}, u32[]{:S(2)}) copy-start(bf16[64,1024]{1,0:T(8,128)(2,1)} %param.14) | copy-start | bytes 393220
  176.8 2.0 %collective-permute-start.33 = (f32[2,128,512]{2,1,0:T(8,128)S(1)}, f32[2,128,512]{2,1,0:T(8,128)S(1)}, u32[]{:S(2)}, u32[]{:S(2)}) collective-permute-start(f32[2,128,512]{2,1,0:T(8,128)S(1)} %dynamic-slice_bitcast_fusion), channel_id=1, source_target_pairs={{0,1},{1,0},{2,3},{3,2},{4,5},{5,4},{6,7},{7,6},{8,9},{9,8},{10,11... | collective-permute-start | bytes 1572872 | tf_op jit(solution)/shard_map/ppermute | solution.py:193
  179.9 5.6 %collective-permute-start.34 = (bf16[1,128,512]{2,1,0:T(8,128)(2,1)S(1)}, bf16[1,128,512]{2,1,0:T(8,128)(2,1)S(1)}, u32[]{:S(2)}, u32[]{:S(2)}) collective-permute-start(bf16[1,128,512]{2,1,0:T(8,128)(2,1)S(1)} %dynamic-slice_convert_fusion), channel_id=1, source_target_pairs={{0,2},{1,3},{2,0},{3,1},{4,6},{5,7},{6,4},{7,5},{8,10},{9,11},{10,... | collective-permute-start | bytes 393224 | tf_op jit(solution)/shard_map/ppermute | solution.py:193
  (9 other events, 22.1 us)

commit v5 on v4

--- a/solution.py
+++ b/solution.py
@@ -11,7 +11,7 @@
 F32 = jnp.float32
 BF16 = jnp.bfloat16
 LANES = 128
-VMEM_LIMIT = 34 * 1024 * 1024
+VMEM_LIMIT = 31 * 1024 * 1024
 
 
 def ring_order(n):

time: 198 us -> 198 us (level)
  no operation moved by 1% of the time
where the time goes in v5:
time: 198 us; the launch traced here: 197 us
  Pallas kernels  86.8 us (44%)
  waiting for transfers between devices  44.5 us (22%)
  starting transfers between devices  28.3 us (14%)
  matrix products  12.3 us (6%)
  blocking collectives  9.96 us (5%)
  local copies, waits for them, and re-layouts  8.82 us (4%)
  other arithmetic  4.85 us (2%)
    pallas_call x8, Pallas kernels, form_project(): pl.pallas_call(functools.partial(form_project_kernel, dims), out_shape=ja...  86.8 us
    ppermute x4, waiting for transfers between devices, per_device(): halves[s + 1] = lax.ppermute(halves[s], 'dp', ahead)  19.9 us
    ppermute x7, starting transfers between devices, per_device(): low[s + 1] = lax.ppermute(low[s], 'dp', ahead)  11.5 us
    all_to_all x1, blocking collectives, per_device(): got = jnp.sum(lax.all_to_all(sent, 'dp', 0, 0), axis=0)  9.96 us
    ppermute x4, starting transfers between devices, per_device(): halves[s + 1] = lax.ppermute(halves[s], 'dp', ahead)  6.4 us
    ppermute x1, waiting for transfers between devices, exchange_total(): x = x + lax.ppermute(x, axis, [(i, i ^ bit) for i in range(n)])  5.87 us
    dot_general x1, matrix products, per_device(): lax.dot_general(grad_rows.reshape(pool * length, outs), select, (((0,), (...  5.76 us
    ppermute x7, waiting for transfers between devices, per_device(): low[s + 1] = lax.ppermute(low[s], 'dp', ahead)  5.7 us
  transfers between devices with their start and end apart: 33, of which 15 were waited for; matrix products, arithmetic and copies ran while one was open for 7% of the time, Pallas kernels for 35%

profile of v5, /device:TPU:0, one launch (start us, length us, event | category | flops | bytes accessed | tf_op | source)
XLA Modules:
  0.0 196.9 jit_solution(10145395457332704114)
XLA Ops:
  0.0 0.9 copy-done
  0.9 3.6 %fusion.37 = f32[2,32,2048]{2,1,0:T(8,128)S(1)} fusion(bf16[2,32,1024]{2,1,0:T(8,128)(2,1)S(1)} %bitcast.79, bf16[2048,1024,1]{1,0,2:T(8,128)(2,1)} %bitcast.82), kind=kOutput, calls=%fused_computation.79 | convolution fusion | flops 268435456 | bytes 4849664 | tf_op jit(solution)/shard_map/dot_general | solution.py:231
  5.3 5.8 %fusion.12 = bf16[512,1536]{1,0:T(8,128)(2,1)S(1)} fusion(bf16[2048,512]{1,0:T(8,128)(2,1)} %bitcast.83, s32[2048]{0:T(1024)S(1)} %select_n.130), kind=kOutput, calls=%fused_computation.17 | convolution fusion | flops 3225157632 | bytes 3678208 | tf_op jit(solution)/shard_map/dot_general | solution.py:217
  11.2 2.6 %collective-permute-start.2 = (bf16[256,1536]{1,0:T(8,128)(2,1)S(1)}, bf16[256,1536]{1,0:T(8,128)(2,1)}, u32[]{:S(2)}, u32[]{:S(2)}) collective-permute-start(bf16[256,1536]{1,0:T(8,128)(2,1)S(1)} %get-tuple-element.225.refs_0_), channel_id=1, source_target_pairs={{4,12},{12,20},{20,28},{28,24},{24,16},{16,8},{8,0},{0,4},{5,13},{... | collective-permute-start | bytes 2359304 | tf_op jit(solution)/shard_map/ppermute | solution.py:287
  15.2 1.0 bitcast_add_fusion.1
  16.1 1.9 collective-permute-start.5
  18.8 5.9 %collective-permute-done.5 = f32[32,2048]{1,0:T(8,128)S(1)} collective-permute-done((f32[32,2048]{1,0:T(8,128)S(1)}, f32[32,2048]{1,0:T(8,128)S(1)}, u32[]{:S(2)}, u32[]{:S(2)}) %collective-permute-start.5) | collective-permute-done | bytes 262176 | tf_op jit(solution)/shard_map/ppermute | solution.py:200
  24.7 2.5 %fusion.13 = bf16[32,1536]{1,0:T(8,128)(2,1)S(1)} fusion(bf16[32,2048]{1,0:T(8,128)(2,1)S(1)} %multiply_convert_fusion, s32[2048]{0:T(1024)S(1)} %select_n.130), kind=kOutput, calls=%fused_computation.18 | convolution fusion | flops 204521472 | bytes 237568 | tf_op jit(solution)/shard_map/dot_general | solution.py:253
  27.2 1.7 collective-permute-start.6
  29.4 4.9 %collective-permute-done.6.refs_3_.refs_2_ = bf16[32,1664]{1,0:T(8,128)(2,1)S(1)} collective-permute-done((bf16[32,1664]{1,0:T(8,128)(2,1)S(1)}, bf16[32,1664]{1,0:T(8,128)(2,1)S(1)}, u32[]{:S(2)}, u32[]{:S(2)}) %collective-permute-start.6) | collective-permute-done | bytes 106528 | tf_op jit(solution)/shard_map/ppermute | solution.py:290
  34.3 1.4 collective-permute-done.7.refs_2_.refs_3_
  35.7 1.6 collective-permute-start.8
  38.3 1.6 collective-permute-start.12
  40.4 11.7 %form_project.8.refs_7_ = f32[512,512]{1,0:T(8,128)S(1)} custom-call(s32[10]{0:T(128)S(1)} %pad_add_fusion.blocks_ref, bf16[256,1536]{1,0:T(8,128)(2,1)S(1)} %get-tuple-element.225.refs_0_, bf16[256,1536]{1,0:T(8,128)(2,1)} %collective-permute-done.2.refs_1_, bf16[32,1664]{1,0:T(8,128)(2,1)S(1)} %pad_maximum_fusion.refs_2_.refs_3_, ...), custom_call_target="tpu_custom_call", output_to_operand_aliasing={{}: (8, {})} | custom-call | flops 2147483648 | bytes 16777216 | tf_op jit(solution)/shard_map/form_project/pallas_call | solution.py:166
  52.1 4.9 %collective-permute-done.12.refs_2_.refs_3_ = bf16[32,1664]{1,0:T(8,128)(2,1)S(1)} collective-permute-done((bf16[32,1664]{1,0:T(8,128)(2,1)S(1)}, bf16[32,1664]{1,0:T(8,128)(2,1)S(1)}, u32[]{:S(2)}, u32[]{:S(2)}) %collective-permute-start.12) | collective-permute-done | bytes 106528 | tf_op jit(solution)/shard_map/ppermute | solution.py:290
  57.1 1.2 collective-permute-done.13.refs_3_.refs_2_
  58.3 1.6 collective-permute-start.14
  60.3 1.6 collective-permute-start.17
  62.3 10.6 %form_project.9.refs_7_ = f32[512,512]{1,0:T(8,128)S(1)} custom-call(s32[10]{0:T(128)S(1)} %pad_add_fusion.blocks_ref, bf16[256,1536]{1,0:T(8,128)(2,1)S(1)} %collective-permute-done.3.refs_0_, bf16[256,1536]{1,0:T(8,128)(2,1)S(1)} %get-tuple-element.224.refs_1_, ...), custom_call_target="tpu_custom_call", output_to_operand_aliasing={{}: (8, {})} | custom-call | flops 2147483648 | bytes 16777216 | tf_op jit(solution)/shard_map/form_project/pallas_call | solution.py:166
  72.9 5.1 %collective-permute-done.17.refs_3_.refs_2_ = bf16[32,1664]{1,0:T(8,128)(2,1)S(1)} collective-permute-done((bf16[32,1664]{1,0:T(8,128)(2,1)S(1)}, bf16[32,1664]{1,0:T(8,128)(2,1)S(1)}, u32[]{:S(2)}, u32[]{:S(2)}) %collective-permute-start.17) | collective-permute-done | bytes 106528 | tf_op jit(solution)/shard_map/ppermute | solution.py:290
  78.1 1.4 collective-permute-done.18.refs_2_.refs_3_
  79.5 1.6 collective-permute-start.19
  82.0 1.6 collective-permute-start.23
  83.6 10.6 %form_project.10.refs_7_ = f32[512,512]{1,0:T(8,128)S(1)} custom-call(s32[10]{0:T(128)S(1)} %pad_add_fusion.blocks_ref, bf16[256,1536]{1,0:T(8,128)(2,1)S(1)} %collective-permute-done.8.refs_0_, bf16[256,1536]{1,0:T(8,128)(2,1)S(1)} %collective-permute-done.14.refs_1_, ...), custom_call_target="tpu_custom_call", output_to_operand_aliasing={{}: (8, {})} | custom-call | flops 2147483648 | bytes 16777216 | tf_op jit(solution)/shard_map/form_project/pallas_call | solution.py:166
  94.3 5.0 %collective-permute-done.23.refs_2_.refs_3_ = bf16[32,1664]{1,0:T(8,128)(2,1)S(1)} collective-permute-done((bf16[32,1664]{1,0:T(8,128)(2,1)S(1)}, bf16[32,1664]{1,0:T(8,128)(2,1)S(1)}, u32[]{:S(2)}, u32[]{:S(2)}) %collective-permute-start.23) | collective-permute-done | bytes 106528 | tf_op jit(solution)/shard_map/ppermute | solution.py:290
  99.3 1.6 collective-permute-start.24
  104.7 11.7 %form_project.11.refs_7_ = f32[512,512]{1,0:T(8,128)} custom-call(s32[10]{0:T(128)S(1)} %pad_add_fusion.blocks_ref, bf16[256,1536]{1,0:T(8,128)(2,1)S(1)} %collective-permute-done.15.refs_0_, bf16[256,1536]{1,0:T(8,128)(2,1)S(1)} %collective-permute-done.9.refs_1_, ...), custom_call_target="tpu_custom_call", output_to_operand_aliasing={{}: (8, {})} | custom-call | flops 2147483648 | bytes 16777216 | tf_op jit(solution)/shard_map/form_project/pallas_call | solution.py:166
  116.4 1.6 collective-permute-start.28
  118.5 1.3 collective-permute-done.30.refs_4_.refs_5_
  119.8 11.8 %form_project.12.refs_7_ = f32[512,512]{1,0:T(8,128)} custom-call(s32[10]{0:T(128)S(1)} %pad_add_fusion.blocks_ref, bf16[256,1536]{1,0:T(8,128)(2,1)S(1)} %collective-permute-done.19.refs_0_, bf16[256,1536]{1,0:T(8,128)(2,1)} %collective-permute-done.24.refs_1_, bf16[32,1664]{1,0:T(8,128)(2,1)S(1)} %copy-done.13, ...), custom_call_target="tpu_custom_call", output_to_operand_aliasing={{}: (8, {})} | custom-call | flops 2147483648 | bytes 16777216 | tf_op jit(solution)/shard_map/form_project/pallas_call | solution.py:166
  131.7 4.6 %collective-permute-done.28.refs_0_ = bf16[256,1536]{1,0:T(8,128)(2,1)S(1)} collective-permute-done((bf16[256,1536]{1,0:T(8,128)(2,1)}, bf16[256,1536]{1,0:T(8,128)(2,1)S(1)}, u32[]{:S(2)}, u32[]{:S(2)}) %collective-permute-start.28) | collective-permute-done | bytes 786464 | tf_op jit(solution)/shard_map/ppermute | solution.py:287
  136.3 1.3 collective-permute-done.29.refs_1_
  137.5 1.0 collective-permute-start.31
  138.6 1.0 collective-permute-start.32
  139.6 0.9 copy-done.7
  140.4 0.9 copy-done.11
  141.3 0.9 copy-done.14
  142.2 0.9 copy-done.16
  143.1 11.8 %form_project.13.refs_7_ = f32[512,512]{1,0:T(8,128)} custom-call(s32[10]{0:T(128)S(1)} %pad_add_fusion.blocks_ref, bf16[256,1536]{1,0:T(8,128)(2,1)} %collective-permute-done.25.refs_0_, bf16[256,1536]{1,0:T(8,128)(2,1)S(1)} %collective-permute-done.20.refs_1_, bf16[32,1664]{1,0:T(8,128)(2,1)S(1)} %copy-done.7, ...), custom_call_target="tpu_custom_call", output_to_operand_aliasing={{}: (8, {})} | custom-call | flops 2147483648 | bytes 16777216 | tf_op jit(solution)/shard_map/form_project/pallas_call | solution.py:166
  154.9 1.1 collective-permute-done.31.refs_1_
  156.7 9.9 %form_project.14.refs_7_ = f32[512,512]{1,0:T(8,128)} custom-call(s32[10]{0:T(128)S(1)} %pad_add_fusion.blocks_ref, bf16[256,1536]{1,0:T(8,128)(2,1)S(1)} %collective-permute-done.28.refs_0_, bf16[256,1536]{1,0:T(8,128)(2,1)} %collective-permute-done.31.refs_1_, ...), custom_call_target="tpu_custom_call", output_to_operand_aliasing={{}: (8, {})} | custom-call | flops 2147483648 | bytes 16777216 | tf_op jit(solution)/shard_map/form_project/pallas_call | solution.py:166
  166.6 8.7 %form_project.15 = f32[512,512]{1,0:T(8,128)} custom-call(s32[10]{0:T(128)S(1)} %pad_add_fusion.blocks_ref, bf16[256,1536]{1,0:T(8,128)(2,1)S(1)} %collective-permute-done.32.refs_0_, bf16[256,1536]{1,0:T(8,128)(2,1)S(1)} %collective-permute-done.29.refs_1_, ...), custom_call_target="tpu_custom_call", output_to_operand_aliasing={{}: (8, {})} | custom-call | flops 2147483648 | bytes 16777216 | tf_op jit(solution)/shard_map/form_project/pallas_call | solution.py:166
  175.6 1.1 dynamic-slice_bitcast_fusion
  176.9 1.9 collective-permute-done.33
  178.7 1.1 bitcast_add_fusion
  179.9 1.6 collective-permute-start.34
  181.7 3.8 %collective-permute-done.34 = bf16[1,128,512]{2,1,0:T(8,128)(2,1)S(1)} collective-permute-done((bf16[1,128,512]{2,1,0:T(8,128)(2,1)S(1)}, bf16[1,128,512]{2,1,0:T(8,128)(2,1)S(1)}, u32[]{:S(2)}, u32[]{:S(2)}) %collective-permute-start.34) | collective-permute-done | bytes 131104 | tf_op jit(solution)/shard_map/ppermute | solution.py:193
  186.2 10.0 %all_to_all.5 = f32[8,34,128]{2,1,0:T(8,128)S(1)} all-to-all(f32[8,34,128]{2,1,0:T(8,128)S(1)} %select_maximum_fusion), channel_id=1, replica_groups=mesh['dp'=8,'fsdp'=4] {'dp'}, dimensions={0} | all-to-all | bytes 278528 | tf_op jit(solution)/shard_map/all_to_all | solution.py:339
  (121 shorter events, 13.2 us)
Async XLA Ops:
  4.5 10.6 %collective-permute-start.4 = (f32[32,2048]{1,0:T(8,128)S(1)}, f32[32,2048]{1,0:T(8,128)}, u32[]{:S(2)}, u32[]{:S(2)}) collective-permute-start(f32[32,2048]{1,0:T(8,128)S(1)} %dynamic-slice_bitcast_fusion.1), channel_id=1, source_target_pairs={{0,1},{1,0},{2,3},{3,2},{4,5},{5,4},{6,7},{7,6},{8,9},{9,8},{10,11... | collective-permute-start | bytes 786440 | tf_op jit(solution)/shard_map/ppermute | solution.py:239
  5.3 8.6 %copy-start.23 = (s32[8]{0:T(128)S(1)}, s32[8]{0:T(128)}, u32[]{:S(2)}) copy-start(s32[8]{0:T(128)} %constant.174.clone) | copy-start | bytes 100
  11.1 7.0 %copy-start.17 = (s32[8]{0:T(128)S(1)}, s32[8]{0:T(128)}, u32[]{:S(2)}) copy-start(s32[8]{0:T(128)} %constant.175.clone) | copy-start | bytes 100
  11.2 24.5 %collective-permute-start.2 = (bf16[256,1536]{1,0:T(8,128)(2,1)S(1)}, bf16[256,1536]{1,0:T(8,128)(2,1)}, u32[]{:S(2)}, u32[]{:S(2)}) collective-permute-start(bf16[256,1536]{1,0:T(8,128)(2,1)S(1)} %get-tuple-element.225.refs_0_), channel_id=1, source_target_pairs={{4,12},{12,20},{20,28},{28,24},{24,16},{16,8},{8,0},{0,4},{5,13},{... | collective-permute-start | bytes 2359304 | tf_op jit(solution)/shard_map/ppermute | solution.py:287
  13.8 21.9 %collective-permute-start.3 = (bf16[256,1536]{1,0:T(8,128)(2,1)S(1)}, bf16[256,1536]{1,0:T(8,128)(2,1)S(1)}, u32[]{:S(2)}, u32[]{:S(2)}) collective-permute-start(bf16[256,1536]{1,0:T(8,128)(2,1)S(1)} %get-tuple-element.224.refs_1_), channel_id=1, source_target_pairs={{12,4},{20,12},{28,20},{24,28},{16,24},{8,16},{0,8},{4,0},{13,5},{... | collective-permute-start | bytes 2359304 | tf_op jit(solution)/shard_map/ppermute | solution.py:288
  16.1 8.5 %collective-permute-start.5 = (f32[32,2048]{1,0:T(8,128)S(1)}, f32[32,2048]{1,0:T(8,128)S(1)}, u32[]{:S(2)}, u32[]{:S(2)}) collective-permute-start(f32[32,2048]{1,0:T(8,128)S(1)} %bitcast_add_fusion.1), channel_id=1, source_target_pairs={{0,2},{1,3},{2,0},{3,1},{4,6},{5,7},{6,4},{7,5},{8,10},{9,11},{10,... | collective-permute-start | bytes 786440 | tf_op jit(solution)/shard_map/ppermute | solution.py:200
  27.2 7.1 %collective-permute-start.6 = (bf16[32,1664]{1,0:T(8,128)(2,1)S(1)}, bf16[32,1664]{1,0:T(8,128)(2,1)S(1)}, u32[]{:S(2)}, u32[]{:S(2)}) collective-permute-start(bf16[32,1664]{1,0:T(8,128)(2,1)S(1)} %pad_maximum_fusion.refs_2_.refs_3_), channel_id=1, source_target_pairs={{4,12},{12,20},{20,28},{28,24},{24,16},{16,8},{8,0},{0,4},{5,13},{... | collective-permute-start | bytes 319496 | tf_op jit(solution)/shard_map/ppermute | solution.py:290
  28.9 6.8 %collective-permute-start.7 = (bf16[32,1664]{1,0:T(8,128)(2,1)S(1)}, bf16[32,1664]{1,0:T(8,128)(2,1)S(1)}, u32[]{:S(2)}, u32[]{:S(2)}) collective-permute-start(bf16[32,1664]{1,0:T(8,128)(2,1)S(1)} %pad_maximum_fusion.refs_2_.refs_3_), channel_id=1, source_target_pairs={{12,4},{20,12},{28,20},{24,28},{16,24},{8,16},{0,8},{4,0},{13,5},{... | collective-permute-start | bytes 319496 | tf_op jit(solution)/shard_map/ppermute | solution.py:292
  35.7 22.5 %collective-permute-start.8 = (bf16[256,1536]{1,0:T(8,128)(2,1)}, bf16[256,1536]{1,0:T(8,128)(2,1)S(1)}, u32[]{:S(2)}, u32[]{:S(2)}) collective-permute-start(bf16[256,1536]{1,0:T(8,128)(2,1)} %collective-permute-done.2.refs_1_), channel_id=1, source_target_pairs={{4,12},{12,20},{20,28},{28,24},{24,16},{16,8},{8,0},{0,4},{5,13},{... | collective-permute-start | bytes 2359304 | tf_op jit(solution)/shard_map/ppermute | solution.py:287
  37.3 20.9 %collective-permute-start.9 = (bf16[256,1536]{1,0:T(8,128)(2,1)S(1)}, bf16[256,1536]{1,0:T(8,128)(2,1)S(1)}, u32[]{:S(2)}, u32[]{:S(2)}) collective-permute-start(bf16[256,1536]{1,0:T(8,128)(2,1)S(1)} %collective-permute-done.3.refs_0_), channel_id=1, source_target_pairs={{12,4},{20,12},{28,20},{24,28},{16,24},{8,16},{0,8},{4,0},{13,5},{... | collective-permute-start | bytes 2359304 | tf_op jit(solution)/shard_map/ppermute | solution.py:288
  37.8 2.1 %collective-permute-start.10 = (bf16[32,1664]{1,0:T(8,128)(2,1)S(1)}, bf16[32,1664]{1,0:T(8,128)(2,1)S(1)}, u32[]{:S(2)}, u32[]{:S(2)}) collective-permute-start(bf16[32,1664]{1,0:T(8,128)(2,1)S(1)} %pad_maximum_fusion.refs_2_.refs_3_), channel_id=1, source_target_pairs={{0,1},{1,0},{2,3},{3,2},{4,5},{5,4},{6,7},{7,6},{8,9},{9,8},{10,11... | collective-permute-start | bytes 319496 | tf_op jit(solution)/shard_map/ppermute | solution.py:294
  37.8 2.5 %collective-permute-start.11 = (bf16[32,1664]{1,0:T(8,128)(2,1)S(1)}, bf16[32,1664]{1,0:T(8,128)(2,1)S(1)}, u32[]{:S(2)}, u32[]{:S(2)}) collective-permute-start(bf16[32,1664]{1,0:T(8,128)(2,1)S(1)} %collective-permute-done.6.refs_3_.refs_2_), channel_id=1, source_target_pairs={{0,1},{1,0},{2,3},{3,2},{4,5},{5,4},{6,7},{7,6},{8,9},{9,8},{10,11... | collective-permute-start | bytes 319496 | tf_op jit(solution)/shard_map/ppermute | solution.py:294
  38.3 18.8 %collective-permute-start.12 = (bf16[32,1664]{1,0:T(8,128)(2,1)S(1)}, bf16[32,1664]{1,0:T(8,128)(2,1)S(1)}, u32[]{:S(2)}, u32[]{:S(2)}) collective-permute-start(bf16[32,1664]{1,0:T(8,128)(2,1)S(1)} %collective-permute-done.6.refs_3_.refs_2_), channel_id=1, source_target_pairs={{4,12},{12,20},{20,28},{28,24},{24,16},{16,8},{8,0},{0,4},{5,13},{... | collective-permute-start | bytes 319496 | tf_op jit(solution)/shard_map/ppermute | solution.py:290
  39.9 18.4 %collective-permute-start.13 = (bf16[32,1664]{1,0:T(8,128)(2,1)S(1)}, bf16[32,1664]{1,0:T(8,128)(2,1)}, u32[]{:S(2)}, u32[]{:S(2)}) collective-permute-start(bf16[32,1664]{1,0:T(8,128)(2,1)S(1)} %collective-permute-done.7.refs_2_.refs_3_), channel_id=1, source_target_pairs={{12,4},{20,12},{28,20},{24,28},{16,24},{8,16},{0,8},{4,0},{13,5},{... | collective-permute-start | bytes 319496 | tf_op jit(solution)/shard_map/ppermute | solution.py:292
  57.1 44.3 %copy-start.2 = (bf16[32,1664]{1,0:T(8,128)(2,1)}, bf16[32,1664]{1,0:T(8,128)(2,1)S(1)}, u32[]{:S(2)}) copy-start(bf16[32,1664]{1,0:T(8,128)(2,1)S(1)} %collective-permute-done.12.refs_2_.refs_3_) | copy-start | bytes 319492
  58.3 21.2 %collective-permute-start.14 = (bf16[256,1536]{1,0:T(8,128)(2,1)S(1)}, bf16[256,1536]{1,0:T(8,128)(2,1)S(1)}, u32[]{:S(2)}, u32[]{:S(2)}) collective-permute-start(bf16[256,1536]{1,0:T(8,128)(2,1)S(1)} %collective-permute-done.8.refs_0_), channel_id=1, source_target_pairs={{4,12},{12,20},{20,28},{28,24},{24,16},{16,8},{8,0},{0,4},{5,13},{... | collective-permute-start | bytes 2359304 | tf_op jit(solution)/shard_map/ppermute | solution.py:287
  59.8 19.6 %collective-permute-start.15 = (bf16[256,1536]{1,0:T(8,128)(2,1)S(1)}, bf16[256,1536]{1,0:T(8,128)(2,1)S(1)}, u32[]{:S(2)}, u32[]{:S(2)}) collective-permute-start(bf16[256,1536]{1,0:T(8,128)(2,1)S(1)} %collective-permute-done.9.refs_1_), channel_id=1, source_target_pairs={{12,4},{20,12},{28,20},{24,28},{16,24},{8,16},{0,8},{4,0},{13,5},{... | collective-permute-start | bytes 2359304 | tf_op jit(solution)/shard_map/ppermute | solution.py:288
  60.3 2.0 %collective-permute-start.16 = (bf16[32,1664]{1,0:T(8,128)(2,1)S(1)}, bf16[32,1664]{1,0:T(8,128)(2,1)S(1)}, u32[]{:S(2)}, u32[]{:S(2)}) collective-permute-start(bf16[32,1664]{1,0:T(8,128)(2,1)S(1)} %collective-permute-done.7.refs_2_.refs_3_), channel_id=1, source_target_pairs={{0,1},{1,0},{2,3},{3,2},{4,5},{5,4},{6,7},{7,6},{8,9},{9,8},{10,11... | collective-permute-start | bytes 319496 | tf_op jit(solution)/shard_map/ppermute | solution.py:294
  60.3 17.8 %collective-permute-start.17 = (bf16[32,1664]{1,0:T(8,128)(2,1)S(1)}, bf16[32,1664]{1,0:T(8,128)(2,1)S(1)}, u32[]{:S(2)}, u32[]{:S(2)}) collective-permute-start(bf16[32,1664]{1,0:T(8,128)(2,1)S(1)} %collective-permute-done.12.refs_2_.refs_3_), channel_id=1, source_target_pairs={{4,12},{12,20},{20,28},{28,24},{24,16},{16,8},{8,0},{0,4},{5,13},{... | collective-permute-start | bytes 319496 | tf_op jit(solution)/shard_map/ppermute | solution.py:290
  61.9 17.6 %collective-permute-start.18 = (bf16[32,1664]{1,0:T(8,128)(2,1)}, bf16[32,1664]{1,0:T(8,128)(2,1)}, u32[]{:S(2)}, u32[]{:S(2)}) collective-permute-start(bf16[32,1664]{1,0:T(8,128)(2,1)} %collective-permute-done.13.refs_3_.refs_2_), channel_id=1, source_target_pairs={{12,4},{20,12},{28,20},{24,28},{16,24},{8,16},{0,8},{4,0},{13,5},{... | collective-permute-start | bytes 319496 | tf_op jit(solution)/shard_map/ppermute | solution.py:292
  62.3 10.6 %copy-start.4 = (bf16[32,1664]{1,0:T(8,128)(2,1)}, bf16[32,1664]{1,0:T(8,128)(2,1)S(1)}, u32[]{:S(2)}) copy-start(bf16[32,1664]{1,0:T(8,128)(2,1)S(1)} %collective-permute-done.16.refs_4_.refs_5_) | copy-start | bytes 319492
  78.1 24.0 %copy-start.6 = (bf16[32,1664]{1,0:T(8,128)(2,1)}, bf16[32,1664]{1,0:T(8,128)(2,1)S(1)}, u32[]{:S(2)}) copy-start(bf16[32,1664]{1,0:T(8,128)(2,1)S(1)} %collective-permute-done.17.refs_3_.refs_2_) | copy-start | bytes 319492
  79.5 19.8 %collective-permute-start.19 = (bf16[256,1536]{1,0:T(8,128)(2,1)S(1)}, bf16[256,1536]{1,0:T(8,128)(2,1)S(1)}, u32[]{:S(2)}, u32[]{:S(2)}) collective-permute-start(bf16[256,1536]{1,0:T(8,128)(2,1)S(1)} %collective-permute-done.14.refs_1_), channel_id=1, source_target_pairs={{4,12},{12,20},{20,28},{28,24},{24,16},{16,8},{8,0},{0,4},{5,13},{... | collective-permute-start | bytes 2359304 | tf_op jit(solution)/shard_map/ppermute | solution.py:287
  81.0 18.2 %collective-permute-start.20 = (bf16[256,1536]{1,0:T(8,128)(2,1)S(1)}, bf16[256,1536]{1,0:T(8,128)(2,1)S(1)}, u32[]{:S(2)}, u32[]{:S(2)}) collective-permute-start(bf16[256,1536]{1,0:T(8,128)(2,1)S(1)} %collective-permute-done.15.refs_0_), channel_id=1, source_target_pairs={{12,4},{20,12},{28,20},{24,28},{16,24},{8,16},{0,8},{4,0},{13,5},{... | collective-permute-start | bytes 2359304 | tf_op jit(solution)/shard_map/ppermute | solution.py:288
  81.5 2.1 %collective-permute-start.21 = (bf16[32,1664]{1,0:T(8,128)(2,1)S(1)}, bf16[32,1664]{1,0:T(8,128)(2,1)S(1)}, u32[]{:S(2)}, u32[]{:S(2)}) collective-permute-start(bf16[32,1664]{1,0:T(8,128)(2,1)S(1)} %collective-permute-done.12.refs_2_.refs_3_), channel_id=1, source_target_pairs={{0,1},{1,0},{2,3},{3,2},{4,5},{5,4},{6,7},{7,6},{8,9},{9,8},{10,11... | collective-permute-start | bytes 319496 | tf_op jit(solution)/shard_map/ppermute | solution.py:294
  81.5 2.1 %collective-permute-start.22 = (bf16[32,1664]{1,0:T(8,128)(2,1)S(1)}, bf16[32,1664]{1,0:T(8,128)(2,1)S(1)}, u32[]{:S(2)}, u32[]{:S(2)}) collective-permute-start(bf16[32,1664]{1,0:T(8,128)(2,1)S(1)} %collective-permute-done.17.refs_3_.refs_2_), channel_id=1, source_target_pairs={{0,1},{1,0},{2,3},{3,2},{4,5},{5,4},{6,7},{7,6},{8,9},{9,8},{10,11... | collective-permute-start | bytes 319496 | tf_op jit(solution)/shard_map/ppermute | solution.py:294
  82.0 17.2 %collective-permute-start.23 = (bf16[32,1664]{1,0:T(8,128)(2,1)S(1)}, bf16[32,1664]{1,0:T(8,128)(2,1)S(1)}, u32[]{:S(2)}, u32[]{:S(2)}) collective-permute-start(bf16[32,1664]{1,0:T(8,128)(2,1)S(1)} %collective-permute-done.17.refs_3_.refs_2_), channel_id=1, source_target_pairs={{4,12},{12,20},{20,28},{28,24},{24,16},{16,8},{8,0},{0,4},{5,13},{... | collective-permute-start | bytes 319496 | tf_op jit(solution)/shard_map/ppermute | solution.py:290
  83.6 10.6 %copy-start.8 = (bf16[32,1664]{1,0:T(8,128)(2,1)}, bf16[32,1664]{1,0:T(8,128)(2,1)S(1)}, u32[]{:S(2)}) copy-start(bf16[32,1664]{1,0:T(8,128)(2,1)S(1)} %collective-permute-done.21.refs_4_.refs_5_) | copy-start | bytes 319492
  83.6 10.6 %copy-start.10 = (bf16[32,1664]{1,0:T(8,128)(2,1)}, bf16[32,1664]{1,0:T(8,128)(2,1)S(1)}, u32[]{:S(2)}) copy-start(bf16[32,1664]{1,0:T(8,128)(2,1)S(1)} %collective-permute-done.22.refs_5_.refs_4_) | copy-start | bytes 319492
  94.2 7.8 %copy-start.18 = (f32[512,512]{1,0:T(8,128)}, f32[512,512]{1,0:T(8,128)S(1)}, u32[]{:S(2)}) copy-start(f32[512,512]{1,0:T(8,128)S(1)} %form_project.10.refs_7_) | copy-start | bytes 3145732
  99.3 17.2 %collective-permute-start.24 = (bf16[256,1536]{1,0:T(8,128)(2,1)S(1)}, bf16[256,1536]{1,0:T(8,128)(2,1)}, u32[]{:S(2)}, u32[]{:S(2)}) collective-permute-start(bf16[256,1536]{1,0:T(8,128)(2,1)S(1)} %collective-permute-done.19.refs_0_), channel_id=1, source_target_pairs={{4,12},{12,20},{20,28},{28,24},{24,16},{16,8},{8,0},{0,4},{5,13},{... | collective-permute-start | bytes 2359304 | tf_op jit(solution)/shard_map/ppermute | solution.py:287
  100.8 15.6 %collective-permute-start.25 = (bf16[256,1536]{1,0:T(8,128)(2,1)S(1)}, bf16[256,1536]{1,0:T(8,128)(2,1)}, u32[]{:S(2)}, u32[]{:S(2)}) collective-permute-start(bf16[256,1536]{1,0:T(8,128)(2,1)S(1)} %collective-permute-done.20.refs_1_), channel_id=1, source_target_pairs={{12,4},{20,12},{28,20},{24,28},{16,24},{8,16},{0,8},{4,0},{13,5},{... | collective-permute-start | bytes 2359304 | tf_op jit(solution)/shard_map/ppermute | solution.py:288
  102.0 2.7 %collective-permute-start.27 = (bf16[32,1664]{1,0:T(8,128)(2,1)}, bf16[32,1664]{1,0:T(8,128)(2,1)}, u32[]{:S(2)}, u32[]{:S(2)}) collective-permute-start(bf16[32,1664]{1,0:T(8,128)(2,1)} %collective-permute-done.13.refs_3_.refs_2_), channel_id=1, source_target_pairs={{0,1},{1,0},{2,3},{3,2},{4,5},{5,4},{6,7},{7,6},{8,9},{9,8},{10,11... | collective-permute-start | bytes 319496 | tf_op jit(solution)/shard_map/ppermute | solution.py:294
  102.7 2.0 %collective-permute-start.26 = (bf16[32,1664]{1,0:T(8,128)(2,1)}, bf16[32,1664]{1,0:T(8,128)(2,1)}, u32[]{:S(2)}, u32[]{:S(2)}) collective-permute-start(bf16[32,1664]{1,0:T(8,128)(2,1)} %collective-permute-done.18.refs_2_.refs_3_), channel_id=1, source_target_pairs={{0,1},{1,0},{2,3},{3,2},{4,5},{5,4},{6,7},{7,6},{8,9},{9,8},{10,11... | collective-permute-start | bytes 319496 | tf_op jit(solution)/shard_map/ppermute | solution.py:294
  104.7 13.8 %copy-start.13 = (bf16[32,1664]{1,0:T(8,128)(2,1)S(1)}, bf16[32,1664]{1,0:T(8,128)(2,1)}, u32[]{:S(2)}) copy-start(bf16[32,1664]{1,0:T(8,128)(2,1)} %copy-done.12) | copy-start | bytes 319492
  116.4 19.8 %collective-permute-start.28 = (bf16[256,1536]{1,0:T(8,128)(2,1)}, bf16[256,1536]{1,0:T(8,128)(2,1)S(1)}, u32[]{:S(2)}, u32[]{:S(2)}) collective-permute-start(bf16[256,1536]{1,0:T(8,128)(2,1)} %collective-permute-done.24.refs_1_), channel_id=1, source_target_pairs={{4,12},{12,20},{20,28},{28,24},{24,16},{16,8},{8,0},{0,4},{5,13},{... | collective-permute-start | bytes 2359304 | tf_op jit(solution)/shard_map/ppermute | solution.py:287
  118.0 19.5 %collective-permute-start.29 = (bf16[256,1536]{1,0:T(8,128)(2,1)}, bf16[256,1536]{1,0:T(8,128)(2,1)S(1)}, u32[]{:S(2)}, u32[]{:S(2)}) collective-permute-start(bf16[256,1536]{1,0:T(8,128)(2,1)} %collective-permute-done.25.refs_0_), channel_id=1, source_target_pairs={{12,4},{20,12},{28,20},{24,28},{16,24},{8,16},{0,8},{4,0},{13,5},{... | collective-permute-start | bytes 2359304 | tf_op jit(solution)/shard_map/ppermute | solution.py:288
  118.5 1.3 collective-permute-start.30
  119.8 11.8 %copy-start.15 = (bf16[32,1664]{1,0:T(8,128)(2,1)}, bf16[32,1664]{1,0:T(8,128)(2,1)S(1)}, u32[]{:S(2)}) copy-start(bf16[32,1664]{1,0:T(8,128)(2,1)S(1)} %collective-permute-done.30.refs_4_.refs_5_) | copy-start | bytes 319492
  137.5 18.5 %collective-permute-start.31 = (bf16[256,1536]{1,0:T(8,128)(2,1)S(1)}, bf16[256,1536]{1,0:T(8,128)(2,1)}, u32[]{:S(2)}, u32[]{:S(2)}) collective-permute-start(bf16[256,1536]{1,0:T(8,128)(2,1)S(1)} %collective-permute-done.28.refs_0_), channel_id=1, source_target_pairs={{4,12},{12,20},{20,28},{28,24},{24,16},{16,8},{8,0},{0,4},{5,13},{... | collective-permute-start | bytes 2359304 | tf_op jit(solution)/shard_map/ppermute | solution.py:287
  138.6 18.1 %collective-permute-start.32 = (bf16[256,1536]{1,0:T(8,128)(2,1)S(1)}, bf16[256,1536]{1,0:T(8,128)(2,1)S(1)}, u32[]{:S(2)}, u32[]{:S(2)}) collective-permute-start(bf16[256,1536]{1,0:T(8,128)(2,1)S(1)} %collective-permute-done.29.refs_1_), channel_id=1, source_target_pairs={{12,4},{20,12},{28,20},{24,28},{16,24},{8,16},{0,8},{4,0},{13,5},{... | collective-permute-start | bytes 2359304 | tf_op jit(solution)/shard_map/ppermute | solution.py:288
  143.1 13.5 %copy-start.5 = (bf16[32,1664]{1,0:T(8,128)(2,1)S(1)}, bf16[32,1664]{1,0:T(8,128)(2,1)}, u32[]{:S(2)}) copy-start(bf16[32,1664]{1,0:T(8,128)(2,1)} %copy-done.4) | copy-start | bytes 319492
  154.9 11.7 %copy-start.3 = (bf16[32,1664]{1,0:T(8,128)(2,1)S(1)}, bf16[32,1664]{1,0:T(8,128)(2,1)}, u32[]{:S(2)}) copy-start(bf16[32,1664]{1,0:T(8,128)(2,1)} %copy-done.2) | copy-start | bytes 319492
  154.9 11.7 %copy-start.9 = (bf16[32,1664]{1,0:T(8,128)(2,1)S(1)}, bf16[32,1664]{1,0:T(8,128)(2,1)}, u32[]{:S(2)}) copy-start(bf16[32,1664]{1,0:T(8,128)(2,1)} %copy-done.8) | copy-start | bytes 319492
  166.6 8.7 %copy-start.21 = (bf16[32,2048]{1,0:T(8,128)(2,1)S(1)}, bf16[32,2048]{1,0:T(8,128)(2,1)}, u32[]{:S(2)}) copy-start(bf16[32,2048]{1,0:T(8,128)(2,1)} %copy-done.20) | copy-start | bytes 393220
  175.6 21.2 %copy-start.1 = (bf16[64,1024]{1,0:T(8,128)(2,1)S(1)}, bf16[64,1024]{1,0:T(8,128)(2,1)}, u32[]{:S(2)}) copy-start(bf16[64,1024]{1,0:T(8,128)(2,1)} %param.14) | copy-start | bytes 393220
  176.8 2.0 %collective-permute-start.33 = (f32[2,128,512]{2,1,0:T(8,128)S(1)}, f32[2,128,512]{2,1,0:T(8,128)S(1)}, u32[]{:S(2)}, u32[]{:S(2)}) collective-permute-start(f32[2,128,512]{2,1,0:T(8,128)S(1)} %dynamic-slice_bitcast_fusion), channel_id=1, source_target_pairs={{0,1},{1,0},{2,3},{3,2},{4,5},{5,4},{6,7},{7,6},{8,9},{9,8},{10,11... | collective-permute-start | bytes 1572872 | tf_op jit(solution)/shard_map/ppermute | solution.py:193
  179.9 5.6 %collective-permute-start.34 = (bf16[1,128,512]{2,1,0:T(8,128)(2,1)S(1)}, bf16[1,128,512]{2,1,0:T(8,128)(2,1)S(1)}, u32[]{:S(2)}, u32[]{:S(2)}) collective-permute-start(bf16[1,128,512]{2,1,0:T(8,128)(2,1)S(1)} %dynamic-slice_convert_fusion), channel_id=1, source_target_pairs={{0,2},{1,3},{2,0},{3,1},{4,6},{5,7},{6,4},{7,5},{8,10},{9,11},{10,... | collective-permute-start | bytes 393224 | tf_op jit(solution)/shard_map/ppermute | solution.py:193
  (9 other events, 22.1 us)
